TPU v7x, 512 devices: a whole 4x4x16 slice. The times are simulated.
512 devices in a mesh: dp: 8 (over x, core), seq: 64 (over z, y).
Axes of the slice: x: 4, y: 4, z: 16, core: 2. Of those that a mesh axis runs over, the one named last changes fastest.
Arguments:
- queries: bfloat16 [65536, 2048], P(('dp', 'seq')), may hold values from -170 to 170
- database: bfloat16 [2048, 8, 896], P('seq'), may hold values from -90 to 90
- enc_gain: float32 [896], replicated, may hold values from 0.1 to 1.9
- key_weight: bfloat16 [896, 2048], P(None, 'dp'), may hold values from -0.1875 to 0.1875
- value_weight: bfloat16 [896, 2048], P(None, 'dp'), may hold values from -0.1875 to 0.1875
- ret_shard: int32 [1024, 16], P(('dp', 'seq')), may hold values from 0 to 63, all different within a row; in each aligned block of 2 rows (0 to 1, 2 to 3, ...) at most 2 rows name the same one
- ret_row: int32 [1024, 16], P(('dp', 'seq')), may hold values from 0 to 31
Outputs:
- attended: bfloat16 [65536, 2048], P(('dp', 'seq'))
Inputs may be any that keep to these rules, and one draw needn't show every extreme that they name: `ret_shard`: the 16 neighbours of one span name different shards; among the 32 entries of the spans of one device, at most 2 name one shard, and exactly 2 do so for some shard in some devices.
All inputs are finite; a program needn't handle non-finite values.
Results may differ from a plain program's by a relative error of at most 0.008.
Values may be sent and summed in bfloat16 or wider, within the bound.
A program may use at most 64 MiB of HBM per device.

v0:
```python
import math

import jax
import jax.numpy as jnp
from jax import lax
from jax.sharding import PartitionSpec as P

HEADS = 16
DH = 128
SPAN = 64


eps_norm = 1e-06


def from_behind(block, axis, distance):
    devices = range(lax.axis_size(axis))
    route = [(i - distance, i) for i in devices if i - distance in devices]
    return lax.ppermute(block, axis, route)


def normalize(nbr_rows, enc_gain):
    widened = nbr_rows.astype(jnp.float32)
    mean_square = jnp.mean(widened * widened, axis=-1, keepdims=True)
    return (widened * lax.rsqrt(mean_square + eps_norm) * enc_gain).astype(jnp.bfloat16)


def project(nbr_rows, enc_gain, key_weight, value_weight):
    group_count = nbr_rows.shape[0]
    normed = normalize(nbr_rows, enc_gain)
    flat_rows = normed.reshape(-1, normed.shape[-1])
    key_part = jnp.dot(
        flat_rows,
        lax.all_gather(key_weight, "dp", axis=1, tiled=True),
        preferred_element_type=jnp.float32,
    )
    value_part = jnp.dot(
        flat_rows,
        lax.all_gather(value_weight, "dp", axis=1, tiled=True),
        preferred_element_type=jnp.float32,
    )
    keys_out = key_part.astype(jnp.bfloat16)
    values_out = value_part.astype(jnp.bfloat16)
    return (
        keys_out.reshape(group_count, -1, keys_out.shape[-1]),
        values_out.reshape(group_count, -1, values_out.shape[-1]),
    )


def attend(grouped, keys_in, values_in):
    group_count = grouped.shape[0]
    query_heads = grouped.reshape(group_count, SPAN, HEADS, DH)
    key_heads = keys_in.reshape(group_count, -1, HEADS, DH)
    value_heads = values_in.reshape(group_count, -1, HEADS, DH)
    scores = jnp.einsum(
        "gqhd,gkhd->ghqk", query_heads, key_heads, preferred_element_type=jnp.float32
    ) * (1.0 / math.sqrt(DH))
    row_max = jnp.max(scores, axis=-1, keepdims=True)
    expo = jnp.exp(scores - row_max)
    probs_low = (expo / jnp.sum(expo, axis=-1, keepdims=True)).astype(jnp.bfloat16)
    mixed = jnp.einsum(
        "ghqk,gkhd->gqhd", probs_low, value_heads, preferred_element_type=jnp.float32
    )
    return mixed.reshape(group_count * SPAN, HEADS * DH).astype(jnp.bfloat16)


def body(queries, database, enc_gain, key_weight, value_weight, ret_shard, ret_row):
    spans = ret_shard.shape[0]
    nbr_count = ret_shard.shape[1]
    owners = lax.axis_size("seq")
    capacity = max(2, min(spans, 2 * spans * nbr_count // owners))
    requests = spans * nbr_count
    length = database.shape[1]
    enc_width = database.shape[2]
    shard_flat = ret_shard.reshape(requests)
    row_flat = ret_row.reshape(requests)
    order = jnp.arange(requests, dtype=jnp.int32)
    same_owner = shard_flat[:, None] == shard_flat[None, :]
    earlier = order[None, :] < order[:, None]
    slot_rank = jnp.sum(jnp.logical_and(same_owner, earlier), axis=1)
    owner_ids = jnp.arange(owners, dtype=jnp.int32)
    slot_ids = jnp.arange(capacity, dtype=jnp.int32)
    matches = jnp.logical_and(
        shard_flat[None, None, :] == owner_ids[:, None, None],
        slot_rank[None, None, :] == slot_ids[None, :, None],
    )
    wanted = jnp.sum(jnp.where(matches, row_flat[None, None, :] + 1, 0), axis=2)
    asked_rows = lax.all_to_all(wanted, "seq", split_axis=0, concat_axis=0, tiled=True)
    filled = asked_rows.reshape(-1) > 0
    picked = jnp.take(database, jnp.maximum(asked_rows.reshape(-1) - 1, 0), axis=0)
    picked = jnp.where(filled[:, None, None], picked, jnp.zeros((), picked.dtype))
    reply_rows = picked.reshape(owners, capacity, length, enc_width)
    arrived = lax.all_to_all(reply_rows, "seq", split_axis=0, concat_axis=0, tiled=True)
    arrived = arrived.reshape(owners * capacity, length, enc_width)
    fetched = jnp.take(arrived, shard_flat * capacity + slot_rank, axis=0).reshape(
        spans, nbr_count, length, enc_width
    )
    keys_own, values_own = project(fetched, enc_gain, key_weight, value_weight)
    prior_pair = from_behind(jnp.stack([keys_own[-1], values_own[-1]]), ("dp", "seq"), 1)
    keys_all = jnp.concatenate([prior_pair[0:1], keys_own], axis=0)
    values_all = jnp.concatenate([prior_pair[1:2], values_own], axis=0)
    token_count = queries.shape[0]
    columns = queries.shape[1]
    padded = jnp.concatenate(
        [
            jnp.zeros((1, columns), queries.dtype),
            queries,
            jnp.zeros((SPAN - 1, columns), queries.dtype),
        ],
        axis=0,
    )
    grouped = padded.reshape(spans + 1, SPAN, columns)
    return attend(grouped, keys_all, values_all)[1 : 1 + token_count]


def solution(mesh):
    return jax.shard_map(
        body,
        mesh=mesh,
        in_specs=(
            P(("dp", "seq"), None),
            P("seq", None, None),
            P(),
            P(None, "dp"),
            P(None, "dp"),
            P(("dp", "seq"), None),
            P(("dp", "seq"), None),
        ),
        out_specs=P(("dp", "seq"), None),
        check_vma=False,
    )
```

profile of v0, /device:TPU:6, one launch (start us, length us, event | category | flops | bytes accessed | tf_op | source)
XLA Modules:
  0.0 186.5 jit_solution(5132230510288883860)
XLA Ops:
  6.5 0.7 all-gather.3.cloned.1.call-update
  7.3 0.8 reshape.195
  8.0 0.7 broadcast_add_fusion
  8.8 0.2 convert_reduce_fusion
  9.0 0.1 select_reduce_fusion
  9.2 33.1 %all_to_all.14 = s32[64,1,2]{2,1,0:T(1,128)S(1)} all-to-all(s32[64,1,2]{2,1,0:T(1,128)S(1)} %copy.46), channel_id=1, replica_groups=mesh['dp'=8,'seq'=64] {'seq'}, dimensions={0} | all-to-all | bytes 1024 | tf_op jit(solution)/shard_map/all_to_all | solution.py:88
  42.5 0.1 copy.48
  42.6 0.1 copy.50
  42.8 0.1 reshape.199
  43.0 0.9 gather_fusion
  43.8 1.6 select_select_fusion
  45.4 4.8 %all-to-all-start.1 = ((bf16[64,2,8,896]{3,2,1,0:T(8,128)(2,1)}), bf16[64,2,8,896]{3,2,1,0:T(8,128)(2,1)S(1)}, u32[]{:S(2)}, u32[]{:S(2)}) async-start(bf16[64,2,8,896]{3,2,1,0:T(8,128)(2,1)} %select_select_fusion), calls=%async_computation.1 | async-start | bytes 3670016 | tf_op jit(solution)/shard_map/all_to_all | solution.py:93
  50.3 0.7 all-gather.5.cloned.1.call-update
  51.4 86.7 %all-to-all-done.1 = bf16[64,2,8,896]{3,2,1,0:T(8,128)(2,1)S(1)} async-done(((bf16[64,2,8,896]{3,2,1,0:T(8,128)(2,1)}), bf16[64,2,8,896]{3,2,1,0:T(8,128)(2,1)S(1)}, u32[]{:S(2)}, u32[]{:S(2)}) %all-to-all-start.1) | async-done | bytes 1835040 | tf_op jit(solution)/shard_map/all_to_all | solution.py:93
  138.1 0.6 gather_fusion.1
  138.7 0.3 multiply_reduce_fusion
  139.1 3.4 %convolution_convert_fusion.1 = bf16[256,2048]{1,0:T(8,128)(2,1)S(1)} fusion(bf16[896,2048]{1,0:T(8,128)(2,1)} %all-gather.3.cloned.1.call-done, bf16[32,8,896]{2,1,0:T(8,128)(2,1)S(1)} %gather_fusion.1, f32[896]{0:T(1024)S(1)} %copy-done.3, f32[256]{0:T(256)S(1)} %rsqrt.12, pred[256]{0:T(512)(128)(4,1)S(1)} %broadcast_in_dim.69), kind=kOutput, calls=%fused_computation.4 | convolution fusion | flops 941195264 | bytes 5182208 | tf_op jit(solution)/shard_map/dot_general | solution.py:32
  142.6 3.4 %convolution_convert_fusion = bf16[256,2048]{1,0:T(8,128)(2,1)S(1)} fusion(bf16[896,2048]{1,0:T(8,128)(2,1)} %all-gather.5.cloned.1.call-done, bf16[32,8,896]{2,1,0:T(8,128)(2,1)S(1)} %gather_fusion.1, f32[896]{0:T(1024)S(1)} %copy-done.3, f32[256]{0:T(256)S(1)} %rsqrt.12, pred[256]{0:T(512)(128)(4,1)S(1)} %broadcast_in_dim.69), kind=kOutput, calls=%fused_computation.3 | convolution fusion | flops 941195264 | bytes 5182208 | tf_op jit(solution)/shard_map/dot_general | solution.py:37
  146.2 3.4 %collective-permute-start = (bf16[2,128,2048]{2,1,0:T(8,128)(2,1)S(1)}, bf16[2,128,2048]{2,1,0:T(8,128)(2,1)S(1)}, u32[]{:S(2)}, u32[]{:S(2)}) collective-permute-start(bf16[2,128,2048]{2,1,0:T(8,128)(2,1)S(1)} %pad_maximum_fusion), channel_id=1, source_target_pairs={{0,1},{1,2},{2,3},{3,4},{4,5},{5,6},{6,7},{7,8},{8,9},{9,10},{10,1... | collective-permute-start | bytes 3145736 | tf_op jit(solution)/shard_map/ppermute | solution.py:19
  149.7 0.4 maximum_bitcast_fusion
  150.1 0.2 copy.60
  150.3 0.2 copy.61
  150.5 0.3 copy.55
  150.8 0.2 copy.62
  151.0 0.3 copy.53
  151.3 19.7 %collective-permute-done = bf16[2,128,2048]{2,1,0:T(8,128)(2,1)S(1)} collective-permute-done((bf16[2,128,2048]{2,1,0:T(8,128)(2,1)S(1)}, bf16[2,128,2048]{2,1,0:T(8,128)(2,1)S(1)}, u32[]{:S(2)}, u32[]{:S(2)}) %collective-permute-start) | collective-permute-done | bytes 1048608 | tf_op jit(solution)/shard_map/ppermute | solution.py:19
  171.1 1.3 copy_bitcast_fusion.1
  172.4 3.5 %fusion.38 = (f32[3,16,64]{2,1,0:T(8,128)S(1)}, f32[3,16,64,128]{3,2,1,0:T(8,128)}) fusion(bf16[2,128,16,128]{3,1,2,0:T(8,128)(2,1)S(1)} %copy.55, bf16[1,128,16,128]{3,1,2,0:T(8,128)(2,1)} %get-tuple-element.12, bf16[3,64,16,128]{3,2,1,0:T(8,128)(2,1)S(1)} %bitcast.61), kind=kOutput, calls=%fused_computation.60 | convolution fusion | flops 102629504 | bytes 3944448 | tf_op jit(solution)/shard_map/sub | solution.py:59
  175.9 2.1 %fusion.17 = bf16[3,64,16,128]{3,1,2,0:T(8,128)(2,1)S(1)} fusion(bf16[2,128,16,128]{3,1,2,0:T(8,128)(2,1)S(1)} %copy.53, bf16[1,128,16,128]{3,1,2,0:T(8,128)(2,1)} %get-tuple-element.11, f32[3,16,64,128]{3,2,1,0:T(8,128)} %get-tuple-element.10, f32[3,16,64]{2,1,0:T(8,128)S(1)} %get-tuple-element.9), kind=kOutput, calls=%fused_computation.19 | convolution fusion | flops 104988672 | bytes 3944448 | tf_op jit(solution)/shard_map/ghqk,gkhd->gqhd/dot_general | solution.py:61
  178.0 0.5 copy.57
  178.5 0.2 copy.75
  178.7 0.9 slice.36
  (39 shorter events, 1.4 us)
Async XLA Ops:
  6.5 36.4 %copy-start = (bf16[32,8,896]{2,1,0:T(8,128)(2,1)S(1)}, bf16[32,8,896]{2,1,0:T(8,128)(2,1)}, u32[]{:S(2)}) copy-start(bf16[32,8,896]{2,1,0:T(8,128)(2,1)} %param.8) | copy-start | bytes 1376260
  6.5 132.6 %all-gather.3.cloned.1.call-start = ((), (), s32[]{:S(2)}) async-start(), calls=%async_computation.2 | async-start | bytes 4128768 | tf_op jit(solution)/shard_map/all_gather | solution.py:34
  45.4 5.7 %copy-start.2 = (s32[2,16]{1,0:T(2,128)S(1)}, s32[2,16]{1,0:T(2,128)}, u32[]{:S(2)}) copy-start(s32[2,16]{1,0:T(2,128)} %param.12) | copy-start | bytes 388
  45.4 92.7 %all-to-all-start.1 = ((bf16[64,2,8,896]{3,2,1,0:T(8,128)(2,1)}), bf16[64,2,8,896]{3,2,1,0:T(8,128)(2,1)S(1)}, u32[]{:S(2)}, u32[]{:S(2)}) async-start(bf16[64,2,8,896]{3,2,1,0:T(8,128)(2,1)} %select_select_fusion), calls=%async_computation.1 | async-start | bytes 3670016 | tf_op jit(solution)/shard_map/all_to_all | solution.py:93
  50.2 88.9 %copy-start.3 = (f32[896]{0:T(1024)S(1)}, f32[896]{0:T(1024)}, u32[]{:S(2)}) copy-start(f32[896]{0:T(1024)} %param.9) | copy-start | bytes 10756
  50.3 92.4 %all-gather.5.cloned.1.call-start = ((), (), s32[]{:S(2)}) async-start(), calls=%async_computation.3 | async-start | bytes 4128768 | tf_op jit(solution)/shard_map/all_gather | solution.py:39
  146.0 3.6 %copy-start.1 = (bf16[128,2048]{1,0:T(8,128)(2,1)S(1)}, bf16[128,2048]{1,0:T(8,128)(2,1)}, u32[]{:S(2)}) copy-start(bf16[128,2048]{1,0:T(8,128)(2,1)} %param.7) | copy-start | bytes 1572868
  146.2 24.8 %collective-permute-start = (bf16[2,128,2048]{2,1,0:T(8,128)(2,1)S(1)}, bf16[2,128,2048]{2,1,0:T(8,128)(2,1)S(1)}, u32[]{:S(2)}, u32[]{:S(2)}) collective-permute-start(bf16[2,128,2048]{2,1,0:T(8,128)(2,1)S(1)} %pad_maximum_fusion), channel_id=1, source_target_pairs={{0,1},{1,2},{2,3},{3,4},{4,5},{5,6},{6,7},{7,8},{8,9},{9,10},{10,1... | collective-permute-start | bytes 3145736 | tf_op jit(solution)/shard_map/ppermute | solution.py:19
Sparse Core Ops, SparseCore 0:
  9.5 45.2 all-gather.2
  56.9 42.5 all-gather.4
where the time goes:
time: 187 us
  waiting for transfers between devices  108 us (58%)
  blocking collectives  33.1 us (18%)
  between operations  13.7 us (7%)
  matrix products  12.4 us (7%)
  starting transfers between devices  8.24 us (4%)
  local copies, waits for them, and re-layouts  7.73 us (4%)
  other arithmetic  3.47 us (2%)
    all_to_all x1, waiting for transfers between devices, body(): lax.all_to_all(reply_rows, 'seq', split_axis=0, concat_axis=0, tiled=True)  86.7 us
    all_to_all x1, blocking collectives, body(): lax.all_to_all(wanted, 'seq', split_axis=0, concat_axis=0, tiled=True)  33.1 us
    ppermute x1, waiting for transfers between devices, from_behind(): return lax.ppermute(block, axis, route)  19.7 us
    all_to_all x1, starting transfers between devices, body(): lax.all_to_all(reply_rows, 'seq', split_axis=0, concat_axis=0, tiled=True)  4.81 us
  transfers between devices with their start and end apart: 4, of which 2 were waited for; matrix products, arithmetic and copies ran while one was open for 6% of the time, Pallas kernels for 0%

commit v1 on v0

--- a/solution.py
+++ b/solution.py
@@ -95,10 +95,11 @@
     fetched = jnp.take(arrived, shard_flat * capacity + slot_rank, axis=0).reshape(
         spans, nbr_count, length, enc_width
     )
+    prior_rows = from_behind(fetched[-1:], ("dp", "seq"), 1)
     keys_own, values_own = project(fetched, enc_gain, key_weight, value_weight)
-    prior_pair = from_behind(jnp.stack([keys_own[-1], values_own[-1]]), ("dp", "seq"), 1)
-    keys_all = jnp.concatenate([prior_pair[0:1], keys_own], axis=0)
-    values_all = jnp.concatenate([prior_pair[1:2], values_own], axis=0)
+    keys_prior, values_prior = project(prior_rows, enc_gain, key_weight, value_weight)
+    keys_all = jnp.concatenate([keys_prior, keys_own], axis=0)
+    values_all = jnp.concatenate([values_prior, values_own], axis=0)
     token_count = queries.shape[0]
     columns = queries.shape[1]
     padded = jnp.concatenate(

time: 187 us -> 171 us (0.914)
  waiting for transfers between devices: 108 us -> 86.7 us
  local copies, waits for them, and re-layouts: 7.73 us -> 10.7 us
    ppermute x1, waiting for transfers between devices: 19.7 us -> 0.14 us  [from_behind(): return lax.ppermute(block, axis, route)]
    unnamed x13 -> x18, local copies, waits for them, and re-layouts: 0.93 us -> 4.2 us
    dot_general x1 -> x2, matrix products: 3.4 us -> 4.19 us  [project(): jnp.dot(flat_rows, lax.all_gather(key_weight, 'dp', axis=1, tiled=True),...]
    dot_general x1 -> x2, matrix products: 3.4 us -> 4.19 us  [project(): jnp.dot(flat_rows, lax.all_gather(value_weight, 'dp', axis=1, tiled=True)...]
  transfers between devices with their start and end apart: 4 -> 4, of which waited for: 2 -> 2; matrix products, arithmetic and copies ran while one was open for 6% -> 9% of each run, Pallas kernels for 0% -> 0%
where the time goes in v1:
time: 171 us; the launch traced here: 170 us
  waiting for transfers between devices  86.7 us (51%)
  blocking collectives  33.1 us (19%)
  matrix products  14 us (8%)
  between operations  13.7 us (8%)
  local copies, waits for them, and re-layouts  10.7 us (6%)
  starting transfers between devices  8.24 us (5%)
  other arithmetic  3.53 us (2%)
    all_to_all x1, waiting for transfers between devices, body(): lax.all_to_all(reply_rows, 'seq', split_axis=0, concat_axis=0, tiled=True)  85.1 us
    all_to_all x1, blocking collectives, body(): lax.all_to_all(wanted, 'seq', split_axis=0, concat_axis=0, tiled=True)  33.1 us
    all_to_all x1, starting transfers between devices, body(): lax.all_to_all(reply_rows, 'seq', split_axis=0, concat_axis=0, tiled=True)  4.82 us
    unnamed x18, local copies, waits for them, and re-layouts  4.2 us
    dot_general x2, matrix products, project(): jnp.dot(flat_rows, lax.all_gather(key_weight, 'dp', axis=1, tiled=True),...  4.19 us
    dot_general x2, matrix products, project(): jnp.dot(flat_rows, lax.all_gather(value_weight, 'dp', axis=1, tiled=True)...  4.19 us
    sub x1, matrix products, attend(): expo = jnp.exp(scores - row_max)  3.56 us
  transfers between devices with their start and end apart: 4, of which 2 were waited for; matrix products, arithmetic and copies ran while one was open for 9% of the time, Pallas kernels for 0%

profile of v1, /device:TPU:6, one launch (start us, length us, event | category | flops | bytes accessed | tf_op | source)
XLA Modules:
  0.0 170.0 jit_solution(602631888019306077)
XLA Ops:
  6.5 0.7 all-gather.5.cloned.1.call-update
  7.3 0.8 reshape.217
  8.0 0.7 broadcast_add_fusion
  8.8 0.2 convert_reduce_fusion
  9.2 33.1 %all_to_all.14 = s32[64,1,2]{2,1,0:T(1,128)S(1)} all-to-all(s32[64,1,2]{2,1,0:T(1,128)S(1)} %copy.46), channel_id=1, replica_groups=mesh['dp'=8,'seq'=64] {'seq'}, dimensions={0} | all-to-all | bytes 1024 | tf_op jit(solution)/shard_map/all_to_all | solution.py:88
  43.0 0.9 gather_fusion
  43.8 1.6 select_select_fusion
  45.4 4.8 %all-to-all-start.1 = ((bf16[64,2,8,896]{3,2,1,0:T(8,128)(2,1)}), bf16[64,2,8,896]{3,2,1,0:T(8,128)(2,1)S(1)}, u32[]{:S(2)}, u32[]{:S(2)}) async-start(bf16[64,2,8,896]{3,2,1,0:T(8,128)(2,1)} %select_select_fusion), calls=%async_computation.1 | async-start | bytes 3670016 | tf_op jit(solution)/shard_map/all_to_all | solution.py:93
  50.3 0.7 all-gather.3.cloned.1.call-update
  51.5 0.4 maximum_bitcast_fusion
  51.9 1.1 copy.58
  53.0 85.1 %all-to-all-done.1 = bf16[64,2,8,896]{3,2,1,0:T(8,128)(2,1)S(1)} async-done(((bf16[64,2,8,896]{3,2,1,0:T(8,128)(2,1)}), bf16[64,2,8,896]{3,2,1,0:T(8,128)(2,1)S(1)}, u32[]{:S(2)}, u32[]{:S(2)}) %all-to-all-start.1) | async-done | bytes 1835040 | tf_op jit(solution)/shard_map/all_to_all | solution.py:93
  138.1 0.6 gather_fusion.1
  138.7 0.3 multiply_reduce_fusion
  139.0 3.4 %collective-permute-start = (bf16[1,16,8,896]{3,2,1,0:T(8,128)(2,1)S(1)}, bf16[1,16,8,896]{3,2,1,0:T(8,128)(2,1)S(1)}, u32[]{:S(2)}, u32[]{:S(2)}) collective-permute-start(bf16[1,16,8,896]{3,2,1,0:T(8,128)(2,1)S(1)} %slice_bitcast_fusion), channel_id=1, source_target_pairs={{0,1},{1,2},{2,3},{3,4},{4,5},{5,6},{6,7},{7,8},{8,9},{9,10},{10,1... | collective-permute-start | bytes 688136 | tf_op jit(solution)/shard_map/ppermute | solution.py:19
  142.6 3.4 %fusion.18 = bf16[32,8,16,128]{3,1,2,0:T(8,128)(2,1)S(1)} fusion(bf16[896,2048]{1,0:T(8,128)(2,1)} %all-gather.5.cloned.1.call-done, bf16[32,8,896]{2,1,0:T(8,128)(2,1)S(1)} %gather_fusion.1, f32[896]{0:T(1024)S(1)} %copy-done.4, f32[256]{0:T(256)S(1)} %rsqrt.21, pred[256]{0:T(512)(128)(4,1)S(1)} %broadcast_in_dim.79), kind=kOutput, calls=%fused_computation.22 | convolution fusion | flops 941195264 | bytes 5182208 | tf_op jit(solution)/shard_map/dot_general | solution.py:32
  146.0 0.2 copy.60
  146.2 0.3 copy.55
  146.5 3.4 %fusion.17 = bf16[32,8,16,128]{3,1,2,0:T(8,128)(2,1)S(1)} fusion(bf16[896,2048]{1,0:T(8,128)(2,1)} %all-gather.3.cloned.1.call-done, bf16[32,8,896]{2,1,0:T(8,128)(2,1)S(1)} %gather_fusion.1, f32[896]{0:T(1024)S(1)} %copy-done.4, f32[256]{0:T(256)S(1)} %rsqrt.21, pred[256]{0:T(512)(128)(4,1)S(1)} %broadcast_in_dim.79), kind=kOutput, calls=%fused_computation.21 | convolution fusion | flops 941195264 | bytes 5182208 | tf_op jit(solution)/shard_map/dot_general | solution.py:37
  149.9 0.2 copy.62
  150.2 0.3 copy.53
  150.5 0.1 collective-permute-done
  150.7 1.2 copy-done.1
  152.0 0.8 fusion.23
  153.0 1.0 copy-done.2
  154.0 0.8 fusion.22
  154.9 0.9 copy.52
  155.9 3.6 %fusion.48 = (f32[3,16,64]{2,1,0:T(8,128)S(1)}, f32[3,16,64,128]{3,2,1,0:T(8,128)}) fusion(bf16[2,128,16,128]{3,1,2,0:T(8,128)(2,1)S(1)} %copy.55, bf16[1,128,16,128]{3,1,2,0:T(8,128)(2,1)S(1)} %copy.54, bf16[3,64,16,128]{3,2,1,0:T(8,128)(2,1)} %bitcast.67), kind=kOutput, calls=%fused_computation.68 | convolution fusion | flops 102629504 | bytes 3944448 | tf_op jit(solution)/shard_map/sub | solution.py:59
  159.4 2.1 %fusion.19 = bf16[3,64,16,128]{3,1,2,0:T(8,128)(2,1)S(1)} fusion(bf16[2,128,16,128]{3,1,2,0:T(8,128)(2,1)S(1)} %copy.53, bf16[1,128,16,128]{3,1,2,0:T(8,128)(2,1)} %copy.52, f32[3,16,64,128]{3,2,1,0:T(8,128)} %get-tuple-element.10, f32[3,16,64]{2,1,0:T(8,128)S(1)} %get-tuple-element.9), kind=kOutput, calls=%fused_computation.23 | convolution fusion | flops 104988672 | bytes 3944448 | tf_op jit(solution)/shard_map/ghqk,gkhd->gqhd/dot_general | solution.py:61
  161.5 0.5 copy.57
  162.1 0.2 copy.73
  162.3 0.9 slice.17
  (47 shorter events, 2.1 us)
Async XLA Ops:
  6.5 36.4 %copy-start = (bf16[32,8,896]{2,1,0:T(8,128)(2,1)S(1)}, bf16[32,8,896]{2,1,0:T(8,128)(2,1)}, u32[]{:S(2)}) copy-start(bf16[32,8,896]{2,1,0:T(8,128)(2,1)} %param.8) | copy-start | bytes 1376260
  6.5 136.0 %all-gather.5.cloned.1.call-start = ((), (), s32[]{:S(2)}) async-start(), calls=%async_computation.3 | async-start | bytes 4128768 | tf_op jit(solution)/shard_map/all_gather | solution.py:34
  45.4 5.7 %copy-start.5 = (s32[2,16]{1,0:T(2,128)S(1)}, s32[2,16]{1,0:T(2,128)}, u32[]{:S(2)}) copy-start(s32[2,16]{1,0:T(2,128)} %param.12) | copy-start | bytes 388
  45.4 6.0 %copy-start.3 = (bf16[128,2048]{1,0:T(8,128)(2,1)S(1)}, bf16[128,2048]{1,0:T(8,128)(2,1)}, u32[]{:S(2)}) copy-start(bf16[128,2048]{1,0:T(8,128)(2,1)} %param.7) | copy-start | bytes 1572868
  45.4 92.7 %all-to-all-start.1 = ((bf16[64,2,8,896]{3,2,1,0:T(8,128)(2,1)}), bf16[64,2,8,896]{3,2,1,0:T(8,128)(2,1)S(1)}, u32[]{:S(2)}, u32[]{:S(2)}) async-start(bf16[64,2,8,896]{3,2,1,0:T(8,128)(2,1)} %select_select_fusion), calls=%async_computation.1 | async-start | bytes 3670016 | tf_op jit(solution)/shard_map/all_to_all | solution.py:93
  50.3 96.3 %all-gather.3.cloned.1.call-start = ((), (), s32[]{:S(2)}) async-start(), calls=%async_computation.2 | async-start | bytes 4128768 | tf_op jit(solution)/shard_map/all_gather | solution.py:39
  51.9 90.7 %copy-start.4 = (f32[896]{0:T(1024)S(1)}, f32[896]{0:T(1024)}, u32[]{:S(2)}) copy-start(f32[896]{0:T(1024)} %param.9) | copy-start | bytes 10756
  139.0 11.6 %collective-permute-start = (bf16[1,16,8,896]{3,2,1,0:T(8,128)(2,1)S(1)}, bf16[1,16,8,896]{3,2,1,0:T(8,128)(2,1)S(1)}, u32[]{:S(2)}, u32[]{:S(2)}) collective-permute-start(bf16[1,16,8,896]{3,2,1,0:T(8,128)(2,1)S(1)} %slice_bitcast_fusion), channel_id=1, source_target_pairs={{0,1},{1,2},{2,3},{3,4},{4,5},{5,6},{6,7},{7,8},{8,9},{9,10},{10,1... | collective-permute-start | bytes 688136 | tf_op jit(solution)/shard_map/ppermute | solution.py:19
  149.9 2.0 %copy-start.1 = (bf16[896,2048]{1,0:T(8,128)(2,1)S(1)}, bf16[896,2048]{1,0:T(8,128)(2,1)}, u32[]{:S(2)}) copy-start(bf16[896,2048]{1,0:T(8,128)(2,1)} %all-gather.5.cloned.1.call-done) | copy-start | bytes 11010052
  152.0 2.0 %copy-start.2 = (bf16[896,2048]{1,0:T(8,128)(2,1)S(1)}, bf16[896,2048]{1,0:T(8,128)(2,1)}, u32[]{:S(2)}) copy-start(bf16[896,2048]{1,0:T(8,128)(2,1)} %all-gather.3.cloned.1.call-done) | copy-start | bytes 11010052
Sparse Core Ops, SparseCore 0:
  9.5 45.2 all-gather.4
  56.9 42.5 all-gather.2

commit v2 on v1

--- a/solution.py
+++ b/solution.py
@@ -1,9 +1,14 @@
+import functools
 import math
 
 import jax
 import jax.numpy as jnp
 from jax import lax
+from jax.experimental import pallas as pl
+from jax.experimental.pallas import tpu as pltpu
 from jax.sharding import PartitionSpec as P
+
+MESH = pl.DeviceIdType.MESH
 
 HEADS = 16
 DH = 128
@@ -17,6 +22,97 @@
     devices = range(lax.axis_size(axis))
     route = [(i - distance, i) for i in devices if i - distance in devices]
     return lax.ppermute(block, axis, route)
+
+
+def gathered_rows(ids, table_ref, length):
+    shape = (2 * length, 128)
+    sub = lax.broadcasted_iota(jnp.int32, shape, 0)
+    lane = lax.broadcasted_iota(jnp.int32, shape, 1)
+    sel = jnp.where(
+        sub < length, jnp.broadcast_to(ids[0:1, :], shape), jnp.broadcast_to(ids[1:2, :], shape)
+    )
+    total = jnp.zeros((2 * length, table_ref.shape[1]), jnp.float32)
+    for h in range(table_ref.shape[0] // 128):
+        col = lane + h * 128
+        hit = jnp.logical_and(col // length == sel, col % length == sub % length)
+        total += jnp.dot(
+            hit.astype(table_ref.dtype),
+            table_ref[h * 128 : (h + 1) * 128, :],
+            preferred_element_type=jnp.float32,
+        )
+    return total.astype(table_ref.dtype)
+
+
+def fetch_kernel(length, wanted_ref, table_ref, out_ref, asked, outgoing, req_send, req_recv, rep_send, rep_recv):
+    n = wanted_ref.shape[0]
+    me = lax.axis_index("seq")
+    dp = lax.axis_index("dp")
+
+    def request(peer, slot):
+        return pltpu.make_async_remote_copy(
+            wanted_ref.at[peer], asked.at[slot], req_send.at[peer], req_recv.at[slot],
+            device_id=(dp, peer), device_id_type=MESH,
+        )
+
+    def reply(peer, slot):
+        return pltpu.make_async_remote_copy(
+            outgoing.at[peer], out_ref.at[slot], rep_send.at[peer], rep_recv.at[slot],
+            device_id=(dp, peer), device_id_type=MESH,
+        )
+
+    barrier = pltpu.get_barrier_semaphore()
+
+    def greet(k, carry):
+        pl.semaphore_signal(barrier, inc=1, device_id=(dp, lax.rem(me + k, n)), device_id_type=MESH)
+        return carry
+
+    lax.fori_loop(1, n, greet, 0)
+    pl.semaphore_wait(barrier, n - 1)
+
+    def ask(k, carry):
+        request(lax.rem(me + k, n), me).start()
+        return carry
+
+    lax.fori_loop(1, n, ask, 0)
+    out_ref[me] = gathered_rows(wanted_ref[me], table_ref, length)
+
+    def serve(k, carry):
+        source = lax.rem(me + n - k, n)
+        request(source, source).wait_recv()
+        outgoing[source] = gathered_rows(asked[source], table_ref, length)
+        reply(source, me).start()
+        return carry
+
+    lax.fori_loop(1, n, serve, 0)
+
+    def finish(k, carry):
+        peer = lax.rem(me + k, n)
+        request(peer, me).wait_send()
+        reply(peer, me).wait_send()
+        reply(peer, peer).wait_recv()
+        return carry
+
+    lax.fori_loop(1, n, finish, 0)
+
+
+def fetch(wanted, table, length):
+    n = wanted.shape[0]
+    width = table.shape[1]
+    return pl.pallas_call(
+        functools.partial(fetch_kernel, length),
+        out_shape=jax.ShapeDtypeStruct((n, 2 * length, width), table.dtype),
+        in_specs=[pl.BlockSpec(memory_space=pltpu.VMEM)] * 2,
+        out_specs=pl.BlockSpec(memory_space=pltpu.VMEM),
+        scratch_shapes=[
+            pltpu.VMEM(wanted.shape, jnp.int32),
+            pltpu.VMEM((n, 2 * length, width), table.dtype),
+            pltpu.SemaphoreType.DMA((n,)),
+            pltpu.SemaphoreType.DMA((n,)),
+            pltpu.SemaphoreType.DMA((n,)),
+            pltpu.SemaphoreType.DMA((n,)),
+        ],
+        compiler_params=pltpu.CompilerParams(collective_id=0, has_side_effects=True),
+    )(wanted, table)
 
 
 def normalize(nbr_rows, enc_gain):
@@ -84,13 +180,11 @@
         shard_flat[None, None, :] == owner_ids[:, None, None],
         slot_rank[None, None, :] == slot_ids[None, :, None],
     )
-    wanted = jnp.sum(jnp.where(matches, row_flat[None, None, :] + 1, 0), axis=2)
-    asked_rows = lax.all_to_all(wanted, "seq", split_axis=0, concat_axis=0, tiled=True)
-    filled = asked_rows.reshape(-1) > 0
-    picked = jnp.take(database, jnp.maximum(asked_rows.reshape(-1) - 1, 0), axis=0)
-    picked = jnp.where(filled[:, None, None], picked, jnp.zeros((), picked.dtype))
-    reply_rows = picked.reshape(owners, capacity, length, enc_width)
-    arrived = lax.all_to_all(reply_rows, "seq", split_axis=0, concat_axis=0, tiled=True)
+    wanted = jnp.sum(jnp.where(matches, row_flat[None, None, :] + 1, 0), axis=2) - 1
+    wanted = jnp.broadcast_to(wanted[:, :, None], (owners, capacity, 128))
+    wanted = jnp.pad(wanted, ((0, 0), (0, 8 - capacity), (0, 0)), constant_values=-1)
+    table = database.reshape(database.shape[0] * length, enc_width)
+    arrived = fetch(wanted, table, length)
     arrived = arrived.reshape(owners * capacity, length, enc_width)
     fetched = jnp.take(arrived, shard_flat * capacity + slot_rank, axis=0).reshape(
         spans, nbr_count, length, enc_width

time: 171 us -> 168 us (0.982)
  Pallas kernels: 0 us -> 116 us
  waiting for transfers between devices: 86.7 us -> 9.97 us
  blocking collectives: 33.1 us -> 0 us
  starting transfers between devices: 8.24 us -> 1.96 us
    pallas_call x0 -> x1, Pallas kernels: none -> 116 us  [fetch(): pl.pallas_call(functools.partial(fetch_kernel, length), out_shape=jax.Sha...]
    all_to_all x1 -> x0, waiting for transfers between devices: 85.1 us -> none  [body(): lax.all_to_all(reply_rows, 'seq', split_axis=0, concat_axis=0, tiled=True)]
    all_to_all x1 -> x0, blocking collectives: 33.1 us -> none  [body(): lax.all_to_all(wanted, 'seq', split_axis=0, concat_axis=0, tiled=True)]
    ppermute x1, waiting for transfers between devices: 0.14 us -> 8.52 us  [from_behind(): return lax.ppermute(block, axis, route)]
    all_to_all x1 -> x0, starting transfers between devices: 4.82 us -> none  [body(): lax.all_to_all(reply_rows, 'seq', split_axis=0, concat_axis=0, tiled=True)]
    unnamed x18, local copies, waits for them, and re-layouts: 4.2 us -> 1.97 us
  transfers between devices with their start and end apart: 4 -> 3, of which waited for: 2 -> 1; matrix products, arithmetic and copies ran while one was open for 9% -> 8% of each run, Pallas kernels for 0% -> 69%
where the time goes in v2:
time: 168 us
  Pallas kernels  116 us (69%)
  matrix products  14.4 us (9%)
  between operations  13.7 us (8%)
  waiting for transfers between devices  9.97 us (6%)
  local copies, waits for them, and re-layouts  9.52 us (6%)
  other arithmetic  2.6 us (2%)
  starting transfers between devices  1.96 us (1%)
    pallas_call x1, Pallas kernels, fetch(): pl.pallas_call(functools.partial(fetch_kernel, length), out_shape=jax.Sha...  116 us
    ppermute x1, waiting for transfers between devices, from_behind(): return lax.ppermute(block, axis, route)  8.52 us
    dot_general x2, matrix products, project(): jnp.dot(flat_rows, lax.all_gather(key_weight, 'dp', axis=1, tiled=True),...  4.36 us
    dot_general x2, matrix products, project(): jnp.dot(flat_rows, lax.all_gather(value_weight, 'dp', axis=1, tiled=True)...  4.36 us
    sub x1, matrix products, attend(): expo = jnp.exp(scores - row_max)  3.62 us
  transfers between devices with their start and end apart: 3, of which 1 were waited for; matrix products, arithmetic and copies ran while one was open for 8% of the time, Pallas kernels for 69%

profile of v2, /device:TPU:6, one launch (start us, length us, event | category | flops | bytes accessed | tf_op | source)
XLA Modules:
  0.0 167.7 jit_solution(17809471556531069449)
XLA Ops:
  6.5 0.7 all-gather.5.cloned.1.call-update
  7.3 0.7 all-gather.3.cloned.1.call-update
  8.0 0.8 reshape.174
  8.8 0.7 broadcast_add_fusion.1
  9.5 0.2 convert_reduce_fusion
  10.0 0.7 broadcast_multiply_fusion
  10.8 0.1 broadcast_in_dim.56
  10.9 0.7 pad.4.wanted_ref
  11.6 115.6 %shard_map.73 = bf16[64,16,896]{2,1,0:T(8,128)(2,1)} custom-call(s32[64,8,128]{2,1,0:T(8,128)} %pad.4.wanted_ref, bf16[256,896]{1,0:T(8,128)(2,1)} %bitcast.60), custom_call_target="tpu_custom_call" | custom-call | tf_op jit(solution)/shard_map/pallas_call | solution.py:101
  127.3 2.2 %gather_fusion = bf16[32,8,896]{2,1,0:T(8,128)(2,1)S(1)} fusion(bf16[128,8,896]{2,1,0:T(8,128)(2,1)} %bitcast.55, s32[1024]{0:T(1024)S(1)} %pad_clamp_fusion), kind=kCustom, calls=%fused_computation | custom fusion | bytes 917632 | tf_op jit(solution)/shard_map/jit(_take)/gather | solution.py:189
  129.5 0.3 multiply_reduce_fusion
  129.8 1.9 %collective-permute-start = (bf16[1,16,8,896]{3,2,1,0:T(8,128)(2,1)S(1)}, bf16[1,16,8,896]{3,2,1,0:T(8,128)(2,1)S(1)}, u32[]{:S(2)}, u32[]{:S(2)}) collective-permute-start(bf16[1,16,8,896]{3,2,1,0:T(8,128)(2,1)S(1)} %slice_bitcast_fusion), channel_id=1, source_target_pairs={{0,1},{1,2},{2,3},{3,4},{4,5},{5,6},{6,7},{7,8},{8,9},{9,10},{10,1... | collective-permute-start | bytes 688136 | tf_op jit(solution)/shard_map/ppermute | solution.py:24
  132.2 0.4 maximum_bitcast_fusion
  132.6 1.0 copy.25
  133.7 8.5 %collective-permute-done = bf16[1,16,8,896]{3,2,1,0:T(8,128)(2,1)S(1)} collective-permute-done((bf16[1,16,8,896]{3,2,1,0:T(8,128)(2,1)S(1)}, bf16[1,16,8,896]{3,2,1,0:T(8,128)(2,1)S(1)}, u32[]{:S(2)}, u32[]{:S(2)}) %collective-permute-start) | collective-permute-done | bytes 229408 | tf_op jit(solution)/shard_map/ppermute | solution.py:24
  142.2 0.1 fusion.26
  142.4 3.0 %fusion.23 = bf16[16,8,16,128]{3,1,2,0:T(8,128)(2,1)S(1)} fusion(bf16[896,2048]{1,0:T(8,128)(2,1)} %all-gather.5.cloned.1.call-done, bf16[1,16,8,896]{3,2,1,0:T(8,128)(2,1)S(1)} %collective-permute-done, f32[896]{0:T(1024)S(1)} %copy-done.4, f32[16,8]{1,0:T(8,128)S(1)} %add_rsqrt_fusion.1), kind=kOutput, calls=%fused_computation.23 | convolution fusion | flops 470482944 | bytes 4427776 | tf_op jit(solution)/shard_map/dot_general | solution.py:128
  145.5 0.1 copy.21
  145.6 1.4 fusion.18
  147.0 0.2 copy.27
  147.3 0.3 copy.22
  147.6 3.0 %fusion.22 = bf16[16,8,16,128]{3,1,2,0:T(8,128)(2,1)S(1)} fusion(bf16[896,2048]{1,0:T(8,128)(2,1)} %all-gather.3.cloned.1.call-done, bf16[1,16,8,896]{3,2,1,0:T(8,128)(2,1)S(1)} %collective-permute-done, f32[896]{0:T(1024)S(1)} %copy-done.4, f32[16,8]{1,0:T(8,128)S(1)} %add_rsqrt_fusion.1), kind=kOutput, calls=%fused_computation.22 | convolution fusion | flops 470482944 | bytes 4427776 | tf_op jit(solution)/shard_map/dot_general | solution.py:133
  150.6 0.1 copy.28
  150.7 0.9 copy.19
  151.6 1.4 fusion.17
  153.0 0.2 copy.29
  153.2 0.3 copy.20
  153.5 3.6 %fusion.48 = (f32[3,16,64]{2,1,0:T(8,128)S(1)}, f32[3,16,64,128]{3,2,1,0:T(8,128)}) fusion(bf16[2,128,16,128]{3,1,2,0:T(8,128)(2,1)S(1)} %copy.22, bf16[1,128,16,128]{3,1,2,0:T(8,128)(2,1)S(1)} %copy.21, bf16[3,64,16,128]{3,2,1,0:T(8,128)(2,1)} %bitcast.59), kind=kOutput, calls=%fused_computation.63 | convolution fusion | flops 102629504 | bytes 3944448 | tf_op jit(solution)/shard_map/sub | solution.py:155
  157.2 2.0 %fusion.19 = bf16[3,64,16,128]{3,1,2,0:T(8,128)(2,1)S(1)} fusion(bf16[2,128,16,128]{3,1,2,0:T(8,128)(2,1)S(1)} %copy.20, bf16[1,128,16,128]{3,1,2,0:T(8,128)(2,1)S(1)} %copy-done.3, f32[3,16,64,128]{3,2,1,0:T(8,128)} %get-tuple-element.8, f32[3,16,64]{2,1,0:T(8,128)S(1)} %get-tuple-element.7), kind=kOutput, calls=%fused_computation.21 | convolution fusion | flops 104988672 | bytes 3944448 | tf_op jit(solution)/shard_map/ghqk,gkhd->gqhd/dot_general | solution.py:157
  159.2 0.5 copy.24
  159.7 0.2 copy.40
  159.9 0.9 slice.15
  (38 shorter events, 1.2 us)
Async XLA Ops:
  6.5 135.8 %all-gather.5.cloned.1.call-start = ((), (), s32[]{:S(2)}) async-start(), calls=%async_computation.1 | async-start | bytes 4128768 | tf_op jit(solution)/shard_map/all_gather | solution.py:130
  7.3 140.3 %all-gather.3.cloned.1.call-start = ((), (), s32[]{:S(2)}) async-start(), calls=%async_computation | async-start | bytes 4128768 | tf_op jit(solution)/shard_map/all_gather | solution.py:135
  127.2 4.7 %copy-start.5 = (s32[2,16]{1,0:T(2,128)S(1)}, s32[2,16]{1,0:T(2,128)}, u32[]{:S(2)}) copy-start(s32[2,16]{1,0:T(2,128)} %param.12) | copy-start | bytes 388
  127.2 5.0 %copy-start.2 = (bf16[128,2048]{1,0:T(8,128)(2,1)S(1)}, bf16[128,2048]{1,0:T(8,128)(2,1)}, u32[]{:S(2)}) copy-start(bf16[128,2048]{1,0:T(8,128)(2,1)} %param.7) | copy-start | bytes 1572868
  129.8 12.4 %collective-permute-start = (bf16[1,16,8,896]{3,2,1,0:T(8,128)(2,1)S(1)}, bf16[1,16,8,896]{3,2,1,0:T(8,128)(2,1)S(1)}, u32[]{:S(2)}, u32[]{:S(2)}) collective-permute-start(bf16[1,16,8,896]{3,2,1,0:T(8,128)(2,1)S(1)} %slice_bitcast_fusion), channel_id=1, source_target_pairs={{0,1},{1,2},{2,3},{3,4},{4,5},{5,6},{6,7},{7,8},{8,9},{9,10},{10,1... | collective-permute-start | bytes 688136 | tf_op jit(solution)/shard_map/ppermute | solution.py:24
  132.1 10.3 %copy-start.4 = (f32[896]{0:T(1024)S(1)}, f32[896]{0:T(1024)}, u32[]{:S(2)}) copy-start(f32[896]{0:T(1024)} %param.9) | copy-start | bytes 10756
  142.4 3.2 %copy-start.1 = (bf16[896,2048]{1,0:T(8,128)(2,1)S(1)}, bf16[896,2048]{1,0:T(8,128)(2,1)}, u32[]{:S(2)}) copy-start(bf16[896,2048]{1,0:T(8,128)(2,1)} %all-gather.5.cloned.1.call-done) | copy-start | bytes 11010052
  147.6 4.0 %copy-start = (bf16[896,2048]{1,0:T(8,128)(2,1)S(1)}, bf16[896,2048]{1,0:T(8,128)(2,1)}, u32[]{:S(2)}) copy-start(bf16[896,2048]{1,0:T(8,128)(2,1)} %all-gather.3.cloned.1.call-done) | copy-start | bytes 11010052
  153.5 3.6 %copy-start.3 = (bf16[1,128,16,128]{3,1,2,0:T(8,128)(2,1)S(1)}, bf16[1,128,16,128]{3,1,2,0:T(8,128)(2,1)}, u32[]{:S(2)}) copy-start(bf16[1,128,16,128]{3,1,2,0:T(8,128)(2,1)} %copy.19) | copy-start | bytes 1572868
Sparse Core Ops, SparseCore 0:
  9.5 45.4 all-gather.4
  57.1 42.7 all-gather.2

commit v3 on v2

--- a/solution.py
+++ b/solution.py
@@ -24,14 +24,16 @@
     return lax.ppermute(block, axis, route)
 
 
-def gathered_rows(ids, table_ref, length):
-    shape = (2 * length, 128)
+def gathered_rows(ids_list, table_ref, length):
+    pieces = []
+    for ids in ids_list:
+        for slot in range(2):
+            pieces.append(jnp.broadcast_to(ids[slot : slot + 1, :], (length, 128)))
+    sel = jnp.concatenate(pieces, axis=0)
+    shape = sel.shape
     sub = lax.broadcasted_iota(jnp.int32, shape, 0)
     lane = lax.broadcasted_iota(jnp.int32, shape, 1)
-    sel = jnp.where(
-        sub < length, jnp.broadcast_to(ids[0:1, :], shape), jnp.broadcast_to(ids[1:2, :], shape)
-    )
-    total = jnp.zeros((2 * length, table_ref.shape[1]), jnp.float32)
+    total = jnp.zeros((shape[0], table_ref.shape[1]), jnp.float32)
     for h in range(table_ref.shape[0] // 128):
         col = lane + h * 128
         hit = jnp.logical_and(col // length == sel, col % length == sub % length)
@@ -43,7 +45,7 @@
     return total.astype(table_ref.dtype)
 
 
-def fetch_kernel(length, wanted_ref, table_ref, out_ref, asked, outgoing, req_send, req_recv, rep_send, rep_recv):
+def fetch_kernel(length, group, wanted_ref, table_ref, out_ref, asked, outgoing, req_send, req_recv, rep_send, rep_recv):
     n = wanted_ref.shape[0]
     me = lax.axis_index("seq")
     dp = lax.axis_index("dp")
@@ -54,9 +56,9 @@
             device_id=(dp, peer), device_id_type=MESH,
         )
 
-    def reply(peer, slot):
+    def reply(step, peer, slot):
         return pltpu.make_async_remote_copy(
-            outgoing.at[peer], out_ref.at[slot], rep_send.at[peer], rep_recv.at[slot],
+            outgoing.at[step], out_ref.at[slot], rep_send.at[step], rep_recv.at[slot],
             device_id=(dp, peer), device_id_type=MESH,
         )
 
@@ -74,22 +76,42 @@
         return carry
 
     lax.fori_loop(1, n, ask, 0)
-    out_ref[me] = gathered_rows(wanted_ref[me], table_ref, length)
-
-    def serve(k, carry):
-        source = lax.rem(me + n - k, n)
-        request(source, source).wait_recv()
-        outgoing[source] = gathered_rows(asked[source], table_ref, length)
-        reply(source, me).start()
-        return carry
-
-    lax.fori_loop(1, n, serve, 0)
+    asked[me] = wanted_ref[me]
+
+    def serve(c, carry):
+        ids_list = []
+        for j in range(group):
+            k = c * group + j
+            source = lax.rem(me + n - k, n)
+
+            @pl.when(k > 0)
+            def _():
+                request(source, source).wait_recv()
+
+            ids_list.append(asked[source])
+        rows = gathered_rows(ids_list, table_ref, length)
+        outgoing[pl.ds(c * group, group)] = rows.reshape(group, 2 * length, rows.shape[-1])
+        for j in range(group):
+            k = c * group + j
+            source = lax.rem(me + n - k, n)
+
+            @pl.when(k == 0)
+            def _():
+                out_ref[me] = outgoing[k]
+
+            @pl.when(k > 0)
+            def _():
+                reply(k, source, me).start()
+
+        return carry
+
+    lax.fori_loop(0, n // group, serve, 0)
 
     def finish(k, carry):
         peer = lax.rem(me + k, n)
         request(peer, me).wait_send()
-        reply(peer, me).wait_send()
-        reply(peer, peer).wait_recv()
+        reply(k, lax.rem(me + n - k, n), me).wait_send()
+        reply(k, peer, peer).wait_recv()
         return carry
 
     lax.fori_loop(1, n, finish, 0)
@@ -99,7 +121,7 @@
     n = wanted.shape[0]
     width = table.shape[1]
     return pl.pallas_call(
-        functools.partial(fetch_kernel, length),
+        functools.partial(fetch_kernel, length, math.gcd(8, n)),
         out_shape=jax.ShapeDtypeStruct((n, 2 * length, width), table.dtype),
         in_specs=[pl.BlockSpec(memory_space=pltpu.VMEM)] * 2,
         out_specs=pl.BlockSpec(memory_space=pltpu.VMEM),

time: 168 us -> 168 us (level)
  Pallas kernels: 116 us -> 114 us
  transfers between devices with their start and end apart: 3 -> 3, of which waited for: 1 -> 1; matrix products, arithmetic and copies ran while one was open for 8% -> 8% of each run, Pallas kernels for 69% -> 68%
where the time goes in v3:
time: 168 us; the launch traced here: 167 us
  Pallas kernels  114 us (68%)
  matrix products  14.4 us (9%)
  between operations  13.7 us (8%)
  waiting for transfers between devices  10.8 us (6%)
  local copies, waits for them, and re-layouts  9.52 us (6%)
  other arithmetic  2.6 us (2%)
  starting transfers between devices  1.96 us (1%)
    pallas_call x1, Pallas kernels, fetch(): pl.pallas_call(functools.partial(fetch_kernel, length, math.gcd(8, n)), o...  114 us
    ppermute x1, waiting for transfers between devices, from_behind(): return lax.ppermute(block, axis, route)  9.33 us
    dot_general x2, matrix products, project(): jnp.dot(flat_rows, lax.all_gather(key_weight, 'dp', axis=1, tiled=True),...  4.36 us
    dot_general x2, matrix products, project(): jnp.dot(flat_rows, lax.all_gather(value_weight, 'dp', axis=1, tiled=True)...  4.35 us
    sub x1, matrix products, attend(): expo = jnp.exp(scores - row_max)  3.62 us
  transfers between devices with their start and end apart: 3, of which 1 were waited for; matrix products, arithmetic and copies ran while one was open for 8% of the time, Pallas kernels for 68%

profile of v3, /device:TPU:6, one launch (start us, length us, event | category | flops | bytes accessed | tf_op | source)
XLA Modules:
  0.0 167.0 jit_solution(3635832888946578886)
XLA Ops:
  6.5 0.7 all-gather.5.cloned.1.call-update
  7.3 0.7 all-gather.3.cloned.1.call-update
  8.0 0.8 reshape.174
  8.8 0.7 broadcast_add_fusion.1
  9.5 0.2 convert_reduce_fusion
  10.0 0.7 broadcast_multiply_fusion
  10.8 0.1 broadcast_in_dim.56
  10.9 0.7 pad.4.wanted_ref
  11.6 114.1 %shard_map.73 = bf16[64,16,896]{2,1,0:T(8,128)(2,1)} custom-call(s32[64,8,128]{2,1,0:T(8,128)} %pad.4.wanted_ref, bf16[256,896]{1,0:T(8,128)(2,1)} %bitcast.60), custom_call_target="tpu_custom_call" | custom-call | tf_op jit(solution)/shard_map/pallas_call | solution.py:123
  125.8 2.2 %gather_fusion = bf16[32,8,896]{2,1,0:T(8,128)(2,1)S(1)} fusion(bf16[128,8,896]{2,1,0:T(8,128)(2,1)} %bitcast.55, s32[1024]{0:T(1024)S(1)} %pad_clamp_fusion), kind=kCustom, calls=%fused_computation | custom fusion | bytes 917632 | tf_op jit(solution)/shard_map/jit(_take)/gather | solution.py:211
  128.0 0.3 multiply_reduce_fusion
  128.3 1.9 %collective-permute-start = (bf16[1,16,8,896]{3,2,1,0:T(8,128)(2,1)S(1)}, bf16[1,16,8,896]{3,2,1,0:T(8,128)(2,1)S(1)}, u32[]{:S(2)}, u32[]{:S(2)}) collective-permute-start(bf16[1,16,8,896]{3,2,1,0:T(8,128)(2,1)S(1)} %slice_bitcast_fusion), channel_id=1, source_target_pairs={{0,1},{1,2},{2,3},{3,4},{4,5},{5,6},{6,7},{7,8},{8,9},{9,10},{10,1... | collective-permute-start | bytes 688136 | tf_op jit(solution)/shard_map/ppermute | solution.py:24
  130.7 0.4 maximum_bitcast_fusion
  131.1 1.0 copy.25
  132.2 9.3 %collective-permute-done = bf16[1,16,8,896]{3,2,1,0:T(8,128)(2,1)S(1)} collective-permute-done((bf16[1,16,8,896]{3,2,1,0:T(8,128)(2,1)S(1)}, bf16[1,16,8,896]{3,2,1,0:T(8,128)(2,1)S(1)}, u32[]{:S(2)}, u32[]{:S(2)}) %collective-permute-start) | collective-permute-done | bytes 229408 | tf_op jit(solution)/shard_map/ppermute | solution.py:24
  141.5 0.1 fusion.26
  141.7 3.0 %fusion.23 = bf16[16,8,16,128]{3,1,2,0:T(8,128)(2,1)S(1)} fusion(bf16[896,2048]{1,0:T(8,128)(2,1)} %all-gather.5.cloned.1.call-done, bf16[1,16,8,896]{3,2,1,0:T(8,128)(2,1)S(1)} %collective-permute-done, f32[896]{0:T(1024)S(1)} %copy-done.4, f32[16,8]{1,0:T(8,128)S(1)} %add_rsqrt_fusion.1), kind=kOutput, calls=%fused_computation.23 | convolution fusion | flops 470482944 | bytes 4427776 | tf_op jit(solution)/shard_map/dot_general | solution.py:150
  144.8 0.1 copy.21
  145.0 1.4 fusion.18
  146.4 0.2 copy.27
  146.6 0.3 copy.22
  146.9 3.0 %fusion.22 = bf16[16,8,16,128]{3,1,2,0:T(8,128)(2,1)S(1)} fusion(bf16[896,2048]{1,0:T(8,128)(2,1)} %all-gather.3.cloned.1.call-done, bf16[1,16,8,896]{3,2,1,0:T(8,128)(2,1)S(1)} %collective-permute-done, f32[896]{0:T(1024)S(1)} %copy-done.4, f32[16,8]{1,0:T(8,128)S(1)} %add_rsqrt_fusion.1), kind=kOutput, calls=%fused_computation.22 | convolution fusion | flops 470482944 | bytes 4427776 | tf_op jit(solution)/shard_map/dot_general | solution.py:155
  149.9 0.1 copy.28
  150.0 0.9 copy.19
  150.9 1.4 fusion.17
  152.3 0.2 copy.29
  152.6 0.3 copy.20
  152.9 3.6 %fusion.48 = (f32[3,16,64]{2,1,0:T(8,128)S(1)}, f32[3,16,64,128]{3,2,1,0:T(8,128)}) fusion(bf16[2,128,16,128]{3,1,2,0:T(8,128)(2,1)S(1)} %copy.22, bf16[1,128,16,128]{3,1,2,0:T(8,128)(2,1)S(1)} %copy.21, bf16[3,64,16,128]{3,2,1,0:T(8,128)(2,1)} %bitcast.59), kind=kOutput, calls=%fused_computation.63 | convolution fusion | flops 102629504 | bytes 3944448 | tf_op jit(solution)/shard_map/sub | solution.py:177
  156.5 2.0 %fusion.19 = bf16[3,64,16,128]{3,1,2,0:T(8,128)(2,1)S(1)} fusion(bf16[2,128,16,128]{3,1,2,0:T(8,128)(2,1)S(1)} %copy.20, bf16[1,128,16,128]{3,1,2,0:T(8,128)(2,1)S(1)} %copy-done.3, f32[3,16,64,128]{3,2,1,0:T(8,128)} %get-tuple-element.8, f32[3,16,64]{2,1,0:T(8,128)S(1)} %get-tuple-element.7), kind=kOutput, calls=%fused_computation.21 | convolution fusion | flops 104988672 | bytes 3944448 | tf_op jit(solution)/shard_map/ghqk,gkhd->gqhd/dot_general | solution.py:179
  158.5 0.5 copy.24
  159.0 0.2 copy.40
  159.3 0.9 slice.15
  (38 shorter events, 1.2 us)
Async XLA Ops:
  6.5 135.1 %all-gather.5.cloned.1.call-start = ((), (), s32[]{:S(2)}) async-start(), calls=%async_computation.1 | async-start | bytes 4128768 | tf_op jit(solution)/shard_map/all_gather | solution.py:152
  7.3 139.6 %all-gather.3.cloned.1.call-start = ((), (), s32[]{:S(2)}) async-start(), calls=%async_computation | async-start | bytes 4128768 | tf_op jit(solution)/shard_map/all_gather | solution.py:157
  125.8 4.7 %copy-start.5 = (s32[2,16]{1,0:T(2,128)S(1)}, s32[2,16]{1,0:T(2,128)}, u32[]{:S(2)}) copy-start(s32[2,16]{1,0:T(2,128)} %param.12) | copy-start | bytes 388
  125.8 5.0 %copy-start.2 = (bf16[128,2048]{1,0:T(8,128)(2,1)S(1)}, bf16[128,2048]{1,0:T(8,128)(2,1)}, u32[]{:S(2)}) copy-start(bf16[128,2048]{1,0:T(8,128)(2,1)} %param.7) | copy-start | bytes 1572868
  128.3 13.2 %collective-permute-start = (bf16[1,16,8,896]{3,2,1,0:T(8,128)(2,1)S(1)}, bf16[1,16,8,896]{3,2,1,0:T(8,128)(2,1)S(1)}, u32[]{:S(2)}, u32[]{:S(2)}) collective-permute-start(bf16[1,16,8,896]{3,2,1,0:T(8,128)(2,1)S(1)} %slice_bitcast_fusion), channel_id=1, source_target_pairs={{0,1},{1,2},{2,3},{3,4},{4,5},{5,6},{6,7},{7,8},{8,9},{9,10},{10,1... | collective-permute-start | bytes 688136 | tf_op jit(solution)/shard_map/ppermute | solution.py:24
  130.6 11.1 %copy-start.4 = (f32[896]{0:T(1024)S(1)}, f32[896]{0:T(1024)}, u32[]{:S(2)}) copy-start(f32[896]{0:T(1024)} %param.9) | copy-start | bytes 10756
  141.7 3.2 %copy-start.1 = (bf16[896,2048]{1,0:T(8,128)(2,1)S(1)}, bf16[896,2048]{1,0:T(8,128)(2,1)}, u32[]{:S(2)}) copy-start(bf16[896,2048]{1,0:T(8,128)(2,1)} %all-gather.5.cloned.1.call-done) | copy-start | bytes 11010052
  146.9 4.0 %copy-start = (bf16[896,2048]{1,0:T(8,128)(2,1)S(1)}, bf16[896,2048]{1,0:T(8,128)(2,1)}, u32[]{:S(2)}) copy-start(bf16[896,2048]{1,0:T(8,128)(2,1)} %all-gather.3.cloned.1.call-done) | copy-start | bytes 11010052
  152.9 3.6 %copy-start.3 = (bf16[1,128,16,128]{3,1,2,0:T(8,128)(2,1)S(1)}, bf16[1,128,16,128]{3,1,2,0:T(8,128)(2,1)}, u32[]{:S(2)}) copy-start(bf16[1,128,16,128]{3,1,2,0:T(8,128)(2,1)} %copy.19) | copy-start | bytes 1572868
Sparse Core Ops, SparseCore 0:
  9.5 45.2 all-gather.4
  56.9 42.5 all-gather.2

commit v4 on v3

--- a/solution.py
+++ b/solution.py
@@ -45,10 +45,26 @@
     return total.astype(table_ref.dtype)
 
 
+def torus_step(k, across, sign):
+    i = k // across
+    j = lax.rem(k, across)
+    dz = sign * ((i + 1) // 2) * (2 * lax.rem(i, 2) - 1)
+    dy = sign * ((j + 1) // 2) * (2 * lax.rem(j, 2) - 1)
+    return dy, dz
+
+
 def fetch_kernel(length, group, wanted_ref, table_ref, out_ref, asked, outgoing, req_send, req_recv, rep_send, rep_recv):
     n = wanted_ref.shape[0]
     me = lax.axis_index("seq")
     dp = lax.axis_index("dp")
+    across = math.gcd(4, n)
+    depth = n // across
+
+    def peer_of(k, sign):
+        dy, dz = torus_step(k, across, sign)
+        y = lax.rem(me, across)
+        z = me // across
+        return lax.rem(z + dz + depth, depth) * across + lax.rem(y + dy + across, across)
 
     def request(peer, slot):
         return pltpu.make_async_remote_copy(
@@ -72,7 +88,7 @@
     pl.semaphore_wait(barrier, n - 1)
 
     def ask(k, carry):
-        request(lax.rem(me + k, n), me).start()
+        request(peer_of(k, 1), me).start()
         return carry
 
     lax.fori_loop(1, n, ask, 0)
@@ -82,7 +98,7 @@
         ids_list = []
         for j in range(group):
             k = c * group + j
-            source = lax.rem(me + n - k, n)
+            source = peer_of(k, -1)
 
             @pl.when(k > 0)
             def _():
@@ -93,7 +109,7 @@
         outgoing[pl.ds(c * group, group)] = rows.reshape(group, 2 * length, rows.shape[-1])
         for j in range(group):
             k = c * group + j
-            source = lax.rem(me + n - k, n)
+            source = peer_of(k, -1)
 
             @pl.when(k == 0)
             def _():
@@ -108,9 +124,9 @@
     lax.fori_loop(0, n // group, serve, 0)
 
     def finish(k, carry):
-        peer = lax.rem(me + k, n)
+        peer = peer_of(k, 1)
         request(peer, me).wait_send()
-        reply(k, lax.rem(me + n - k, n), me).wait_send()
+        reply(k, peer_of(k, -1), me).wait_send()
         reply(k, peer, peer).wait_recv()
         return carry
 

time: 168 us -> 166 us (0.988)
  the two profiles are of different devices: /device:TPU:6 before, /device:TPU:34 now
where the time goes in v4:
time: 166 us
  Pallas kernels  116 us (70%)
  matrix products  14.4 us (9%)
  between operations  13.7 us (8%)
  local copies, waits for them, and re-layouts  9.52 us (6%)
  waiting for transfers between devices  7.84 us (5%)
  starting transfers between devices  2.62 us (2%)
  other arithmetic  2.6 us (2%)
    pallas_call x1, Pallas kernels, fetch(): pl.pallas_call(functools.partial(fetch_kernel, length, math.gcd(8, n)), o...  116 us
    ppermute x1, waiting for transfers between devices, from_behind(): return lax.ppermute(block, axis, route)  6.39 us
    dot_general x2, matrix products, project(): jnp.dot(flat_rows, lax.all_gather(key_weight, 'dp', axis=1, tiled=True),...  4.36 us
    dot_general x2, matrix products, project(): jnp.dot(flat_rows, lax.all_gather(value_weight, 'dp', axis=1, tiled=True)...  4.36 us
    sub x1, matrix products, attend(): expo = jnp.exp(scores - row_max)  3.62 us
  transfers between devices with their start and end apart: 3, of which 1 were waited for; matrix products, arithmetic and copies ran while one was open for 8% of the time, Pallas kernels for 70%

profile of v4, /device:TPU:34, one launch (start us, length us, event | category | flops | bytes accessed | tf_op | source)
XLA Modules:
  0.0 166.2 jit_solution(1819785662742190582)
XLA Ops:
  6.5 0.7 all-gather.5.cloned.1.call-update
  7.3 0.7 all-gather.3.cloned.1.call-update
  8.0 0.8 reshape.174
  8.8 0.7 broadcast_add_fusion.1
  9.5 0.2 convert_reduce_fusion
  10.0 0.7 broadcast_multiply_fusion
  10.8 0.1 broadcast_in_dim.56
  10.9 0.7 pad.4.wanted_ref
  11.6 115.6 %shard_map.73 = bf16[64,16,896]{2,1,0:T(8,128)(2,1)} custom-call(s32[64,8,128]{2,1,0:T(8,128)} %pad.4.wanted_ref, bf16[256,896]{1,0:T(8,128)(2,1)} %bitcast.60), custom_call_target="tpu_custom_call" | custom-call | tf_op jit(solution)/shard_map/pallas_call | solution.py:139
  127.3 2.2 %gather_fusion = bf16[32,8,896]{2,1,0:T(8,128)(2,1)S(1)} fusion(bf16[128,8,896]{2,1,0:T(8,128)(2,1)} %bitcast.55, s32[1024]{0:T(1024)S(1)} %pad_clamp_fusion), kind=kCustom, calls=%fused_computation | custom fusion | bytes 917632 | tf_op jit(solution)/shard_map/jit(_take)/gather | solution.py:227
  129.5 0.3 multiply_reduce_fusion
  129.8 2.6 %collective-permute-start = (bf16[1,16,8,896]{3,2,1,0:T(8,128)(2,1)S(1)}, bf16[1,16,8,896]{3,2,1,0:T(8,128)(2,1)S(1)}, u32[]{:S(2)}, u32[]{:S(2)}) collective-permute-start(bf16[1,16,8,896]{3,2,1,0:T(8,128)(2,1)S(1)} %slice_bitcast_fusion), channel_id=1, source_target_pairs={{0,1},{1,2},{2,3},{3,4},{4,5},{5,6},{6,7},{7,8},{8,9},{9,10},{10,1... | collective-permute-start | bytes 688136 | tf_op jit(solution)/shard_map/ppermute | solution.py:24
  132.8 0.4 maximum_bitcast_fusion
  133.3 1.0 copy.25
  134.3 6.4 %collective-permute-done = bf16[1,16,8,896]{3,2,1,0:T(8,128)(2,1)S(1)} collective-permute-done((bf16[1,16,8,896]{3,2,1,0:T(8,128)(2,1)S(1)}, bf16[1,16,8,896]{3,2,1,0:T(8,128)(2,1)S(1)}, u32[]{:S(2)}, u32[]{:S(2)}) %collective-permute-start) | collective-permute-done | bytes 229408 | tf_op jit(solution)/shard_map/ppermute | solution.py:24
  140.7 0.1 fusion.26
  140.9 3.0 %fusion.23 = bf16[16,8,16,128]{3,1,2,0:T(8,128)(2,1)S(1)} fusion(bf16[896,2048]{1,0:T(8,128)(2,1)} %all-gather.5.cloned.1.call-done, bf16[1,16,8,896]{3,2,1,0:T(8,128)(2,1)S(1)} %collective-permute-done, f32[896]{0:T(1024)S(1)} %copy-done.4, f32[16,8]{1,0:T(8,128)S(1)} %add_rsqrt_fusion.1), kind=kOutput, calls=%fused_computation.23 | convolution fusion | flops 470482944 | bytes 4427776 | tf_op jit(solution)/shard_map/dot_general | solution.py:166
  144.0 0.1 copy.21
  144.1 1.4 fusion.18
  145.5 0.2 copy.27
  145.8 0.3 copy.22
  146.1 3.0 %fusion.22 = bf16[16,8,16,128]{3,1,2,0:T(8,128)(2,1)S(1)} fusion(bf16[896,2048]{1,0:T(8,128)(2,1)} %all-gather.3.cloned.1.call-done, bf16[1,16,8,896]{3,2,1,0:T(8,128)(2,1)S(1)} %collective-permute-done, f32[896]{0:T(1024)S(1)} %copy-done.4, f32[16,8]{1,0:T(8,128)S(1)} %add_rsqrt_fusion.1), kind=kOutput, calls=%fused_computation.22 | convolution fusion | flops 470482944 | bytes 4427776 | tf_op jit(solution)/shard_map/dot_general | solution.py:171
  149.1 0.1 copy.28
  149.2 0.9 copy.19
  150.1 1.4 fusion.17
  151.5 0.2 copy.29
  151.8 0.3 copy.20
  152.1 3.6 %fusion.48 = (f32[3,16,64]{2,1,0:T(8,128)S(1)}, f32[3,16,64,128]{3,2,1,0:T(8,128)}) fusion(bf16[2,128,16,128]{3,1,2,0:T(8,128)(2,1)S(1)} %copy.22, bf16[1,128,16,128]{3,1,2,0:T(8,128)(2,1)S(1)} %copy.21, bf16[3,64,16,128]{3,2,1,0:T(8,128)(2,1)} %bitcast.59), kind=kOutput, calls=%fused_computation.63 | convolution fusion | flops 102629504 | bytes 3944448 | tf_op jit(solution)/shard_map/sub | solution.py:193
  155.7 2.0 %fusion.19 = bf16[3,64,16,128]{3,1,2,0:T(8,128)(2,1)S(1)} fusion(bf16[2,128,16,128]{3,1,2,0:T(8,128)(2,1)S(1)} %copy.20, bf16[1,128,16,128]{3,1,2,0:T(8,128)(2,1)S(1)} %copy-done.3, f32[3,16,64,128]{3,2,1,0:T(8,128)} %get-tuple-element.8, f32[3,16,64]{2,1,0:T(8,128)S(1)} %get-tuple-element.7), kind=kOutput, calls=%fused_computation.21 | convolution fusion | flops 104988672 | bytes 3944448 | tf_op jit(solution)/shard_map/ghqk,gkhd->gqhd/dot_general | solution.py:195
  157.7 0.5 copy.24
  158.2 0.2 copy.40
  158.4 0.9 slice.15
  (38 shorter events, 1.2 us)
Async XLA Ops:
  6.5 134.3 %all-gather.5.cloned.1.call-start = ((), (), s32[]{:S(2)}) async-start(), calls=%async_computation.1 | async-start | bytes 4128768 | tf_op jit(solution)/shard_map/all_gather | solution.py:168
  7.3 138.8 %all-gather.3.cloned.1.call-start = ((), (), s32[]{:S(2)}) async-start(), calls=%async_computation | async-start | bytes 4128768 | tf_op jit(solution)/shard_map/all_gather | solution.py:173
  127.2 5.3 %copy-start.5 = (s32[2,16]{1,0:T(2,128)S(1)}, s32[2,16]{1,0:T(2,128)}, u32[]{:S(2)}) copy-start(s32[2,16]{1,0:T(2,128)} %param.12) | copy-start | bytes 388
  127.2 5.6 %copy-start.2 = (bf16[128,2048]{1,0:T(8,128)(2,1)S(1)}, bf16[128,2048]{1,0:T(8,128)(2,1)}, u32[]{:S(2)}) copy-start(bf16[128,2048]{1,0:T(8,128)(2,1)} %param.7) | copy-start | bytes 1572868
  129.8 10.9 %collective-permute-start = (bf16[1,16,8,896]{3,2,1,0:T(8,128)(2,1)S(1)}, bf16[1,16,8,896]{3,2,1,0:T(8,128)(2,1)S(1)}, u32[]{:S(2)}, u32[]{:S(2)}) collective-permute-start(bf16[1,16,8,896]{3,2,1,0:T(8,128)(2,1)S(1)} %slice_bitcast_fusion), channel_id=1, source_target_pairs={{0,1},{1,2},{2,3},{3,4},{4,5},{5,6},{6,7},{7,8},{8,9},{9,10},{10,1... | collective-permute-start | bytes 688136 | tf_op jit(solution)/shard_map/ppermute | solution.py:24
  132.7 8.1 %copy-start.4 = (f32[896]{0:T(1024)S(1)}, f32[896]{0:T(1024)}, u32[]{:S(2)}) copy-start(f32[896]{0:T(1024)} %param.9) | copy-start | bytes 10756
  140.9 3.3 %copy-start.1 = (bf16[896,2048]{1,0:T(8,128)(2,1)S(1)}, bf16[896,2048]{1,0:T(8,128)(2,1)}, u32[]{:S(2)}) copy-start(bf16[896,2048]{1,0:T(8,128)(2,1)} %all-gather.5.cloned.1.call-done) | copy-start | bytes 11010052
  146.1 4.0 %copy-start = (bf16[896,2048]{1,0:T(8,128)(2,1)S(1)}, bf16[896,2048]{1,0:T(8,128)(2,1)}, u32[]{:S(2)}) copy-start(bf16[896,2048]{1,0:T(8,128)(2,1)} %all-gather.3.cloned.1.call-done) | copy-start | bytes 11010052
  152.0 3.6 %copy-start.3 = (bf16[1,128,16,128]{3,1,2,0:T(8,128)(2,1)S(1)}, bf16[1,128,16,128]{3,1,2,0:T(8,128)(2,1)}, u32[]{:S(2)}) copy-start(bf16[1,128,16,128]{3,1,2,0:T(8,128)(2,1)} %copy.19) | copy-start | bytes 1572868
Sparse Core Ops, SparseCore 0:
  9.5 45.2 all-gather.4
  56.9 42.4 all-gather.2

commit v5 on v4

--- a/solution.py
+++ b/solution.py
@@ -53,8 +53,12 @@
     return dy, dz
 
 
-def fetch_kernel(length, group, wanted_ref, table_ref, out_ref, asked, outgoing, req_send, req_recv, rep_send, rep_recv):
+def fetch_kernel(
+    length, group, wanted_ref, table_ref, wk_ref, wv_ref, out_ref, wk_out, wv_out,
+    asked, outgoing, req_send, req_recv, rep_send, rep_recv, wk_send, wk_recv, wv_send, wv_recv, own_sem,
+):
     n = wanted_ref.shape[0]
+    nd = wk_out.shape[0]
     me = lax.axis_index("seq")
     dp = lax.axis_index("dp")
     across = math.gcd(4, n)
@@ -78,20 +82,51 @@
             device_id=(dp, peer), device_id_type=MESH,
         )
 
+    def weight(src, dst, send, recv, peer, slot):
+        return pltpu.make_async_remote_copy(
+            src, dst.at[slot], send.at[peer], recv.at[slot],
+            device_id=(peer, me), device_id_type=MESH,
+        )
+
+    def weights(peer, slot):
+        return (
+            weight(wk_ref, wk_out, wk_send, wk_recv, peer, slot),
+            weight(wv_ref, wv_out, wv_send, wv_recv, peer, slot),
+        )
+
+    own = (
+        pltpu.make_async_copy(wk_ref, wk_out.at[dp], own_sem.at[0]),
+        pltpu.make_async_copy(wv_ref, wv_out.at[dp], own_sem.at[1]),
+    )
+
     barrier = pltpu.get_barrier_semaphore()
 
     def greet(k, carry):
         pl.semaphore_signal(barrier, inc=1, device_id=(dp, lax.rem(me + k, n)), device_id_type=MESH)
         return carry
 
+    def greet_dp(k, carry):
+        pl.semaphore_signal(barrier, inc=1, device_id=(lax.rem(dp + k, nd), me), device_id_type=MESH)
+        return carry
+
     lax.fori_loop(1, n, greet, 0)
-    pl.semaphore_wait(barrier, n - 1)
+    lax.fori_loop(1, nd, greet_dp, 0)
+    pl.semaphore_wait(barrier, n - 1 + nd - 1)
 
     def ask(k, carry):
         request(peer_of(k, 1), me).start()
         return carry
 
     lax.fori_loop(1, n, ask, 0)
+
+    def share(k, carry):
+        for copy in weights(lax.rem(dp + k, nd), dp):
+            copy.start()
+        return carry
+
+    lax.fori_loop(1, nd, share, 0)
+    for copy in own:
+        copy.start()
     asked[me] = wanted_ref[me]
 
     def serve(c, carry):
@@ -132,15 +167,33 @@
 
     lax.fori_loop(1, n, finish, 0)
 
-
-def fetch(wanted, table, length):
+    def gathered(k, carry):
+        peer = lax.rem(dp + k, nd)
+        for copy in weights(peer, dp):
+            copy.wait_send()
+        for copy in weights(peer, peer):
+            copy.wait_recv()
+        return carry
+
+    lax.fori_loop(1, nd, gathered, 0)
+    for copy in own:
+        copy.wait()
+
+
+def fetch(wanted, table, key_weight, value_weight, length, nd):
     n = wanted.shape[0]
     width = table.shape[1]
+    vmem = pl.BlockSpec(memory_space=pltpu.VMEM)
+    anywhere = pl.BlockSpec(memory_space=pl.ANY)
     return pl.pallas_call(
         functools.partial(fetch_kernel, length, math.gcd(8, n)),
-        out_shape=jax.ShapeDtypeStruct((n, 2 * length, width), table.dtype),
-        in_specs=[pl.BlockSpec(memory_space=pltpu.VMEM)] * 2,
-        out_specs=pl.BlockSpec(memory_space=pltpu.VMEM),
+        out_shape=(
+            jax.ShapeDtypeStruct((n, 2 * length, width), table.dtype),
+            jax.ShapeDtypeStruct((nd,) + key_weight.shape, key_weight.dtype),
+            jax.ShapeDtypeStruct((nd,) + value_weight.shape, value_weight.dtype),
+        ),
+        in_specs=[vmem, vmem, anywhere, anywhere],
+        out_specs=(vmem, anywhere, anywhere),
         scratch_shapes=[
             pltpu.VMEM(wanted.shape, jnp.int32),
             pltpu.VMEM((n, 2 * length, width), table.dtype),
@@ -148,9 +201,14 @@
             pltpu.SemaphoreType.DMA((n,)),
             pltpu.SemaphoreType.DMA((n,)),
             pltpu.SemaphoreType.DMA((n,)),
+            pltpu.SemaphoreType.DMA((nd,)),
+            pltpu.SemaphoreType.DMA((nd,)),
+            pltpu.SemaphoreType.DMA((nd,)),
+            pltpu.SemaphoreType.DMA((nd,)),
+            pltpu.SemaphoreType.DMA((2,)),
         ],
         compiler_params=pltpu.CompilerParams(collective_id=0, has_side_effects=True),
-    )(wanted, table)
+    )(wanted, table, key_weight, value_weight)
 
 
 def normalize(nbr_rows, enc_gain):
@@ -163,16 +221,12 @@
     group_count = nbr_rows.shape[0]
     normed = normalize(nbr_rows, enc_gain)
     flat_rows = normed.reshape(-1, normed.shape[-1])
-    key_part = jnp.dot(
-        flat_rows,
-        lax.all_gather(key_weight, "dp", axis=1, tiled=True),
-        preferred_element_type=jnp.float32,
-    )
-    value_part = jnp.dot(
-        flat_rows,
-        lax.all_gather(value_weight, "dp", axis=1, tiled=True),
-        preferred_element_type=jnp.float32,
-    )
+    key_part = jnp.einsum(
+        "td,idc->tic", flat_rows, key_weight, preferred_element_type=jnp.float32
+    ).reshape(flat_rows.shape[0], -1)
+    value_part = jnp.einsum(
+        "td,idc->tic", flat_rows, value_weight, preferred_element_type=jnp.float32
+    ).reshape(flat_rows.shape[0], -1)
     keys_out = key_part.astype(jnp.bfloat16)
     values_out = value_part.astype(jnp.bfloat16)
     return (
@@ -222,7 +276,9 @@
     wanted = jnp.broadcast_to(wanted[:, :, None], (owners, capacity, 128))
     wanted = jnp.pad(wanted, ((0, 0), (0, 8 - capacity), (0, 0)), constant_values=-1)
     table = database.reshape(database.shape[0] * length, enc_width)
-    arrived = fetch(wanted, table, length)
+    arrived, key_weight, value_weight = fetch(
+        wanted, table, key_weight, value_weight, length, lax.axis_size("dp")
+    )
     arrived = arrived.reshape(owners * capacity, length, enc_width)
     fetched = jnp.take(arrived, shard_flat * capacity + slot_rank, axis=0).reshape(
         spans, nbr_count, length, enc_width

time: 166 us -> 161 us (0.970)
  the two profiles are of different devices: /device:TPU:34 before, /device:TPU:24 now
where the time goes in v5:
time: 161 us
  Pallas kernels  107 us (66%)
  local copies, waits for them, and re-layouts  23.5 us (15%)
  matrix products  15 us (9%)
  starting transfers between devices  12.2 us (8%)
  other arithmetic  2.6 us (2%)
    pallas_call x1, Pallas kernels, fetch(): pl.pallas_call(functools.partial(fetch_kernel, length, math.gcd(8, n)), o...  107 us
    ppermute x1, starting transfers between devices, from_behind(): return lax.ppermute(block, axis, route)  12.2 us
    dot_general x1, local copies, waits for them, and re-layouts, project(): jnp.einsum('td,idc->tic', flat_rows, key_weight, preferred_element_type=j...  6.28 us
    dot_general x1, local copies, waits for them, and re-layouts, project(): jnp.einsum('td,idc->tic', flat_rows, value_weight, preferred_element_type...  6.26 us
    dot_general x2, matrix products, project(): jnp.einsum('td,idc->tic', flat_rows, key_weight, preferred_element_type=j...  4.71 us
    dot_general x2, matrix products, project(): jnp.einsum('td,idc->tic', flat_rows, value_weight, preferred_element_type...  4.7 us
    unnamed x16, local copies, waits for them, and re-layouts  4.45 us
    sub x1, matrix products, attend(): expo = jnp.exp(scores - row_max)  3.56 us
  transfers between devices with their start and end apart: 1, of which 0 were waited for; matrix products, arithmetic and copies ran while one was open for 14% of the time, Pallas kernels for 0%

profile of v5, /device:TPU:24, one launch (start us, length us, event | category | flops | bytes accessed | tf_op | source)
XLA Modules:
  0.0 160.7 jit_solution(2561753679147303036)
XLA Ops:
  0.0 0.8 reshape.306
  0.8 0.2 convert_reduce_fusion
  1.0 0.7 broadcast_multiply_fusion
  1.7 0.7 broadcast_add_fusion.1
  2.9 0.7 pad.4.wanted_ref
  3.6 107.2 %shard_map.73 = (bf16[64,16,896]{2,1,0:T(8,128)(2,1)}, bf16[8,896,256]{2,1,0:T(8,128)(2,1)}, bf16[8,896,256]{2,1,0:T(8,128)(2,1)}) custom-call(s32[64,8,128]{2,1,0:T(8,128)} %pad.4.wanted_ref, bf16[256,896]{1,0:T(8,128)(2,1)} %bitcast.67, bf16[896,256]{1,0:T(8,128)(2,1)} %wk_ref.1, bf16[896,256]{1,0:T(8,128)(2,1)} %wv_ref.1), custom_call_target="tpu_custom_call" | custom-call | tf_op jit(solution)/shard_map/pallas_call | solution.py:188
  110.9 2.1 %gather_fusion = bf16[32,8,896]{2,1,0:T(8,128)(2,1)S(1)} fusion(bf16[128,8,896]{2,1,0:T(8,128)(2,1)} %bitcast.68, s32[1024]{0:T(1024)S(1)} %pad_clamp_fusion), kind=kCustom, calls=%fused_computation | custom fusion | bytes 917632 | tf_op jit(solution)/shard_map/jit(_take)/gather | solution.py:283
  113.0 0.3 multiply_reduce_fusion
  113.3 12.2 %collective-permute-start = (bf16[1,16,8,896]{3,2,1,0:T(8,128)(2,1)S(1)}, bf16[1,16,8,896]{3,2,1,0:T(8,128)(2,1)S(1)}, u32[]{:S(2)}, u32[]{:S(2)}) collective-permute-start(bf16[1,16,8,896]{3,2,1,0:T(8,128)(2,1)S(1)} %slice_bitcast_fusion), channel_id=1, source_target_pairs={{0,1},{1,2},{2,3},{3,4},{4,5},{5,6},{6,7},{7,8},{8,9},{9,10},{10,1... | collective-permute-start | bytes 688136 | tf_op jit(solution)/shard_map/ppermute | solution.py:24
  125.6 6.3 %copy.24 = bf16[8,256,896]{2,1,0:T(8,128)(2,1)} copy(bf16[8,256,896]{1,2,0:T(8,128)(2,1)} %bitcast.61) | data formatting | bytes 7340032 | tf_op jit(solution)/shard_map/td,idc->tic/dot_general | solution.py:224
  132.0 3.4 %fusion.18 = bf16[32,8,16,128]{3,1,2,0:T(8,128)(2,1)S(1)} fusion(bf16[2048,896]{1,0:T(8,128)(2,1)} %bitcast.54, f32[896]{0:T(1024)S(1)} %copy-done.3, f32[32,8]{1,0:T(8,128)S(1)} %add_rsqrt_fusion, bf16[32,8,896]{2,1,0:T(8,128)(2,1)S(1)} %gather_fusion, pred[32]{0:T(512)(128)(4,1)S(1)} %broadcast_in_dim.54), kind=kOutput, calls=%fused_computation.20 | convolution fusion | flops 941195264 | bytes 5181984 | tf_op jit(solution)/shard_map/td,idc->tic/dot_general | solution.py:224
  135.4 0.2 copy.31
  135.7 0.3 copy.26
  136.0 0.7 copy-done.2
  136.7 0.4 maximum_bitcast_fusion
  137.1 1.1 copy.29
  138.2 6.3 %copy.21 = bf16[8,256,896]{2,1,0:T(8,128)(2,1)} copy(bf16[8,256,896]{1,2,0:T(8,128)(2,1)} %bitcast.60) | data formatting | bytes 7340032 | tf_op jit(solution)/shard_map/td,idc->tic/dot_general | solution.py:227
  144.4 3.4 %fusion.17 = bf16[32,8,16,128]{3,1,2,0:T(8,128)(2,1)S(1)} fusion(bf16[2048,896]{1,0:T(8,128)(2,1)} %bitcast.56, f32[896]{0:T(1024)S(1)} %copy-done.3, f32[32,8]{1,0:T(8,128)S(1)} %add_rsqrt_fusion, bf16[32,8,896]{2,1,0:T(8,128)(2,1)S(1)} %gather_fusion, pred[32]{0:T(512)(128)(4,1)S(1)} %broadcast_in_dim.54), kind=kOutput, calls=%fused_computation.19 | convolution fusion | flops 941195264 | bytes 5181984 | tf_op jit(solution)/shard_map/td,idc->tic/dot_general | solution.py:227
  147.9 0.2 copy.33
  148.1 0.3 copy.23
  148.4 0.1 fusion.26
  148.5 1.4 copy-done
  149.9 1.3 fusion.23
  151.3 0.1 copy.25
  151.5 0.4 copy-done.1
  151.9 1.3 fusion.22
  153.4 0.1 copy.22
  153.5 3.6 %fusion.53 = (f32[3,16,64]{2,1,0:T(8,128)S(1)}, f32[3,16,64,128]{3,2,1,0:T(8,128)}) fusion(bf16[2,128,16,128]{3,1,2,0:T(8,128)(2,1)S(1)} %copy.26, bf16[1,128,16,128]{3,1,2,0:T(8,128)(2,1)S(1)} %copy.25, bf16[3,64,16,128]{3,2,1,0:T(8,128)(2,1)} %bitcast.66), kind=kOutput, calls=%fused_computation.65 | convolution fusion | flops 102629504 | bytes 3944448 | tf_op jit(solution)/shard_map/sub | solution.py:247
  157.1 2.0 %fusion.19 = bf16[3,64,16,128]{3,1,2,0:T(8,128)(2,1)S(1)} fusion(bf16[2,128,16,128]{3,1,2,0:T(8,128)(2,1)S(1)} %copy.23, bf16[1,128,16,128]{3,1,2,0:T(8,128)(2,1)S(1)} %copy.22, f32[3,16,64,128]{3,2,1,0:T(8,128)} %get-tuple-element.14, f32[3,16,64]{2,1,0:T(8,128)S(1)} %get-tuple-element.13), kind=kOutput, calls=%fused_computation.21 | convolution fusion | flops 104988672 | bytes 3944448 | tf_op jit(solution)/shard_map/ghqk,gkhd->gqhd/dot_general | solution.py:249
  159.1 0.5 copy.28
  159.6 0.2 copy.44
  159.8 0.9 slice.15
  (30 shorter events, 1.1 us)
Async XLA Ops:
  113.3 35.1 %collective-permute-start = (bf16[1,16,8,896]{3,2,1,0:T(8,128)(2,1)S(1)}, bf16[1,16,8,896]{3,2,1,0:T(8,128)(2,1)S(1)}, u32[]{:S(2)}, u32[]{:S(2)}) collective-permute-start(bf16[1,16,8,896]{3,2,1,0:T(8,128)(2,1)S(1)} %slice_bitcast_fusion), channel_id=1, source_target_pairs={{0,1},{1,2},{2,3},{3,4},{4,5},{5,6},{6,7},{7,8},{8,9},{9,10},{10,1... | collective-permute-start | bytes 688136 | tf_op jit(solution)/shard_map/ppermute | solution.py:24
  125.6 6.3 %copy-start.4 = (s32[2,16]{1,0:T(2,128)S(1)}, s32[2,16]{1,0:T(2,128)}, u32[]{:S(2)}) copy-start(s32[2,16]{1,0:T(2,128)} %param.12) | copy-start | bytes 388
  125.6 6.4 %copy-start.3 = (f32[896]{0:T(1024)S(1)}, f32[896]{0:T(1024)}, u32[]{:S(2)}) copy-start(f32[896]{0:T(1024)} %param.9) | copy-start | bytes 10756
  135.7 1.0 copy-start.2
  147.8 2.0 %copy-start = (bf16[8,256,896]{2,1,0:T(8,128)(2,1)S(1)}, bf16[8,256,896]{2,1,0:T(8,128)(2,1)}, u32[]{:S(2)}) copy-start(bf16[8,256,896]{2,1,0:T(8,128)(2,1)} %copy.24) | copy-start | bytes 11010052
  149.9 2.0 %copy-start.1 = (bf16[8,256,896]{2,1,0:T(8,128)(2,1)S(1)}, bf16[8,256,896]{2,1,0:T(8,128)(2,1)}, u32[]{:S(2)}) copy-start(bf16[8,256,896]{2,1,0:T(8,128)(2,1)} %copy.21) | copy-start | bytes 11010052

commit v6 on v5

--- a/solution.py
+++ b/solution.py
@@ -58,7 +58,7 @@
     asked, outgoing, req_send, req_recv, rep_send, rep_recv, wk_send, wk_recv, wv_send, wv_recv, own_sem,
 ):
     n = wanted_ref.shape[0]
-    nd = wk_out.shape[0]
+    nd = wk_out.shape[1] // wk_ref.shape[1]
     me = lax.axis_index("seq")
     dp = lax.axis_index("dp")
     across = math.gcd(4, n)
@@ -82,9 +82,11 @@
             device_id=(dp, peer), device_id_type=MESH,
         )
 
+    cols = wk_ref.shape[1]
+
     def weight(src, dst, send, recv, peer, slot):
         return pltpu.make_async_remote_copy(
-            src, dst.at[slot], send.at[peer], recv.at[slot],
+            src, dst.at[:, pl.ds(slot * cols, cols)], send.at[peer], recv.at[slot],
             device_id=(peer, me), device_id_type=MESH,
         )
 
@@ -95,8 +97,8 @@
         )
 
     own = (
-        pltpu.make_async_copy(wk_ref, wk_out.at[dp], own_sem.at[0]),
-        pltpu.make_async_copy(wv_ref, wv_out.at[dp], own_sem.at[1]),
+        pltpu.make_async_copy(wk_ref, wk_out.at[:, pl.ds(dp * cols, cols)], own_sem.at[0]),
+        pltpu.make_async_copy(wv_ref, wv_out.at[:, pl.ds(dp * cols, cols)], own_sem.at[1]),
     )
 
     barrier = pltpu.get_barrier_semaphore()
@@ -189,8 +191,8 @@
         functools.partial(fetch_kernel, length, math.gcd(8, n)),
         out_shape=(
             jax.ShapeDtypeStruct((n, 2 * length, width), table.dtype),
-            jax.ShapeDtypeStruct((nd,) + key_weight.shape, key_weight.dtype),
-            jax.ShapeDtypeStruct((nd,) + value_weight.shape, value_weight.dtype),
+            jax.ShapeDtypeStruct((key_weight.shape[0], nd * key_weight.shape[1]), key_weight.dtype),
+            jax.ShapeDtypeStruct((value_weight.shape[0], nd * value_weight.shape[1]), value_weight.dtype),
         ),
         in_specs=[vmem, vmem, anywhere, anywhere],
         out_specs=(vmem, anywhere, anywhere),
@@ -221,12 +223,8 @@
     group_count = nbr_rows.shape[0]
     normed = normalize(nbr_rows, enc_gain)
     flat_rows = normed.reshape(-1, normed.shape[-1])
-    key_part = jnp.einsum(
-        "td,idc->tic", flat_rows, key_weight, preferred_element_type=jnp.float32
-    ).reshape(flat_rows.shape[0], -1)
-    value_part = jnp.einsum(
-        "td,idc->tic", flat_rows, value_weight, preferred_element_type=jnp.float32
-    ).reshape(flat_rows.shape[0], -1)
+    key_part = jnp.dot(flat_rows, key_weight, preferred_element_type=jnp.float32)
+    value_part = jnp.dot(flat_rows, value_weight, preferred_element_type=jnp.float32)
     keys_out = key_part.astype(jnp.bfloat16)
     values_out = value_part.astype(jnp.bfloat16)
     return (

time: 161 us -> 147 us (0.913)
  local copies, waits for them, and re-layouts: 23.5 us -> 12 us
  matrix products: 15 us -> 11.9 us
    dot_general x2 -> x0, local copies, waits for them, and re-layouts: 12.5 us -> none  [the longest x1 6.28 us: project(): jnp.einsum('td,idc->tic', flat_rows, key_weight, preferred_element_type=j...]
    dot_general x4, matrix products: 9.41 us -> 6.37 us  [the longest x2 4.19 us: project(): jnp.dot(flat_rows, key_weight, preferred_element_type=jnp.float32)]
  transfers between devices with their start and end apart: 1 -> 1, of which waited for: 0 -> 0; matrix products, arithmetic and copies ran while one was open for 14% -> 5% of each run, Pallas kernels for 0% -> 0%
where the time goes in v6:
time: 147 us; the launch traced here: 146 us
  Pallas kernels  107 us (73%)
  starting transfers between devices  12.2 us (8%)
  local copies, waits for them, and re-layouts  12 us (8%)
  matrix products  11.9 us (8%)
  other arithmetic  2.6 us (2%)
    pallas_call x1, Pallas kernels, fetch(): pl.pallas_call(functools.partial(fetch_kernel, length, math.gcd(8, n)), o...  107 us
    ppermute x1, starting transfers between devices, from_behind(): return lax.ppermute(block, axis, route)  12.2 us
    dot_general x2, matrix products, project(): jnp.dot(flat_rows, key_weight, preferred_element_type=jnp.float32)  4.19 us
    unnamed x16, local copies, waits for them, and re-layouts  3.68 us
    sub x1, matrix products, attend(): expo = jnp.exp(scores - row_max)  3.46 us
  transfers between devices with their start and end apart: 1, of which 0 were waited for; matrix products, arithmetic and copies ran while one was open for 5% of the time, Pallas kernels for 0%

profile of v6, /device:TPU:24, one launch (start us, length us, event | category | flops | bytes accessed | tf_op | source)
XLA Modules:
  0.0 146.3 jit_solution(15096624244639710705)
XLA Ops:
  0.0 0.8 reshape.174
  0.8 0.2 convert_reduce_fusion
  1.0 0.7 broadcast_multiply_fusion
  1.7 0.7 broadcast_add_fusion.1
  2.8 0.1 broadcast_in_dim.56
  2.9 0.7 pad.4.wanted_ref
  3.6 107.3 %shard_map.73 = (bf16[64,16,896]{2,1,0:T(8,128)(2,1)}, bf16[896,2048]{1,0:T(8,128)(2,1)}, bf16[896,2048]{1,0:T(8,128)(2,1)}) custom-call(s32[64,8,128]{2,1,0:T(8,128)} %pad.4.wanted_ref, bf16[256,896]{1,0:T(8,128)(2,1)} %bitcast.59, bf16[896,256]{1,0:T(8,128)(2,1)} %wk_ref.1, bf16[896,256]{1,0:T(8,128)(2,1)} %wv_ref.1), custom_call_target="tpu_custom_call" | custom-call | tf_op jit(solution)/shard_map/pallas_call | solution.py:190
  111.0 2.1 %gather_fusion = bf16[32,8,896]{2,1,0:T(8,128)(2,1)S(1)} fusion(bf16[128,8,896]{2,1,0:T(8,128)(2,1)} %bitcast.60, s32[1024]{0:T(1024)S(1)} %pad_clamp_fusion), kind=kCustom, calls=%fused_computation | custom fusion | bytes 917632 | tf_op jit(solution)/shard_map/jit(_take)/gather | solution.py:281
  113.1 0.3 multiply_reduce_fusion
  113.4 12.2 %collective-permute-start = (bf16[1,16,8,896]{3,2,1,0:T(8,128)(2,1)S(1)}, bf16[1,16,8,896]{3,2,1,0:T(8,128)(2,1)S(1)}, u32[]{:S(2)}, u32[]{:S(2)}) collective-permute-start(bf16[1,16,8,896]{3,2,1,0:T(8,128)(2,1)S(1)} %slice_bitcast_fusion), channel_id=1, source_target_pairs={{0,1},{1,2},{2,3},{3,4},{4,5},{5,6},{6,7},{7,8},{8,9},{9,10},{10,1... | collective-permute-start | bytes 688136 | tf_op jit(solution)/shard_map/ppermute | solution.py:24
  126.0 3.4 %fusion.18 = bf16[32,8,16,128]{3,1,2,0:T(8,128)(2,1)S(1)} fusion(bf16[896,2048]{1,0:T(8,128)(2,1)} %get-tuple-element.10, bf16[32,8,896]{2,1,0:T(8,128)(2,1)S(1)} %gather_fusion, f32[896]{0:T(1024)S(1)} %copy-done.3, f32[256]{0:T(256)S(1)} %rsqrt.21, pred[256]{0:T(512)(128)(4,1)S(1)} %broadcast_in_dim.59), kind=kOutput, calls=%fused_computation.20 | convolution fusion | flops 941195264 | bytes 5182208 | tf_op jit(solution)/shard_map/dot_general | solution.py:226
  129.4 0.2 copy.27
  129.7 0.3 copy.22
  130.1 0.7 copy-done.2
  130.7 0.4 maximum_bitcast_fusion
  131.1 0.2 copy.25
  131.3 0.6 copy-done
  131.9 1.4 fusion.17
  133.3 0.2 copy.29
  133.5 0.3 copy.20
  133.8 0.1 fusion.26
  134.0 1.4 copy-done.1
  135.3 0.8 fusion.23
  136.1 0.1 copy.26
  136.2 1.0 copy.21
  137.2 0.8 fusion.22
  138.1 0.9 copy.19
  139.0 3.5 %fusion.48 = (f32[3,16,64]{2,1,0:T(8,128)S(1)}, f32[3,16,64,128]{3,2,1,0:T(8,128)}) fusion(bf16[2,128,16,128]{3,1,2,0:T(8,128)(2,1)S(1)} %copy.22, bf16[1,128,16,128]{3,1,2,0:T(8,128)(2,1)} %copy.21, bf16[3,64,16,128]{3,2,1,0:T(8,128)(2,1)S(1)} %bitcast.58), kind=kOutput, calls=%fused_computation.63 | convolution fusion | flops 102629504 | bytes 3944448 | tf_op jit(solution)/shard_map/sub | solution.py:245
  142.5 2.1 %fusion.19 = bf16[3,64,16,128]{3,1,2,0:T(8,128)(2,1)S(1)} fusion(bf16[2,128,16,128]{3,1,2,0:T(8,128)(2,1)S(1)} %copy.20, bf16[1,128,16,128]{3,1,2,0:T(8,128)(2,1)} %copy.19, f32[3,16,64,128]{3,2,1,0:T(8,128)} %get-tuple-element.14, f32[3,16,64]{2,1,0:T(8,128)S(1)} %get-tuple-element.13), kind=kOutput, calls=%fused_computation.21 | convolution fusion | flops 104988672 | bytes 3944448 | tf_op jit(solution)/shard_map/ghqk,gkhd->gqhd/dot_general | solution.py:247
  144.6 0.5 copy.24
  145.2 0.2 copy.40
  145.4 0.9 slice.15
  (30 shorter events, 1.1 us)
Async XLA Ops:
  110.9 14.9 %copy-start.4 = (s32[2,16]{1,0:T(2,128)S(1)}, s32[2,16]{1,0:T(2,128)}, u32[]{:S(2)}) copy-start(s32[2,16]{1,0:T(2,128)} %param.12) | copy-start | bytes 388
  110.9 15.1 %copy-start.3 = (f32[896]{0:T(1024)S(1)}, f32[896]{0:T(1024)}, u32[]{:S(2)}) copy-start(f32[896]{0:T(1024)} %param.9) | copy-start | bytes 10756
  113.4 20.4 %collective-permute-start = (bf16[1,16,8,896]{3,2,1,0:T(8,128)(2,1)S(1)}, bf16[1,16,8,896]{3,2,1,0:T(8,128)(2,1)S(1)}, u32[]{:S(2)}, u32[]{:S(2)}) collective-permute-start(bf16[1,16,8,896]{3,2,1,0:T(8,128)(2,1)S(1)} %slice_bitcast_fusion), channel_id=1, source_target_pairs={{0,1},{1,2},{2,3},{3,4},{4,5},{5,6},{6,7},{7,8},{8,9},{9,10},{10,1... | collective-permute-start | bytes 688136 | tf_op jit(solution)/shard_map/ppermute | solution.py:24
  129.7 1.0 copy-start.2
  129.7 2.2 %copy-start = (bf16[896,2048]{1,0:T(8,128)(2,1)S(1)}, bf16[896,2048]{1,0:T(8,128)(2,1)}, u32[]{:S(2)}) copy-start(bf16[896,2048]{1,0:T(8,128)(2,1)} %get-tuple-element.9) | copy-start | bytes 11010052
  133.3 2.0 %copy-start.1 = (bf16[896,2048]{1,0:T(8,128)(2,1)S(1)}, bf16[896,2048]{1,0:T(8,128)(2,1)}, u32[]{:S(2)}) copy-start(bf16[896,2048]{1,0:T(8,128)(2,1)} %get-tuple-element.10) | copy-start | bytes 11010052

commit v7 on v6

--- a/solution.py
+++ b/solution.py
@@ -281,11 +281,6 @@
     fetched = jnp.take(arrived, shard_flat * capacity + slot_rank, axis=0).reshape(
         spans, nbr_count, length, enc_width
     )
-    prior_rows = from_behind(fetched[-1:], ("dp", "seq"), 1)
-    keys_own, values_own = project(fetched, enc_gain, key_weight, value_weight)
-    keys_prior, values_prior = project(prior_rows, enc_gain, key_weight, value_weight)
-    keys_all = jnp.concatenate([keys_prior, keys_own], axis=0)
-    values_all = jnp.concatenate([values_prior, values_own], axis=0)
     token_count = queries.shape[0]
     columns = queries.shape[1]
     padded = jnp.concatenate(
@@ -297,8 +292,13 @@
         axis=0,
     )
     grouped = padded.reshape(spans + 1, SPAN, columns)
-    return attend(grouped, keys_all, values_all)[1 : 1 + token_count]
-
+    keys_own, values_own = project(fetched, enc_gain, key_weight, value_weight)
+    own_out = attend(grouped[1:], keys_own, values_own)
+    last_rows, own_out = lax.optimization_barrier((fetched[-1:], own_out))
+    prior_rows = from_behind(last_rows, ("dp", "seq"), 1)
+    keys_prior, values_prior = project(prior_rows, enc_gain, key_weight, value_weight)
+    prior_out = attend(grouped[:1], keys_prior, values_prior)
+    return jnp.concatenate([prior_out[1:], own_out[: token_count - SPAN + 1]], axis=0)
 
 def solution(mesh):
     return jax.shard_map(

time: 147 us -> 155 us (1.054)
  the two profiles are of different devices: /device:TPU:24 before, /device:TPU:38 now
where the time goes in v7:
time: 155 us; the launch traced here: 154 us
  Pallas kernels  116 us (75%)
  matrix products  15.1 us (10%)
  waiting for transfers between devices  8.31 us (5%)
  local copies, waits for them, and re-layouts  7.2 us (5%)
  other arithmetic  4.7 us (3%)
  starting transfers between devices  2.85 us (2%)
    pallas_call x1, Pallas kernels, fetch(): pl.pallas_call(functools.partial(fetch_kernel, length, math.gcd(8, n)), o...  116 us
    ppermute x1, waiting for transfers between devices, from_behind(): return lax.ppermute(block, axis, route)  8.31 us
    dot_general x2, matrix products, project(): jnp.dot(flat_rows, key_weight, preferred_element_type=jnp.float32)  6.22 us
    dot_general x2, matrix products, attend(): jnp.einsum('ghqk,gkhd->gqhd', probs_low, value_heads, preferred_element_t...  5.41 us
  transfers between devices with their start and end apart: 1, of which 1 were waited for; matrix products, arithmetic and copies ran while one was open for 0% of the time, Pallas kernels for 0%

profile of v7, /device:TPU:38, one launch (start us, length us, event | category | flops | bytes accessed | tf_op | source)
XLA Modules:
  0.0 154.4 jit_solution(17194985148649294571)
XLA Ops:
  0.0 0.8 reshape.202
  0.8 0.2 convert_reduce_fusion
  1.1 0.7 broadcast_multiply_fusion
  1.8 0.7 compare_and_fusion
  2.5 0.7 broadcast_add_fusion.1
  3.7 1.1 fusion.14
  4.8 0.1 copy.32
  4.9 0.1 broadcast_in_dim.54
  5.1 0.7 pad.6.wanted_ref
  5.8 116.0 %shard_map.73 = (bf16[64,16,896]{2,1,0:T(8,128)(2,1)}, bf16[896,2048]{1,0:T(8,128)(2,1)}, bf16[896,2048]{1,0:T(8,128)(2,1)}) custom-call(s32[64,8,128]{2,1,0:T(8,128)} %pad.6.wanted_ref, bf16[256,896]{1,0:T(8,128)(2,1)} %bitcast.82, bf16[896,256]{1,0:T(8,128)(2,1)} %wk_ref.1, bf16[896,256]{1,0:T(8,128)(2,1)} %wv_ref.1), custom_call_target="tpu_custom_call" | custom-call | tf_op jit(solution)/shard_map/pallas_call | solution.py:190
  121.8 2.1 %gather_fusion = bf16[32,8,896]{2,1,0:T(8,128)(2,1)S(1)} fusion(bf16[128,8,896]{2,1,0:T(8,128)(2,1)} %bitcast.83, s32[1024]{0:T(1024)S(1)} %pad_clamp_fusion), kind=kCustom, calls=%fused_computation | custom fusion | bytes 917632 | tf_op jit(solution)/shard_map/jit(_take)/gather | solution.py:281
  123.9 0.3 multiply_reduce_fusion
  124.3 3.4 %fusion.5 = bf16[32,8,16,128]{3,1,2,0:T(8,128)(2,1)S(1)} fusion(bf16[896,2048]{1,0:T(8,128)(2,1)} %get-tuple-element.12, bf16[32,8,896]{2,1,0:T(8,128)(2,1)S(1)} %gather_fusion, f32[896]{0:T(1024)S(1)} %copy-done.3, f32[256]{0:T(256)S(1)} %rsqrt.20, pred[256]{0:T(512)(128)(4,1)S(1)} %broadcast_in_dim.57), kind=kOutput, calls=%fused_computation.10 | convolution fusion | flops 941195264 | bytes 5182208 | tf_op jit(solution)/shard_map/dot_general | solution.py:226
  127.8 0.2 copy.33
  128.0 0.8 convolution_multiply_fusion
  128.8 0.6 fusion.35
  129.4 0.3 copy-done
  129.8 1.4 fusion.4
  131.2 0.2 copy.34
  131.4 3.6 %fusion.10 = bf16[2,64,16,128]{3,1,2,0:T(8,128)(2,1)S(1)} fusion(bf16[2,128,16,128]{3,2,1,0:T(8,128)(2,1)S(1)} %bitcast.79, f32[2,16,64]{2,1,0:T(8,128)S(1)} %fusion.35, f32[2,16,64,128]{3,2,1,0:T(8,128)S(1)} %convolution_multiply_fusion), kind=kOutput, calls=%fused_computation.17 | convolution fusion | flops 68159616 | bytes 2629632 | tf_op jit(solution)/shard_map/ghqk,gkhd->gqhd/dot_general | solution.py:247
  135.0 0.3 copy.24
  135.4 0.1 copy.57
  135.5 2.9 %collective-permute-start = (bf16[1,16,8,896]{3,2,1,0:T(8,128)(2,1)S(1)}, bf16[1,16,8,896]{3,2,1,0:T(8,128)(2,1)S(1)}, u32[]{:S(2)}, u32[]{:S(2)}) collective-permute-start(bf16[1,16,8,896]{3,2,1,0:T(8,128)(2,1)S(1)} %slice_bitcast_fusion), channel_id=1, source_target_pairs={{0,1},{1,2},{2,3},{3,4},{4,5},{5,6},{6,7},{7,8},{8,9},{9,10},{10,1... | collective-permute-start | bytes 688136 | tf_op jit(solution)/shard_map/ppermute | solution.py:24
  138.4 8.3 %collective-permute-done = bf16[1,16,8,896]{3,2,1,0:T(8,128)(2,1)S(1)} collective-permute-done((bf16[1,16,8,896]{3,2,1,0:T(8,128)(2,1)S(1)}, bf16[1,16,8,896]{3,2,1,0:T(8,128)(2,1)S(1)}, u32[]{:S(2)}, u32[]{:S(2)}) %collective-permute-start) | collective-permute-done | bytes 229408 | tf_op jit(solution)/shard_map/ppermute | solution.py:24
  146.7 0.1 fusion.21
  146.9 2.8 %fusion.8 = bf16[16,16,8,128]{3,2,1,0:T(8,128)(2,1)S(1)} fusion(bf16[896,2048]{1,0:T(8,128)(2,1)} %get-tuple-element.12, bf16[1,16,8,896]{3,2,1,0:T(8,128)(2,1)S(1)} %collective-permute-done, f32[896]{0:T(1024)S(1)} %copy-done.3, f32[16,8]{1,0:T(8,128)S(1)} %add_rsqrt_fusion.1), kind=kOutput, calls=%fused_computation.15 | convolution fusion | flops 470482944 | bytes 4427776 | tf_op jit(solution)/shard_map/dot_general | solution.py:226
  149.7 0.5 convolution_multiply_fusion.1
  150.2 0.3 fusion.36
  150.5 0.8 fusion.7
  151.3 1.8 %fusion.11 = bf16[1,64,16,128]{3,1,2,0:T(8,128)(2,1)S(1)} fusion(bf16[16,16,8,128]{3,2,1,0:T(8,128)(2,1)S(1)} %fusion.7, f32[16,64]{1,0:T(8,128)S(1)} %fusion.36, f32[16,64,128]{2,1,0:T(8,128)S(1)} %convolution_multiply_fusion.1), kind=kOutput, calls=%fused_computation.20 | convolution fusion | flops 34079872 | bytes 1314816 | tf_op jit(solution)/shard_map/ghqk,gkhd->gqhd/dot_general | solution.py:247
  153.2 0.2 copy.58
  153.5 0.9 pad_maximum_fusion
  (28 shorter events, 1.1 us)
Async XLA Ops:
  0.0 124.3 %copy-start.3 = (f32[896]{0:T(1024)S(1)}, f32[896]{0:T(1024)}, u32[]{:S(2)}) copy-start(f32[896]{0:T(1024)} %param.9) | copy-start | bytes 10756
  127.7 2.0 %copy-start = (bf16[896,2048]{1,0:T(8,128)(2,1)S(1)}, bf16[896,2048]{1,0:T(8,128)(2,1)}, u32[]{:S(2)}) copy-start(bf16[896,2048]{1,0:T(8,128)(2,1)} %get-tuple-element.11) | copy-start | bytes 11010052
  135.0 14.7 %copy-start.2 = (bf16[128,2048]{1,0:T(8,128)(2,1)S(1)}, bf16[128,2048]{1,0:T(8,128)(2,1)}, u32[]{:S(2)}) copy-start(bf16[128,2048]{1,0:T(8,128)(2,1)} %param.7) | copy-start | bytes 1572868
  135.5 15.0 %copy-start.1 = (bf16[896,2048]{1,0:T(8,128)(2,1)S(1)}, bf16[896,2048]{1,0:T(8,128)(2,1)}, u32[]{:S(2)}) copy-start(bf16[896,2048]{1,0:T(8,128)(2,1)} %get-tuple-element.11) | copy-start | bytes 11010052
  135.5 11.2 %collective-permute-start = (bf16[1,16,8,896]{3,2,1,0:T(8,128)(2,1)S(1)}, bf16[1,16,8,896]{3,2,1,0:T(8,128)(2,1)S(1)}, u32[]{:S(2)}, u32[]{:S(2)}) collective-permute-start(bf16[1,16,8,896]{3,2,1,0:T(8,128)(2,1)S(1)} %slice_bitcast_fusion), channel_id=1, source_target_pairs={{0,1},{1,2},{2,3},{3,4},{4,5},{5,6},{6,7},{7,8},{8,9},{9,10},{10,1... | collective-permute-start | bytes 688136 | tf_op jit(solution)/shard_map/ppermute | solution.py:24

commit v8 on v6

--- a/solution.py
+++ b/solution.py
@@ -45,8 +45,8 @@
     return total.astype(table_ref.dtype)
 
 
-def torus_step(k, across, sign):
-    i = k // across
+def torus_step(k, across, depth, sign):
+    i = lax.rem(depth - k // across, depth)
     j = lax.rem(k, across)
     dz = sign * ((i + 1) // 2) * (2 * lax.rem(i, 2) - 1)
     dy = sign * ((j + 1) // 2) * (2 * lax.rem(j, 2) - 1)
@@ -65,7 +65,7 @@
     depth = n // across
 
     def peer_of(k, sign):
-        dy, dz = torus_step(k, across, sign)
+        dy, dz = torus_step(k, across, depth, sign)
         y = lax.rem(me, across)
         z = me // across
         return lax.rem(z + dz + depth, depth) * across + lax.rem(y + dy + across, across)

time: 147 us -> 146 us (level)
  the two profiles are of different devices: /device:TPU:24 before, /device:TPU:6 now
where the time goes in v8:
time: 146 us; the launch traced here: 145 us
  Pallas kernels  115 us (79%)
  matrix products  12 us (8%)
  local copies, waits for them, and re-layouts  10.6 us (7%)
  other arithmetic  2.6 us (2%)
  waiting for transfers between devices  2.48 us (2%)
  starting transfers between devices  2.41 us (2%)
    pallas_call x1, Pallas kernels, fetch(): pl.pallas_call(functools.partial(fetch_kernel, length, math.gcd(8, n)), o...  115 us
    dot_general x2, matrix products, project(): jnp.dot(flat_rows, key_weight, preferred_element_type=jnp.float32)  4.19 us
    sub x1, matrix products, attend(): expo = jnp.exp(scores - row_max)  3.46 us
  transfers between devices with their start and end apart: 1, of which 1 were waited for; matrix products, arithmetic and copies ran while one was open for 5% of the time, Pallas kernels for 0%

profile of v8, /device:TPU:6, one launch (start us, length us, event | category | flops | bytes accessed | tf_op | source)
XLA Modules:
  0.0 145.4 jit_solution(11173029339918301069)
XLA Ops:
  0.0 0.8 reshape.174
  0.8 0.2 convert_reduce_fusion
  1.0 0.7 broadcast_multiply_fusion
  1.7 0.7 broadcast_add_fusion.1
  2.8 0.1 broadcast_in_dim.56
  2.9 0.7 pad.4.wanted_ref
  3.6 115.0 %shard_map.73 = (bf16[64,16,896]{2,1,0:T(8,128)(2,1)}, bf16[896,2048]{1,0:T(8,128)(2,1)}, bf16[896,2048]{1,0:T(8,128)(2,1)}) custom-call(s32[64,8,128]{2,1,0:T(8,128)} %pad.4.wanted_ref, bf16[256,896]{1,0:T(8,128)(2,1)} %bitcast.59, bf16[896,256]{1,0:T(8,128)(2,1)} %wk_ref.1, bf16[896,256]{1,0:T(8,128)(2,1)} %wv_ref.1), custom_call_target="tpu_custom_call" | custom-call | tf_op jit(solution)/shard_map/pallas_call | solution.py:190
  118.7 2.1 %gather_fusion = bf16[32,8,896]{2,1,0:T(8,128)(2,1)S(1)} fusion(bf16[128,8,896]{2,1,0:T(8,128)(2,1)} %bitcast.60, s32[1024]{0:T(1024)S(1)} %pad_clamp_fusion), kind=kCustom, calls=%fused_computation | custom fusion | bytes 917632 | tf_op jit(solution)/shard_map/jit(_take)/gather | solution.py:281
  120.9 0.3 multiply_reduce_fusion
  121.2 2.4 %collective-permute-start = (bf16[1,16,8,896]{3,2,1,0:T(8,128)(2,1)S(1)}, bf16[1,16,8,896]{3,2,1,0:T(8,128)(2,1)S(1)}, u32[]{:S(2)}, u32[]{:S(2)}) collective-permute-start(bf16[1,16,8,896]{3,2,1,0:T(8,128)(2,1)S(1)} %slice_bitcast_fusion), channel_id=1, source_target_pairs={{0,1},{1,2},{2,3},{3,4},{4,5},{5,6},{6,7},{7,8},{8,9},{9,10},{10,1... | collective-permute-start | bytes 688136 | tf_op jit(solution)/shard_map/ppermute | solution.py:24
  124.0 3.4 %fusion.18 = bf16[32,8,16,128]{3,1,2,0:T(8,128)(2,1)S(1)} fusion(bf16[896,2048]{1,0:T(8,128)(2,1)} %get-tuple-element.10, bf16[32,8,896]{2,1,0:T(8,128)(2,1)S(1)} %gather_fusion, f32[896]{0:T(1024)S(1)} %copy-done.3, f32[256]{0:T(256)S(1)} %rsqrt.21, pred[256]{0:T(512)(128)(4,1)S(1)} %broadcast_in_dim.59), kind=kOutput, calls=%fused_computation.20 | convolution fusion | flops 941195264 | bytes 5182208 | tf_op jit(solution)/shard_map/dot_general | solution.py:226
  127.4 0.2 copy.27
  127.6 0.3 copy.22
  128.0 0.7 copy-done.2
  128.7 0.4 maximum_bitcast_fusion
  129.1 0.2 copy.25
  129.2 0.6 copy-done
  129.8 1.4 fusion.17
  131.2 0.2 copy.29
  131.5 0.3 copy.20
  131.8 2.5 %collective-permute-done = bf16[1,16,8,896]{3,2,1,0:T(8,128)(2,1)S(1)} collective-permute-done((bf16[1,16,8,896]{3,2,1,0:T(8,128)(2,1)S(1)}, bf16[1,16,8,896]{3,2,1,0:T(8,128)(2,1)S(1)}, u32[]{:S(2)}, u32[]{:S(2)}) %collective-permute-start) | collective-permute-done | bytes 229408 | tf_op jit(solution)/shard_map/ppermute | solution.py:24
  134.2 0.1 fusion.26
  134.4 0.8 fusion.23
  135.2 0.1 copy.26
  135.3 1.0 copy.21
  136.3 0.8 fusion.22
  137.2 0.9 copy.19
  138.1 3.5 %fusion.48 = (f32[3,16,64]{2,1,0:T(8,128)S(1)}, f32[3,16,64,128]{3,2,1,0:T(8,128)}) fusion(bf16[2,128,16,128]{3,1,2,0:T(8,128)(2,1)S(1)} %copy.22, bf16[1,128,16,128]{3,1,2,0:T(8,128)(2,1)} %copy.21, bf16[3,64,16,128]{3,2,1,0:T(8,128)(2,1)S(1)} %bitcast.58), kind=kOutput, calls=%fused_computation.63 | convolution fusion | flops 102629504 | bytes 3944448 | tf_op jit(solution)/shard_map/sub | solution.py:245
  141.6 2.1 %fusion.19 = bf16[3,64,16,128]{3,1,2,0:T(8,128)(2,1)S(1)} fusion(bf16[2,128,16,128]{3,1,2,0:T(8,128)(2,1)S(1)} %copy.20, bf16[1,128,16,128]{3,1,2,0:T(8,128)(2,1)} %copy.19, f32[3,16,64,128]{3,2,1,0:T(8,128)} %get-tuple-element.14, f32[3,16,64]{2,1,0:T(8,128)S(1)} %get-tuple-element.13), kind=kOutput, calls=%fused_computation.21 | convolution fusion | flops 104988672 | bytes 3944448 | tf_op jit(solution)/shard_map/ghqk,gkhd->gqhd/dot_general | solution.py:247
  143.7 0.5 copy.24
  144.2 0.2 copy.40
  144.4 0.9 slice.15
  (30 shorter events, 1.1 us)
Async XLA Ops:
  118.7 5.1 %copy-start.4 = (s32[2,16]{1,0:T(2,128)S(1)}, s32[2,16]{1,0:T(2,128)}, u32[]{:S(2)}) copy-start(s32[2,16]{1,0:T(2,128)} %param.12) | copy-start | bytes 388
  118.7 5.3 %copy-start.3 = (f32[896]{0:T(1024)S(1)}, f32[896]{0:T(1024)}, u32[]{:S(2)}) copy-start(f32[896]{0:T(1024)} %param.9) | copy-start | bytes 10756
  121.2 13.1 %collective-permute-start = (bf16[1,16,8,896]{3,2,1,0:T(8,128)(2,1)S(1)}, bf16[1,16,8,896]{3,2,1,0:T(8,128)(2,1)S(1)}, u32[]{:S(2)}, u32[]{:S(2)}) collective-permute-start(bf16[1,16,8,896]{3,2,1,0:T(8,128)(2,1)S(1)} %slice_bitcast_fusion), channel_id=1, source_target_pairs={{0,1},{1,2},{2,3},{3,4},{4,5},{5,6},{6,7},{7,8},{8,9},{9,10},{10,1... | collective-permute-start | bytes 688136 | tf_op jit(solution)/shard_map/ppermute | solution.py:24
  127.6 1.0 copy-start.2
  127.6 2.2 %copy-start = (bf16[896,2048]{1,0:T(8,128)(2,1)S(1)}, bf16[896,2048]{1,0:T(8,128)(2,1)}, u32[]{:S(2)}) copy-start(bf16[896,2048]{1,0:T(8,128)(2,1)} %get-tuple-element.9) | copy-start | bytes 11010052
  131.2 3.1 %copy-start.1 = (bf16[896,2048]{1,0:T(8,128)(2,1)S(1)}, bf16[896,2048]{1,0:T(8,128)(2,1)}, u32[]{:S(2)}) copy-start(bf16[896,2048]{1,0:T(8,128)(2,1)} %get-tuple-element.10) | copy-start | bytes 11010052

commit v9 on v8

--- a/solution.py
+++ b/solution.py
@@ -126,9 +126,6 @@
             copy.start()
         return carry
 
-    lax.fori_loop(1, nd, share, 0)
-    for copy in own:
-        copy.start()
     asked[me] = wanted_ref[me]
 
     def serve(c, carry):
@@ -159,6 +156,9 @@
         return carry
 
     lax.fori_loop(0, n // group, serve, 0)
+    lax.fori_loop(1, nd, share, 0)
+    for copy in own:
+        copy.start()
 
     def finish(k, carry):
         peer = peer_of(k, 1)

time: 146 us -> 149 us (1.021); the launches traced: 145 us -> 146 us
  no operation moved by 1% of the time
where the time goes in v9:
time: 149 us; the launch traced here: 146 us
  Pallas kernels  115 us (77%)
  matrix products  12 us (8%)
  local copies, waits for them, and re-layouts  10.6 us (7%)
  waiting for transfers between devices  3.35 us (2%)
  other arithmetic  2.6 us (2%)
  starting transfers between devices  2.49 us (2%)
    pallas_call x1, Pallas kernels, fetch(): pl.pallas_call(functools.partial(fetch_kernel, length, math.gcd(8, n)), o...  115 us
    dot_general x2, matrix products, project(): jnp.dot(flat_rows, key_weight, preferred_element_type=jnp.float32)  4.19 us
    sub x1, matrix products, attend(): expo = jnp.exp(scores - row_max)  3.46 us
    ppermute x1, waiting for transfers between devices, from_behind(): return lax.ppermute(block, axis, route)  3.35 us
  transfers between devices with their start and end apart: 1, of which 1 were waited for; matrix products, arithmetic and copies ran while one was open for 5% of the time, Pallas kernels for 0%

profile of v9, /device:TPU:6, one launch (start us, length us, event | category | flops | bytes accessed | tf_op | source)
XLA Modules:
  0.0 146.5 jit_solution(1612168620236565719)
XLA Ops:
  0.0 0.8 reshape.174
  0.8 0.2 convert_reduce_fusion
  1.0 0.7 broadcast_multiply_fusion
  1.7 0.7 broadcast_add_fusion.1
  2.8 0.1 broadcast_in_dim.56
  2.9 0.7 pad.4.wanted_ref
  3.6 115.2 %shard_map.73 = (bf16[64,16,896]{2,1,0:T(8,128)(2,1)}, bf16[896,2048]{1,0:T(8,128)(2,1)}, bf16[896,2048]{1,0:T(8,128)(2,1)}) custom-call(s32[64,8,128]{2,1,0:T(8,128)} %pad.4.wanted_ref, bf16[256,896]{1,0:T(8,128)(2,1)} %bitcast.59, bf16[896,256]{1,0:T(8,128)(2,1)} %wk_ref.1, bf16[896,256]{1,0:T(8,128)(2,1)} %wv_ref.1), custom_call_target="tpu_custom_call" | custom-call | tf_op jit(solution)/shard_map/pallas_call | solution.py:190
  118.9 2.1 %gather_fusion = bf16[32,8,896]{2,1,0:T(8,128)(2,1)S(1)} fusion(bf16[128,8,896]{2,1,0:T(8,128)(2,1)} %bitcast.60, s32[1024]{0:T(1024)S(1)} %pad_clamp_fusion), kind=kCustom, calls=%fused_computation | custom fusion | bytes 917632 | tf_op jit(solution)/shard_map/jit(_take)/gather | solution.py:281
  121.0 0.3 multiply_reduce_fusion
  121.3 2.5 %collective-permute-start = (bf16[1,16,8,896]{3,2,1,0:T(8,128)(2,1)S(1)}, bf16[1,16,8,896]{3,2,1,0:T(8,128)(2,1)S(1)}, u32[]{:S(2)}, u32[]{:S(2)}) collective-permute-start(bf16[1,16,8,896]{3,2,1,0:T(8,128)(2,1)S(1)} %slice_bitcast_fusion), channel_id=1, source_target_pairs={{0,1},{1,2},{2,3},{3,4},{4,5},{5,6},{6,7},{7,8},{8,9},{9,10},{10,1... | collective-permute-start | bytes 688136 | tf_op jit(solution)/shard_map/ppermute | solution.py:24
  124.2 3.4 %fusion.18 = bf16[32,8,16,128]{3,1,2,0:T(8,128)(2,1)S(1)} fusion(bf16[896,2048]{1,0:T(8,128)(2,1)} %get-tuple-element.10, bf16[32,8,896]{2,1,0:T(8,128)(2,1)S(1)} %gather_fusion, f32[896]{0:T(1024)S(1)} %copy-done.3, f32[256]{0:T(256)S(1)} %rsqrt.21, pred[256]{0:T(512)(128)(4,1)S(1)} %broadcast_in_dim.59), kind=kOutput, calls=%fused_computation.20 | convolution fusion | flops 941195264 | bytes 5182208 | tf_op jit(solution)/shard_map/dot_general | solution.py:226
  127.6 0.2 copy.27
  127.9 0.3 copy.22
  128.3 0.7 copy-done.2
  128.9 0.4 maximum_bitcast_fusion
  129.3 0.2 copy.25
  129.5 0.6 copy-done
  130.1 1.4 fusion.17
  131.5 0.2 copy.29
  131.7 0.3 copy.20
  132.0 3.3 %collective-permute-done = bf16[1,16,8,896]{3,2,1,0:T(8,128)(2,1)S(1)} collective-permute-done((bf16[1,16,8,896]{3,2,1,0:T(8,128)(2,1)S(1)}, bf16[1,16,8,896]{3,2,1,0:T(8,128)(2,1)S(1)}, u32[]{:S(2)}, u32[]{:S(2)}) %collective-permute-start) | collective-permute-done | bytes 229408 | tf_op jit(solution)/shard_map/ppermute | solution.py:24
  135.4 0.1 fusion.26
  135.5 0.8 fusion.23
  136.3 0.1 copy.26
  136.4 1.0 copy.21
  137.4 0.8 fusion.22
  138.3 0.9 copy.19
  139.2 3.5 %fusion.48 = (f32[3,16,64]{2,1,0:T(8,128)S(1)}, f32[3,16,64,128]{3,2,1,0:T(8,128)}) fusion(bf16[2,128,16,128]{3,1,2,0:T(8,128)(2,1)S(1)} %copy.22, bf16[1,128,16,128]{3,1,2,0:T(8,128)(2,1)} %copy.21, bf16[3,64,16,128]{3,2,1,0:T(8,128)(2,1)S(1)} %bitcast.58), kind=kOutput, calls=%fused_computation.63 | convolution fusion | flops 102629504 | bytes 3944448 | tf_op jit(solution)/shard_map/sub | solution.py:245
  142.7 2.1 %fusion.19 = bf16[3,64,16,128]{3,1,2,0:T(8,128)(2,1)S(1)} fusion(bf16[2,128,16,128]{3,1,2,0:T(8,128)(2,1)S(1)} %copy.20, bf16[1,128,16,128]{3,1,2,0:T(8,128)(2,1)} %copy.19, f32[3,16,64,128]{3,2,1,0:T(8,128)} %get-tuple-element.14, f32[3,16,64]{2,1,0:T(8,128)S(1)} %get-tuple-element.13), kind=kOutput, calls=%fused_computation.21 | convolution fusion | flops 104988672 | bytes 3944448 | tf_op jit(solution)/shard_map/ghqk,gkhd->gqhd/dot_general | solution.py:247
  144.8 0.5 copy.24
  145.3 0.2 copy.40
  145.5 0.9 slice.15
  (30 shorter events, 1.1 us)
Async XLA Ops:
  118.9 5.2 %copy-start.4 = (s32[2,16]{1,0:T(2,128)S(1)}, s32[2,16]{1,0:T(2,128)}, u32[]{:S(2)}) copy-start(s32[2,16]{1,0:T(2,128)} %param.12) | copy-start | bytes 388
  118.9 5.3 %copy-start.3 = (f32[896]{0:T(1024)S(1)}, f32[896]{0:T(1024)}, u32[]{:S(2)}) copy-start(f32[896]{0:T(1024)} %param.9) | copy-start | bytes 10756
  121.3 14.0 %collective-permute-start = (bf16[1,16,8,896]{3,2,1,0:T(8,128)(2,1)S(1)}, bf16[1,16,8,896]{3,2,1,0:T(8,128)(2,1)S(1)}, u32[]{:S(2)}, u32[]{:S(2)}) collective-permute-start(bf16[1,16,8,896]{3,2,1,0:T(8,128)(2,1)S(1)} %slice_bitcast_fusion), channel_id=1, source_target_pairs={{0,1},{1,2},{2,3},{3,4},{4,5},{5,6},{6,7},{7,8},{8,9},{9,10},{10,1... | collective-permute-start | bytes 688136 | tf_op jit(solution)/shard_map/ppermute | solution.py:24
  127.9 1.0 copy-start.2
  127.9 2.2 %copy-start = (bf16[896,2048]{1,0:T(8,128)(2,1)S(1)}, bf16[896,2048]{1,0:T(8,128)(2,1)}, u32[]{:S(2)}) copy-start(bf16[896,2048]{1,0:T(8,128)(2,1)} %get-tuple-element.9) | copy-start | bytes 11010052
  131.5 4.0 %copy-start.1 = (bf16[896,2048]{1,0:T(8,128)(2,1)S(1)}, bf16[896,2048]{1,0:T(8,128)(2,1)}, u32[]{:S(2)}) copy-start(bf16[896,2048]{1,0:T(8,128)(2,1)} %get-tuple-element.10) | copy-start | bytes 11010052

commit v10 on v8

--- a/solution.py
+++ b/solution.py
@@ -115,12 +115,6 @@
     lax.fori_loop(1, nd, greet_dp, 0)
     pl.semaphore_wait(barrier, n - 1 + nd - 1)
 
-    def ask(k, carry):
-        request(peer_of(k, 1), me).start()
-        return carry
-
-    lax.fori_loop(1, n, ask, 0)
-
     def share(k, carry):
         for copy in weights(lax.rem(dp + k, nd), dp):
             copy.start()
@@ -129,6 +123,13 @@
     lax.fori_loop(1, nd, share, 0)
     for copy in own:
         copy.start()
+
+    def ask(k, carry):
+        request(peer_of(k, 1), me).start()
+        return carry
+
+    lax.fori_loop(1, n, ask, 0)
+
     asked[me] = wanted_ref[me]
 
     def serve(c, carry):

time: 146 us -> 146 us (level)
  no operation moved by 1% of the time
where the time goes in v10:
time: 146 us; the launch traced here: 145 us
  Pallas kernels  115 us (79%)
  matrix products  11.9 us (8%)
  local copies, waits for them, and re-layouts  10.6 us (7%)
  other arithmetic  2.6 us (2%)
  waiting for transfers between devices  2.57 us (2%)
  starting transfers between devices  2.33 us (2%)
    pallas_call x1, Pallas kernels, fetch(): pl.pallas_call(functools.partial(fetch_kernel, length, math.gcd(8, n)), o...  115 us
    dot_general x2, matrix products, project(): jnp.dot(flat_rows, key_weight, preferred_element_type=jnp.float32)  4.19 us
    sub x1, matrix products, attend(): expo = jnp.exp(scores - row_max)  3.46 us
  transfers between devices with their start and end apart: 1, of which 1 were waited for; matrix products, arithmetic and copies ran while one was open for 5% of the time, Pallas kernels for 0%

profile of v10, /device:TPU:6, one launch (start us, length us, event | category | flops | bytes accessed | tf_op | source)
XLA Modules:
  0.0 145.5 jit_solution(11966142192620267829)
XLA Ops:
  0.0 0.8 reshape.174
  0.8 0.2 convert_reduce_fusion
  1.0 0.7 broadcast_multiply_fusion
  1.7 0.7 broadcast_add_fusion.1
  2.8 0.1 broadcast_in_dim.56
  2.9 0.7 pad.4.wanted_ref
  3.6 115.2 %shard_map.73 = (bf16[64,16,896]{2,1,0:T(8,128)(2,1)}, bf16[896,2048]{1,0:T(8,128)(2,1)}, bf16[896,2048]{1,0:T(8,128)(2,1)}) custom-call(s32[64,8,128]{2,1,0:T(8,128)} %pad.4.wanted_ref, bf16[256,896]{1,0:T(8,128)(2,1)} %bitcast.59, bf16[896,256]{1,0:T(8,128)(2,1)} %wk_ref.1, bf16[896,256]{1,0:T(8,128)(2,1)} %wv_ref.1), custom_call_target="tpu_custom_call" | custom-call | tf_op jit(solution)/shard_map/pallas_call | solution.py:191
  118.8 2.1 %gather_fusion = bf16[32,8,896]{2,1,0:T(8,128)(2,1)S(1)} fusion(bf16[128,8,896]{2,1,0:T(8,128)(2,1)} %bitcast.60, s32[1024]{0:T(1024)S(1)} %pad_clamp_fusion), kind=kCustom, calls=%fused_computation | custom fusion | bytes 917632 | tf_op jit(solution)/shard_map/jit(_take)/gather | solution.py:282
  121.0 0.3 multiply_reduce_fusion
  121.3 2.3 %collective-permute-start = (bf16[1,16,8,896]{3,2,1,0:T(8,128)(2,1)S(1)}, bf16[1,16,8,896]{3,2,1,0:T(8,128)(2,1)S(1)}, u32[]{:S(2)}, u32[]{:S(2)}) collective-permute-start(bf16[1,16,8,896]{3,2,1,0:T(8,128)(2,1)S(1)} %slice_bitcast_fusion), channel_id=1, source_target_pairs={{0,1},{1,2},{2,3},{3,4},{4,5},{5,6},{6,7},{7,8},{8,9},{9,10},{10,1... | collective-permute-start | bytes 688136 | tf_op jit(solution)/shard_map/ppermute | solution.py:24
  124.0 3.4 %fusion.18 = bf16[32,8,16,128]{3,1,2,0:T(8,128)(2,1)S(1)} fusion(bf16[896,2048]{1,0:T(8,128)(2,1)} %get-tuple-element.10, bf16[32,8,896]{2,1,0:T(8,128)(2,1)S(1)} %gather_fusion, f32[896]{0:T(1024)S(1)} %copy-done.3, f32[256]{0:T(256)S(1)} %rsqrt.21, pred[256]{0:T(512)(128)(4,1)S(1)} %broadcast_in_dim.59), kind=kOutput, calls=%fused_computation.20 | convolution fusion | flops 941195264 | bytes 5182208 | tf_op jit(solution)/shard_map/dot_general | solution.py:227
  127.4 0.2 copy.27
  127.7 0.3 copy.22
  128.0 0.7 copy-done.2
  128.7 0.4 maximum_bitcast_fusion
  129.1 0.2 copy.25
  129.3 0.6 copy-done
  129.9 1.4 fusion.17
  131.3 0.2 copy.29
  131.5 0.3 copy.20
  131.8 2.6 %collective-permute-done = bf16[1,16,8,896]{3,2,1,0:T(8,128)(2,1)S(1)} collective-permute-done((bf16[1,16,8,896]{3,2,1,0:T(8,128)(2,1)S(1)}, bf16[1,16,8,896]{3,2,1,0:T(8,128)(2,1)S(1)}, u32[]{:S(2)}, u32[]{:S(2)}) %collective-permute-start) | collective-permute-done | bytes 229408 | tf_op jit(solution)/shard_map/ppermute | solution.py:24
  134.4 0.1 fusion.26
  134.5 0.8 fusion.23
  135.3 0.1 copy.26
  135.4 1.0 copy.21
  136.4 0.8 fusion.22
  137.3 0.9 copy.19
  138.2 3.5 %fusion.48 = (f32[3,16,64]{2,1,0:T(8,128)S(1)}, f32[3,16,64,128]{3,2,1,0:T(8,128)}) fusion(bf16[2,128,16,128]{3,1,2,0:T(8,128)(2,1)S(1)} %copy.22, bf16[1,128,16,128]{3,1,2,0:T(8,128)(2,1)} %copy.21, bf16[3,64,16,128]{3,2,1,0:T(8,128)(2,1)S(1)} %bitcast.58), kind=kOutput, calls=%fused_computation.63 | convolution fusion | flops 102629504 | bytes 3944448 | tf_op jit(solution)/shard_map/sub | solution.py:246
  141.7 2.1 %fusion.19 = bf16[3,64,16,128]{3,1,2,0:T(8,128)(2,1)S(1)} fusion(bf16[2,128,16,128]{3,1,2,0:T(8,128)(2,1)S(1)} %copy.20, bf16[1,128,16,128]{3,1,2,0:T(8,128)(2,1)} %copy.19, f32[3,16,64,128]{3,2,1,0:T(8,128)} %get-tuple-element.14, f32[3,16,64]{2,1,0:T(8,128)S(1)} %get-tuple-element.13), kind=kOutput, calls=%fused_computation.21 | convolution fusion | flops 104988672 | bytes 3944448 | tf_op jit(solution)/shard_map/ghqk,gkhd->gqhd/dot_general | solution.py:248
  143.8 0.5 copy.24
  144.3 0.2 copy.40
  144.5 0.9 slice.15
  (30 shorter events, 1.1 us)
Async XLA Ops:
  118.8 5.0 %copy-start.4 = (s32[2,16]{1,0:T(2,128)S(1)}, s32[2,16]{1,0:T(2,128)}, u32[]{:S(2)}) copy-start(s32[2,16]{1,0:T(2,128)} %param.12) | copy-start | bytes 388
  118.8 5.2 %copy-start.3 = (f32[896]{0:T(1024)S(1)}, f32[896]{0:T(1024)}, u32[]{:S(2)}) copy-start(f32[896]{0:T(1024)} %param.9) | copy-start | bytes 10756
  121.3 13.1 %collective-permute-start = (bf16[1,16,8,896]{3,2,1,0:T(8,128)(2,1)S(1)}, bf16[1,16,8,896]{3,2,1,0:T(8,128)(2,1)S(1)}, u32[]{:S(2)}, u32[]{:S(2)}) collective-permute-start(bf16[1,16,8,896]{3,2,1,0:T(8,128)(2,1)S(1)} %slice_bitcast_fusion), channel_id=1, source_target_pairs={{0,1},{1,2},{2,3},{3,4},{4,5},{5,6},{6,7},{7,8},{8,9},{9,10},{10,1... | collective-permute-start | bytes 688136 | tf_op jit(solution)/shard_map/ppermute | solution.py:24
  127.6 1.0 copy-start.2
  127.7 2.2 %copy-start = (bf16[896,2048]{1,0:T(8,128)(2,1)S(1)}, bf16[896,2048]{1,0:T(8,128)(2,1)}, u32[]{:S(2)}) copy-start(bf16[896,2048]{1,0:T(8,128)(2,1)} %get-tuple-element.9) | copy-start | bytes 11010052
  131.3 3.2 %copy-start.1 = (bf16[896,2048]{1,0:T(8,128)(2,1)S(1)}, bf16[896,2048]{1,0:T(8,128)(2,1)}, u32[]{:S(2)}) copy-start(bf16[896,2048]{1,0:T(8,128)(2,1)} %get-tuple-element.10) | copy-start | bytes 11010052

commit v11 on v10

--- a/solution.py
+++ b/solution.py
@@ -77,10 +77,15 @@
         )
 
     def reply(step, peer, slot):
-        return pltpu.make_async_remote_copy(
-            outgoing.at[step], out_ref.at[slot], rep_send.at[step], rep_recv.at[slot],
-            device_id=(dp, peer), device_id_type=MESH,
-        )
+        return [
+            pltpu.make_async_remote_copy(
+                outgoing.at[step, pl.ds(half * length, length)],
+                out_ref.at[slot, pl.ds(half * length, length)],
+                rep_send.at[half, step], rep_recv.at[half, slot],
+                device_id=(dp, peer), device_id_type=MESH,
+            )
+            for half in range(2)
+        ]
 
     cols = wk_ref.shape[1]
 
@@ -155,7 +160,8 @@
 
             @pl.when(k > 0)
             def _():
-                reply(k, source, me).start()
+                for copy in reply(k, source, me):
+                    copy.start()
 
         return carry
 
@@ -164,8 +170,10 @@
     def finish(k, carry):
         peer = peer_of(k, 1)
         request(peer, me).wait_send()
-        reply(k, peer_of(k, -1), me).wait_send()
-        reply(k, peer, peer).wait_recv()
+        for copy in reply(k, peer_of(k, -1), me):
+            copy.wait_send()
+        for copy in reply(k, peer, peer):
+            copy.wait_recv()
         return carry
 
     lax.fori_loop(1, n, finish, 0)
@@ -202,8 +210,8 @@
             pltpu.VMEM((n, 2 * length, width), table.dtype),
             pltpu.SemaphoreType.DMA((n,)),
             pltpu.SemaphoreType.DMA((n,)),
-            pltpu.SemaphoreType.DMA((n,)),
-            pltpu.SemaphoreType.DMA((n,)),
+            pltpu.SemaphoreType.DMA((2, n)),
+            pltpu.SemaphoreType.DMA((2, n)),
             pltpu.SemaphoreType.DMA((nd,)),
             pltpu.SemaphoreType.DMA((nd,)),
             pltpu.SemaphoreType.DMA((nd,)),

time: 146 us -> 147 us (level)
  no operation moved by 1% of the time
where the time goes in v11:
time: 147 us
  Pallas kernels  116 us (79%)
  matrix products  12 us (8%)
  local copies, waits for them, and re-layouts  10.6 us (7%)
  other arithmetic  2.6 us (2%)
  waiting for transfers between devices  2.56 us (2%)
  starting transfers between devices  2.33 us (2%)
    pallas_call x1, Pallas kernels, fetch(): pl.pallas_call(functools.partial(fetch_kernel, length, math.gcd(8, n)), o...  116 us
    dot_general x2, matrix products, project(): jnp.dot(flat_rows, key_weight, preferred_element_type=jnp.float32)  4.19 us
    sub x1, matrix products, attend(): expo = jnp.exp(scores - row_max)  3.46 us
  transfers between devices with their start and end apart: 1, of which 1 were waited for; matrix products, arithmetic and copies ran while one was open for 5% of the time, Pallas kernels for 0%

profile of v11, /device:TPU:6, one launch (start us, length us, event | category | flops | bytes accessed | tf_op | source)
XLA Modules:
  0.0 146.6 jit_solution(12220151355062412908)
XLA Ops:
  0.0 0.8 reshape.174
  0.8 0.2 convert_reduce_fusion
  1.0 0.7 broadcast_multiply_fusion
  1.7 0.7 broadcast_add_fusion.1
  2.8 0.1 broadcast_in_dim.56
  2.9 0.7 pad.4.wanted_ref
  3.6 116.3 %shard_map.73 = (bf16[64,16,896]{2,1,0:T(8,128)(2,1)}, bf16[896,2048]{1,0:T(8,128)(2,1)}, bf16[896,2048]{1,0:T(8,128)(2,1)}) custom-call(s32[64,8,128]{2,1,0:T(8,128)} %pad.4.wanted_ref, bf16[256,896]{1,0:T(8,128)(2,1)} %bitcast.59, bf16[896,256]{1,0:T(8,128)(2,1)} %wk_ref.1, bf16[896,256]{1,0:T(8,128)(2,1)} %wv_ref.1), custom_call_target="tpu_custom_call" | custom-call | tf_op jit(solution)/shard_map/pallas_call | solution.py:199
  120.0 2.1 %gather_fusion = bf16[32,8,896]{2,1,0:T(8,128)(2,1)S(1)} fusion(bf16[128,8,896]{2,1,0:T(8,128)(2,1)} %bitcast.60, s32[1024]{0:T(1024)S(1)} %pad_clamp_fusion), kind=kCustom, calls=%fused_computation | custom fusion | bytes 917632 | tf_op jit(solution)/shard_map/jit(_take)/gather | solution.py:290
  122.1 0.3 multiply_reduce_fusion
  122.4 2.3 %collective-permute-start = (bf16[1,16,8,896]{3,2,1,0:T(8,128)(2,1)S(1)}, bf16[1,16,8,896]{3,2,1,0:T(8,128)(2,1)S(1)}, u32[]{:S(2)}, u32[]{:S(2)}) collective-permute-start(bf16[1,16,8,896]{3,2,1,0:T(8,128)(2,1)S(1)} %slice_bitcast_fusion), channel_id=1, source_target_pairs={{0,1},{1,2},{2,3},{3,4},{4,5},{5,6},{6,7},{7,8},{8,9},{9,10},{10,1... | collective-permute-start | bytes 688136 | tf_op jit(solution)/shard_map/ppermute | solution.py:24
  125.2 3.4 %fusion.18 = bf16[32,8,16,128]{3,1,2,0:T(8,128)(2,1)S(1)} fusion(bf16[896,2048]{1,0:T(8,128)(2,1)} %get-tuple-element.10, bf16[32,8,896]{2,1,0:T(8,128)(2,1)S(1)} %gather_fusion, f32[896]{0:T(1024)S(1)} %copy-done.3, f32[256]{0:T(256)S(1)} %rsqrt.21, pred[256]{0:T(512)(128)(4,1)S(1)} %broadcast_in_dim.59), kind=kOutput, calls=%fused_computation.20 | convolution fusion | flops 941195264 | bytes 5182208 | tf_op jit(solution)/shard_map/dot_general | solution.py:235
  128.6 0.2 copy.27
  128.8 0.3 copy.22
  129.2 0.7 copy-done.2
  129.9 0.4 maximum_bitcast_fusion
  130.3 0.2 copy.25
  130.4 0.6 copy-done
  131.0 1.4 fusion.17
  132.4 0.2 copy.29
  132.7 0.3 copy.20
  132.9 2.6 %collective-permute-done = bf16[1,16,8,896]{3,2,1,0:T(8,128)(2,1)S(1)} collective-permute-done((bf16[1,16,8,896]{3,2,1,0:T(8,128)(2,1)S(1)}, bf16[1,16,8,896]{3,2,1,0:T(8,128)(2,1)S(1)}, u32[]{:S(2)}, u32[]{:S(2)}) %collective-permute-start) | collective-permute-done | bytes 229408 | tf_op jit(solution)/shard_map/ppermute | solution.py:24
  135.5 0.1 fusion.26
  135.7 0.8 fusion.23
  136.5 0.1 copy.26
  136.6 1.0 copy.21
  137.5 0.8 fusion.22
  138.4 0.9 copy.19
  139.4 3.5 %fusion.48 = (f32[3,16,64]{2,1,0:T(8,128)S(1)}, f32[3,16,64,128]{3,2,1,0:T(8,128)}) fusion(bf16[2,128,16,128]{3,1,2,0:T(8,128)(2,1)S(1)} %copy.22, bf16[1,128,16,128]{3,1,2,0:T(8,128)(2,1)} %copy.21, bf16[3,64,16,128]{3,2,1,0:T(8,128)(2,1)S(1)} %bitcast.58), kind=kOutput, calls=%fused_computation.63 | convolution fusion | flops 102629504 | bytes 3944448 | tf_op jit(solution)/shard_map/sub | solution.py:254
  142.8 2.1 %fusion.19 = bf16[3,64,16,128]{3,1,2,0:T(8,128)(2,1)S(1)} fusion(bf16[2,128,16,128]{3,1,2,0:T(8,128)(2,1)S(1)} %copy.20, bf16[1,128,16,128]{3,1,2,0:T(8,128)(2,1)} %copy.19, f32[3,16,64,128]{3,2,1,0:T(8,128)} %get-tuple-element.14, f32[3,16,64]{2,1,0:T(8,128)S(1)} %get-tuple-element.13), kind=kOutput, calls=%fused_computation.21 | convolution fusion | flops 104988672 | bytes 3944448 | tf_op jit(solution)/shard_map/ghqk,gkhd->gqhd/dot_general | solution.py:256
  145.0 0.5 copy.24
  145.5 0.2 copy.40
  145.7 0.9 slice.15
  (30 shorter events, 1.1 us)
Async XLA Ops:
  120.0 5.0 %copy-start.4 = (s32[2,16]{1,0:T(2,128)S(1)}, s32[2,16]{1,0:T(2,128)}, u32[]{:S(2)}) copy-start(s32[2,16]{1,0:T(2,128)} %param.12) | copy-start | bytes 388
  120.0 5.2 %copy-start.3 = (f32[896]{0:T(1024)S(1)}, f32[896]{0:T(1024)}, u32[]{:S(2)}) copy-start(f32[896]{0:T(1024)} %param.9) | copy-start | bytes 10756
  122.4 13.1 %collective-permute-start = (bf16[1,16,8,896]{3,2,1,0:T(8,128)(2,1)S(1)}, bf16[1,16,8,896]{3,2,1,0:T(8,128)(2,1)S(1)}, u32[]{:S(2)}, u32[]{:S(2)}) collective-permute-start(bf16[1,16,8,896]{3,2,1,0:T(8,128)(2,1)S(1)} %slice_bitcast_fusion), channel_id=1, source_target_pairs={{0,1},{1,2},{2,3},{3,4},{4,5},{5,6},{6,7},{7,8},{8,9},{9,10},{10,1... | collective-permute-start | bytes 688136 | tf_op jit(solution)/shard_map/ppermute | solution.py:24
  128.8 1.0 copy-start.2
  128.8 2.2 %copy-start = (bf16[896,2048]{1,0:T(8,128)(2,1)S(1)}, bf16[896,2048]{1,0:T(8,128)(2,1)}, u32[]{:S(2)}) copy-start(bf16[896,2048]{1,0:T(8,128)(2,1)} %get-tuple-element.9) | copy-start | bytes 11010052
  132.4 3.2 %copy-start.1 = (bf16[896,2048]{1,0:T(8,128)(2,1)S(1)}, bf16[896,2048]{1,0:T(8,128)(2,1)}, u32[]{:S(2)}) copy-start(bf16[896,2048]{1,0:T(8,128)(2,1)} %get-tuple-element.10) | copy-start | bytes 11010052

commit v12 on v10

--- a/solution.py
+++ b/solution.py
@@ -55,7 +55,8 @@
 
 def fetch_kernel(
     length, group, wanted_ref, table_ref, wk_ref, wv_ref, out_ref, wk_out, wv_out,
-    asked, outgoing, req_send, req_recv, rep_send, rep_recv, wk_send, wk_recv, wv_send, wv_recv, own_sem,
+    asked, outgoing, req_send, req_recv, rep_send, rep_recv, wk_send, wk_recv, wv_send, wv_recv, wk_fwd, wv_fwd,
+    own_sem,
 ):
     n = wanted_ref.shape[0]
     nd = wk_out.shape[1] // wk_ref.shape[1]
@@ -83,17 +84,25 @@
         )
 
     cols = wk_ref.shape[1]
-
-    def weight(src, dst, send, recv, peer, slot):
-        return pltpu.make_async_remote_copy(
-            src, dst.at[:, pl.ds(slot * cols, cols)], send.at[peer], recv.at[slot],
-            device_id=(peer, me), device_id_type=MESH,
-        )
-
-    def weights(peer, slot):
-        return (
-            weight(wk_ref, wk_out, wk_send, wk_recv, peer, slot),
-            weight(wv_ref, wv_out, wv_send, wv_recv, peer, slot),
+    partner = dp + 1 - 2 * lax.rem(dp, 2)
+    pairs = nd // 2
+
+    def weights(src_k, src_v, peer, slot, sent_k, sent_v, sent_slot):
+        return [
+            pltpu.make_async_remote_copy(
+                src, dst.at[:, pl.ds(slot * cols, cols)], sent.at[sent_slot], recv.at[slot],
+                device_id=(peer, me), device_id_type=MESH,
+            )
+            for src, dst, sent, recv in ((src_k, wk_out, sent_k, wk_recv), (src_v, wv_out, sent_v, wv_recv))
+        ]
+
+    def own_shard(peer):
+        return weights(wk_ref, wv_ref, peer, dp, wk_send, wv_send, peer)
+
+    def relayed(slot, peer):
+        return weights(
+            wk_out.at[:, pl.ds(slot * cols, cols)], wv_out.at[:, pl.ds(slot * cols, cols)],
+            peer, slot, wk_fwd, wv_fwd, slot,
         )
 
     own = (
@@ -115,12 +124,14 @@
     lax.fori_loop(1, nd, greet_dp, 0)
     pl.semaphore_wait(barrier, n - 1 + nd - 1)
 
-    def share(k, carry):
-        for copy in weights(lax.rem(dp + k, nd), dp):
+    def share(m, carry):
+        for copy in own_shard(lax.rem(dp + 2 * m, nd)):
             copy.start()
         return carry
 
-    lax.fori_loop(1, nd, share, 0)
+    for copy in own_shard(partner):
+        copy.start()
+    lax.fori_loop(1, pairs, share, 0)
     for copy in own:
         copy.start()
 
@@ -161,6 +172,16 @@
 
     lax.fori_loop(0, n // group, serve, 0)
 
+    def relay(m, carry):
+        slot = lax.rem(dp + 2 * m, nd)
+        for copy in relayed(slot, partner):
+            copy.wait_recv()
+        for copy in relayed(slot, partner):
+            copy.start()
+        return carry
+
+    lax.fori_loop(1, pairs, relay, 0)
+
     def finish(k, carry):
         peer = peer_of(k, 1)
         request(peer, me).wait_send()
@@ -170,15 +191,21 @@
 
     lax.fori_loop(1, n, finish, 0)
 
-    def gathered(k, carry):
-        peer = lax.rem(dp + k, nd)
-        for copy in weights(peer, dp):
+    def gathered(m, carry):
+        peer = lax.rem(dp + 2 * m, nd)
+        for copy in own_shard(peer):
             copy.wait_send()
-        for copy in weights(peer, peer):
+        for copy in relayed(peer, partner):
+            copy.wait_send()
+        for copy in relayed(lax.rem(partner + 2 * m, nd), partner):
             copy.wait_recv()
         return carry
 
-    lax.fori_loop(1, nd, gathered, 0)
+    lax.fori_loop(1, pairs, gathered, 0)
+    for copy in own_shard(partner):
+        copy.wait_send()
+    for copy in relayed(partner, partner):
+        copy.wait_recv()
     for copy in own:
         copy.wait()
 
@@ -208,6 +235,8 @@
             pltpu.SemaphoreType.DMA((nd,)),
             pltpu.SemaphoreType.DMA((nd,)),
             pltpu.SemaphoreType.DMA((nd,)),
+            pltpu.SemaphoreType.DMA((nd,)),
+            pltpu.SemaphoreType.DMA((nd,)),
             pltpu.SemaphoreType.DMA((2,)),
         ],
         compiler_params=pltpu.CompilerParams(collective_id=0, has_side_effects=True),

time: 146 us -> 146 us (level)
  no operation moved by 1% of the time
where the time goes in v12:
time: 146 us; the launch traced here: 145 us
  Pallas kernels  115 us (79%)
  matrix products  11.9 us (8%)
  local copies, waits for them, and re-layouts  10.6 us (7%)
  other arithmetic  2.6 us (2%)
  waiting for transfers between devices  2.52 us (2%)
  starting transfers between devices  2.37 us (2%)
    pallas_call x1, Pallas kernels, fetch(): pl.pallas_call(functools.partial(fetch_kernel, length, math.gcd(8, n)), o...  115 us
    dot_general x2, matrix products, project(): jnp.dot(flat_rows, key_weight, preferred_element_type=jnp.float32)  4.19 us
    sub x1, matrix products, attend(): expo = jnp.exp(scores - row_max)  3.46 us
  transfers between devices with their start and end apart: 1, of which 1 were waited for; matrix products, arithmetic and copies ran while one was open for 5% of the time, Pallas kernels for 0%

profile of v12, /device:TPU:6, one launch (start us, length us, event | category | flops | bytes accessed | tf_op | source)
XLA Modules:
  0.0 145.5 jit_solution(15807492711351115740)
XLA Ops:
  0.0 0.8 reshape.174
  0.8 0.2 convert_reduce_fusion
  1.0 0.7 broadcast_multiply_fusion
  1.7 0.7 broadcast_add_fusion.1
  2.8 0.1 broadcast_in_dim.56
  2.9 0.7 pad.4.wanted_ref
  3.6 115.2 %shard_map.73 = (bf16[64,16,896]{2,1,0:T(8,128)(2,1)}, bf16[896,2048]{1,0:T(8,128)(2,1)}, bf16[896,2048]{1,0:T(8,128)(2,1)}) custom-call(s32[64,8,128]{2,1,0:T(8,128)} %pad.4.wanted_ref, bf16[256,896]{1,0:T(8,128)(2,1)} %bitcast.59, bf16[896,256]{1,0:T(8,128)(2,1)} %wk_ref.1, bf16[896,256]{1,0:T(8,128)(2,1)} %wv_ref.1), custom_call_target="tpu_custom_call" | custom-call | tf_op jit(solution)/shard_map/pallas_call | solution.py:218
  118.8 2.1 %gather_fusion = bf16[32,8,896]{2,1,0:T(8,128)(2,1)S(1)} fusion(bf16[128,8,896]{2,1,0:T(8,128)(2,1)} %bitcast.60, s32[1024]{0:T(1024)S(1)} %pad_clamp_fusion), kind=kCustom, calls=%fused_computation | custom fusion | bytes 917632 | tf_op jit(solution)/shard_map/jit(_take)/gather | solution.py:311
  121.0 0.3 multiply_reduce_fusion
  121.3 2.4 %collective-permute-start = (bf16[1,16,8,896]{3,2,1,0:T(8,128)(2,1)S(1)}, bf16[1,16,8,896]{3,2,1,0:T(8,128)(2,1)S(1)}, u32[]{:S(2)}, u32[]{:S(2)}) collective-permute-start(bf16[1,16,8,896]{3,2,1,0:T(8,128)(2,1)S(1)} %slice_bitcast_fusion), channel_id=1, source_target_pairs={{0,1},{1,2},{2,3},{3,4},{4,5},{5,6},{6,7},{7,8},{8,9},{9,10},{10,1... | collective-permute-start | bytes 688136 | tf_op jit(solution)/shard_map/ppermute | solution.py:24
  124.1 3.4 %fusion.18 = bf16[32,8,16,128]{3,1,2,0:T(8,128)(2,1)S(1)} fusion(bf16[896,2048]{1,0:T(8,128)(2,1)} %get-tuple-element.10, bf16[32,8,896]{2,1,0:T(8,128)(2,1)S(1)} %gather_fusion, f32[896]{0:T(1024)S(1)} %copy-done.3, f32[256]{0:T(256)S(1)} %rsqrt.21, pred[256]{0:T(512)(128)(4,1)S(1)} %broadcast_in_dim.59), kind=kOutput, calls=%fused_computation.20 | convolution fusion | flops 941195264 | bytes 5182208 | tf_op jit(solution)/shard_map/dot_general | solution.py:256
  127.5 0.2 copy.27
  127.7 0.3 copy.22
  128.1 0.7 copy-done.2
  128.7 0.4 maximum_bitcast_fusion
  129.2 0.2 copy.25
  129.3 0.6 copy-done
  129.9 1.4 fusion.17
  131.3 0.2 copy.29
  131.6 0.3 copy.20
  131.8 2.5 %collective-permute-done = bf16[1,16,8,896]{3,2,1,0:T(8,128)(2,1)S(1)} collective-permute-done((bf16[1,16,8,896]{3,2,1,0:T(8,128)(2,1)S(1)}, bf16[1,16,8,896]{3,2,1,0:T(8,128)(2,1)S(1)}, u32[]{:S(2)}, u32[]{:S(2)}) %collective-permute-start) | collective-permute-done | bytes 229408 | tf_op jit(solution)/shard_map/ppermute | solution.py:24
  134.4 0.1 fusion.26
  134.5 0.8 fusion.23
  135.4 1.0 copy.21
  136.4 0.8 fusion.22
  137.2 0.1 copy.28
  137.3 0.9 copy.19
  138.2 3.5 %fusion.48 = (f32[3,16,64]{2,1,0:T(8,128)S(1)}, f32[3,16,64,128]{3,2,1,0:T(8,128)}) fusion(bf16[2,128,16,128]{3,1,2,0:T(8,128)(2,1)S(1)} %copy.22, bf16[1,128,16,128]{3,1,2,0:T(8,128)(2,1)} %copy.21, bf16[3,64,16,128]{3,2,1,0:T(8,128)(2,1)S(1)} %bitcast.58), kind=kOutput, calls=%fused_computation.63 | convolution fusion | flops 102629504 | bytes 3944448 | tf_op jit(solution)/shard_map/sub | solution.py:275
  141.7 2.1 %fusion.19 = bf16[3,64,16,128]{3,1,2,0:T(8,128)(2,1)S(1)} fusion(bf16[2,128,16,128]{3,1,2,0:T(8,128)(2,1)S(1)} %copy.20, bf16[1,128,16,128]{3,1,2,0:T(8,128)(2,1)} %copy.19, f32[3,16,64,128]{3,2,1,0:T(8,128)} %get-tuple-element.14, f32[3,16,64]{2,1,0:T(8,128)S(1)} %get-tuple-element.13), kind=kOutput, calls=%fused_computation.21 | convolution fusion | flops 104988672 | bytes 3944448 | tf_op jit(solution)/shard_map/ghqk,gkhd->gqhd/dot_general | solution.py:277
  143.8 0.5 copy.24
  144.3 0.2 copy.40
  144.5 0.9 slice.15
  (30 shorter events, 1.1 us)
Async XLA Ops:
  118.8 5.0 %copy-start.4 = (s32[2,16]{1,0:T(2,128)S(1)}, s32[2,16]{1,0:T(2,128)}, u32[]{:S(2)}) copy-start(s32[2,16]{1,0:T(2,128)} %param.12) | copy-start | bytes 388
  118.8 5.2 %copy-start.3 = (f32[896]{0:T(1024)S(1)}, f32[896]{0:T(1024)}, u32[]{:S(2)}) copy-start(f32[896]{0:T(1024)} %param.9) | copy-start | bytes 10756
  121.3 13.1 %collective-permute-start = (bf16[1,16,8,896]{3,2,1,0:T(8,128)(2,1)S(1)}, bf16[1,16,8,896]{3,2,1,0:T(8,128)(2,1)S(1)}, u32[]{:S(2)}, u32[]{:S(2)}) collective-permute-start(bf16[1,16,8,896]{3,2,1,0:T(8,128)(2,1)S(1)} %slice_bitcast_fusion), channel_id=1, source_target_pairs={{0,1},{1,2},{2,3},{3,4},{4,5},{5,6},{6,7},{7,8},{8,9},{9,10},{10,1... | collective-permute-start | bytes 688136 | tf_op jit(solution)/shard_map/ppermute | solution.py:24
  127.7 1.0 copy-start.2
  127.7 2.2 %copy-start = (bf16[896,2048]{1,0:T(8,128)(2,1)S(1)}, bf16[896,2048]{1,0:T(8,128)(2,1)}, u32[]{:S(2)}) copy-start(bf16[896,2048]{1,0:T(8,128)(2,1)} %get-tuple-element.9) | copy-start | bytes 11010052
  131.3 3.2 %copy-start.1 = (bf16[896,2048]{1,0:T(8,128)(2,1)S(1)}, bf16[896,2048]{1,0:T(8,128)(2,1)}, u32[]{:S(2)}) copy-start(bf16[896,2048]{1,0:T(8,128)(2,1)} %get-tuple-element.10) | copy-start | bytes 11010052

commit v13 on v10

--- a/solution.py
+++ b/solution.py
@@ -282,7 +282,9 @@
     fetched = jnp.take(arrived, shard_flat * capacity + slot_rank, axis=0).reshape(
         spans, nbr_count, length, enc_width
     )
-    prior_rows = from_behind(fetched[-1:], ("dp", "seq"), 1)
+    last_slots = (shard_flat * capacity + slot_rank)[requests - nbr_count :]
+    last_rows = jnp.take(arrived, last_slots, axis=0)[None]
+    prior_rows = from_behind(last_rows, ("dp", "seq"), 1)
     keys_own, values_own = project(fetched, enc_gain, key_weight, value_weight)
     keys_prior, values_prior = project(prior_rows, enc_gain, key_weight, value_weight)
     keys_all = jnp.concatenate([keys_prior, keys_own], axis=0)

time: 146 us -> 147 us (level)
  local copies, waits for them, and re-layouts: 10.6 us -> 14.1 us
  waiting for transfers between devices: 2.57 us -> 0.06 us
    ppermute x1, waiting for transfers between devices: 2.57 us -> 0.06 us  [from_behind(): return lax.ppermute(block, axis, route)]
    gather x0 -> x1, local copies, waits for them, and re-layouts: none -> 2.09 us  [body(): last_rows = jnp.take(arrived, last_slots, axis=0)[None]]
  transfers between devices with their start and end apart: 1 -> 1, of which waited for: 1 -> 1; matrix products, arithmetic and copies ran while one was open for 5% -> 6% of each run, Pallas kernels for 0% -> 0%
where the time goes in v13:
time: 147 us; the launch traced here: 146 us
  Pallas kernels  115 us (78%)
  local copies, waits for them, and re-layouts  14.1 us (10%)
  matrix products  12 us (8%)
  starting transfers between devices  2.32 us (2%)
  other arithmetic  2.08 us (1%)
    pallas_call x1, Pallas kernels, fetch(): pl.pallas_call(functools.partial(fetch_kernel, length, math.gcd(8, n)), o...  115 us
    dot_general x2, matrix products, project(): jnp.dot(flat_rows, key_weight, preferred_element_type=jnp.float32)  4.19 us
    unnamed x16, local copies, waits for them, and re-layouts  3.63 us
    sub x1, matrix products, attend(): expo = jnp.exp(scores - row_max)  3.46 us
  transfers between devices with their start and end apart: 1, of which 1 were waited for; matrix products, arithmetic and copies ran while one was open for 6% of the time, Pallas kernels for 0%

profile of v13, /device:TPU:6, one launch (start us, length us, event | category | flops | bytes accessed | tf_op | source)
XLA Modules:
  0.0 145.9 jit_solution(1701693153307786217)
XLA Ops:
  0.0 0.8 reshape.185
  0.8 0.2 convert_reduce_fusion
  1.1 0.7 broadcast_add_fusion.1
  2.2 0.1 broadcast_in_dim.69
  2.3 0.7 pad.4.wanted_ref
  3.0 115.2 %shard_map.73 = (bf16[64,16,896]{2,1,0:T(8,128)(2,1)}, bf16[896,2048]{1,0:T(8,128)(2,1)}, bf16[896,2048]{1,0:T(8,128)(2,1)}) custom-call(s32[64,8,128]{2,1,0:T(8,128)} %pad.4.wanted_ref, bf16[256,896]{1,0:T(8,128)(2,1)} %bitcast.59, bf16[896,256]{1,0:T(8,128)(2,1)} %wk_ref.1, bf16[896,256]{1,0:T(8,128)(2,1)} %wv_ref.1), custom_call_target="tpu_custom_call" | custom-call | tf_op jit(solution)/shard_map/pallas_call | solution.py:191
  118.2 2.1 %gather_fusion = bf16[16,8,896]{2,1,0:T(8,128)(2,1)S(1)} fusion(bf16[128,8,896]{2,1,0:T(8,128)(2,1)} %bitcast.60, s32[1024]{0:T(1024)S(1)} %pad_clamp_fusion.1), kind=kCustom, calls=%fused_computation | custom fusion | bytes 458816 | tf_op jit(solution)/shard_map/jit(_take)/gather | solution.py:286
  120.4 2.3 %collective-permute-start = (bf16[1,16,8,896]{3,2,1,0:T(8,128)(2,1)S(1)}, bf16[1,16,8,896]{3,2,1,0:T(8,128)(2,1)S(1)}, u32[]{:S(2)}, u32[]{:S(2)}) collective-permute-start(bf16[1,16,8,896]{3,2,1,0:T(8,128)(2,1)S(1)} %bitcast_select_fusion.1), channel_id=1, source_target_pairs={{0,1},{1,2},{2,3},{3,4},{4,5},{5,6},{6,7},{7,8},{8,9},{9,10},{10,1... | collective-permute-start | bytes 688136 | tf_op jit(solution)/shard_map/ppermute | solution.py:24
  122.9 2.1 %gather_fusion.1 = bf16[32,8,896]{2,1,0:T(8,128)(2,1)S(1)} fusion(bf16[128,8,896]{2,1,0:T(8,128)(2,1)} %bitcast.61, s32[1024]{0:T(1024)S(1)} %pad_clamp_fusion), kind=kCustom, calls=%fused_computation.1 | custom fusion | bytes 917632 | tf_op jit(solution)/shard_map/jit(_take)/gather | solution.py:282
  125.1 0.3 multiply_reduce_fusion
  125.6 3.4 %fusion.18 = bf16[32,8,16,128]{3,1,2,0:T(8,128)(2,1)S(1)} fusion(bf16[896,2048]{1,0:T(8,128)(2,1)} %get-tuple-element.10, bf16[32,8,896]{2,1,0:T(8,128)(2,1)S(1)} %gather_fusion.1, f32[896]{0:T(1024)S(1)} %copy-done.3, f32[256]{0:T(256)S(1)} %rsqrt.21, pred[256]{0:T(512)(128)(4,1)S(1)} %broadcast_in_dim.73), kind=kOutput, calls=%fused_computation.21 | convolution fusion | flops 941195264 | bytes 5182208 | tf_op jit(solution)/shard_map/dot_general | solution.py:227
  129.1 0.2 copy.27
  129.3 0.3 copy.22
  129.7 0.7 copy-done.2
  130.3 0.4 maximum_bitcast_fusion
  130.7 0.2 copy.25
  130.9 0.6 copy-done
  131.5 1.4 fusion.17
  132.9 0.2 copy.29
  133.1 0.3 copy.20
  133.5 0.1 fusion.26
  133.6 1.3 copy-done.1
  134.9 0.8 fusion.23
  135.7 0.1 copy.26
  135.9 1.0 copy.21
  136.8 0.8 fusion.22
  137.7 0.9 copy.19
  138.7 3.5 %fusion.48 = (f32[3,16,64]{2,1,0:T(8,128)S(1)}, f32[3,16,64,128]{3,2,1,0:T(8,128)}) fusion(bf16[2,128,16,128]{3,1,2,0:T(8,128)(2,1)S(1)} %copy.22, bf16[1,128,16,128]{3,1,2,0:T(8,128)(2,1)} %copy.21, bf16[3,64,16,128]{3,2,1,0:T(8,128)(2,1)S(1)} %bitcast.58), kind=kOutput, calls=%fused_computation.67 | convolution fusion | flops 102629504 | bytes 3944448 | tf_op jit(solution)/shard_map/sub | solution.py:246
  142.1 2.1 %fusion.19 = bf16[3,64,16,128]{3,1,2,0:T(8,128)(2,1)S(1)} fusion(bf16[2,128,16,128]{3,1,2,0:T(8,128)(2,1)S(1)} %copy.20, bf16[1,128,16,128]{3,1,2,0:T(8,128)(2,1)} %copy.19, f32[3,16,64,128]{3,2,1,0:T(8,128)} %get-tuple-element.16, f32[3,16,64]{2,1,0:T(8,128)S(1)} %get-tuple-element.15), kind=kOutput, calls=%fused_computation.22 | convolution fusion | flops 104988672 | bytes 3944448 | tf_op jit(solution)/shard_map/ghqk,gkhd->gqhd/dot_general | solution.py:248
  144.3 0.5 copy.24
  144.8 0.2 copy.40
  145.0 0.9 slice.12
  (33 shorter events, 1.3 us)
Async XLA Ops:
  0.0 122.7 %copy-start.4 = (s32[2,16]{1,0:T(2,128)S(1)}, s32[2,16]{1,0:T(2,128)}, u32[]{:S(2)}) copy-start(s32[2,16]{1,0:T(2,128)} %param.12) | copy-start | bytes 388
  118.2 7.4 %copy-start.3 = (f32[896]{0:T(1024)S(1)}, f32[896]{0:T(1024)}, u32[]{:S(2)}) copy-start(f32[896]{0:T(1024)} %param.9) | copy-start | bytes 10756
  120.4 13.1 %collective-permute-start = (bf16[1,16,8,896]{3,2,1,0:T(8,128)(2,1)S(1)}, bf16[1,16,8,896]{3,2,1,0:T(8,128)(2,1)S(1)}, u32[]{:S(2)}, u32[]{:S(2)}) collective-permute-start(bf16[1,16,8,896]{3,2,1,0:T(8,128)(2,1)S(1)} %bitcast_select_fusion.1), channel_id=1, source_target_pairs={{0,1},{1,2},{2,3},{3,4},{4,5},{5,6},{6,7},{7,8},{8,9},{9,10},{10,1... | collective-permute-start | bytes 688136 | tf_op jit(solution)/shard_map/ppermute | solution.py:24
  129.3 1.0 copy-start.2
  129.3 2.2 %copy-start = (bf16[896,2048]{1,0:T(8,128)(2,1)S(1)}, bf16[896,2048]{1,0:T(8,128)(2,1)}, u32[]{:S(2)}) copy-start(bf16[896,2048]{1,0:T(8,128)(2,1)} %get-tuple-element.9) | copy-start | bytes 11010052
  132.9 2.0 %copy-start.1 = (bf16[896,2048]{1,0:T(8,128)(2,1)S(1)}, bf16[896,2048]{1,0:T(8,128)(2,1)}, u32[]{:S(2)}) copy-start(bf16[896,2048]{1,0:T(8,128)(2,1)} %get-tuple-element.10) | copy-start | bytes 11010052

commit v14 on v10

--- a/solution.py
+++ b/solution.py
@@ -151,7 +151,7 @@
 
             @pl.when(k == 0)
             def _():
-                out_ref[me] = outgoing[k]
+                pltpu.make_async_copy(outgoing.at[k], out_ref.at[me], own_sem.at[2]).start()
 
             @pl.when(k > 0)
             def _():
@@ -181,6 +181,7 @@
     lax.fori_loop(1, nd, gathered, 0)
     for copy in own:
         copy.wait()
+    pltpu.make_async_copy(outgoing.at[0], out_ref.at[me], own_sem.at[2]).wait()
 
 
 def fetch(wanted, table, key_weight, value_weight, length, nd):
@@ -196,7 +197,7 @@
             jax.ShapeDtypeStruct((value_weight.shape[0], nd * value_weight.shape[1]), value_weight.dtype),
         ),
         in_specs=[vmem, vmem, anywhere, anywhere],
-        out_specs=(vmem, anywhere, anywhere),
+        out_specs=(anywhere, anywhere, anywhere),
         scratch_shapes=[
             pltpu.VMEM(wanted.shape, jnp.int32),
             pltpu.VMEM((n, 2 * length, width), table.dtype),
@@ -208,7 +209,7 @@
             pltpu.SemaphoreType.DMA((nd,)),
             pltpu.SemaphoreType.DMA((nd,)),
             pltpu.SemaphoreType.DMA((nd,)),
-            pltpu.SemaphoreType.DMA((2,)),
+            pltpu.SemaphoreType.DMA((3,)),
         ],
         compiler_params=pltpu.CompilerParams(collective_id=0, has_side_effects=True),
     )(wanted, table, key_weight, value_weight)

time: 146 us -> 145 us (level)
  no operation moved by 1% of the time
where the time goes in v14:
time: 145 us; the launch traced here: 144 us
  Pallas kernels  114 us (79%)
  matrix products  12 us (8%)
  local copies, waits for them, and re-layouts  10.6 us (7%)
  other arithmetic  2.6 us (2%)
  waiting for transfers between devices  2.56 us (2%)
  starting transfers between devices  2.33 us (2%)
    pallas_call x1, Pallas kernels, fetch(): pl.pallas_call(functools.partial(fetch_kernel, length, math.gcd(8, n)), o...  114 us
    dot_general x2, matrix products, project(): jnp.dot(flat_rows, key_weight, preferred_element_type=jnp.float32)  4.2 us
    sub x1, matrix products, attend(): expo = jnp.exp(scores - row_max)  3.46 us
  transfers between devices with their start and end apart: 1, of which 1 were waited for; matrix products, arithmetic and copies ran while one was open for 5% of the time, Pallas kernels for 0%

profile of v14, /device:TPU:6, one launch (start us, length us, event | category | flops | bytes accessed | tf_op | source)
XLA Modules:
  0.0 144.3 jit_solution(999254874553500161)
XLA Ops:
  0.0 0.8 reshape.174
  0.8 0.2 convert_reduce_fusion
  1.0 0.7 broadcast_multiply_fusion
  1.7 0.7 broadcast_add_fusion.1
  2.8 0.1 broadcast_in_dim.56
  2.9 0.7 pad.4.wanted_ref
  3.6 113.9 %shard_map.73 = (bf16[64,16,896]{2,1,0:T(8,128)(2,1)}, bf16[896,2048]{1,0:T(8,128)(2,1)}, bf16[896,2048]{1,0:T(8,128)(2,1)}) custom-call(s32[64,8,128]{2,1,0:T(8,128)} %pad.4.wanted_ref, bf16[256,896]{1,0:T(8,128)(2,1)} %bitcast.59, bf16[896,256]{1,0:T(8,128)(2,1)} %wk_ref.1, bf16[896,256]{1,0:T(8,128)(2,1)} %wv_ref.1), custom_call_target="tpu_custom_call" | custom-call | tf_op jit(solution)/shard_map/pallas_call | solution.py:192
  117.6 2.1 %gather_fusion = bf16[32,8,896]{2,1,0:T(8,128)(2,1)S(1)} fusion(bf16[128,8,896]{2,1,0:T(8,128)(2,1)} %bitcast.60, s32[1024]{0:T(1024)S(1)} %pad_clamp_fusion), kind=kCustom, calls=%fused_computation | custom fusion | bytes 917632 | tf_op jit(solution)/shard_map/jit(_take)/gather | solution.py:283
  119.8 0.3 multiply_reduce_fusion
  120.1 2.3 %collective-permute-start = (bf16[1,16,8,896]{3,2,1,0:T(8,128)(2,1)S(1)}, bf16[1,16,8,896]{3,2,1,0:T(8,128)(2,1)S(1)}, u32[]{:S(2)}, u32[]{:S(2)}) collective-permute-start(bf16[1,16,8,896]{3,2,1,0:T(8,128)(2,1)S(1)} %slice_bitcast_fusion), channel_id=1, source_target_pairs={{0,1},{1,2},{2,3},{3,4},{4,5},{5,6},{6,7},{7,8},{8,9},{9,10},{10,1... | collective-permute-start | bytes 688136 | tf_op jit(solution)/shard_map/ppermute | solution.py:24
  122.8 3.4 %fusion.18 = bf16[32,8,16,128]{3,1,2,0:T(8,128)(2,1)S(1)} fusion(bf16[896,2048]{1,0:T(8,128)(2,1)} %get-tuple-element.10, bf16[32,8,896]{2,1,0:T(8,128)(2,1)S(1)} %gather_fusion, f32[896]{0:T(1024)S(1)} %copy-done.3, f32[256]{0:T(256)S(1)} %rsqrt.21, pred[256]{0:T(512)(128)(4,1)S(1)} %broadcast_in_dim.59), kind=kOutput, calls=%fused_computation.20 | convolution fusion | flops 941195264 | bytes 5182208 | tf_op jit(solution)/shard_map/dot_general | solution.py:228
  126.2 0.2 copy.27
  126.5 0.3 copy.22
  126.8 0.7 copy-done.2
  127.5 0.4 maximum_bitcast_fusion
  127.9 0.2 copy.25
  128.1 0.6 copy-done
  128.7 1.4 fusion.17
  130.1 0.2 copy.29
  130.3 0.3 copy.20
  130.6 2.6 %collective-permute-done = bf16[1,16,8,896]{3,2,1,0:T(8,128)(2,1)S(1)} collective-permute-done((bf16[1,16,8,896]{3,2,1,0:T(8,128)(2,1)S(1)}, bf16[1,16,8,896]{3,2,1,0:T(8,128)(2,1)S(1)}, u32[]{:S(2)}, u32[]{:S(2)}) %collective-permute-start) | collective-permute-done | bytes 229408 | tf_op jit(solution)/shard_map/ppermute | solution.py:24
  133.1 0.1 fusion.26
  133.3 0.8 fusion.23
  134.2 1.0 copy.21
  135.2 0.8 fusion.22
  136.0 0.1 copy.28
  136.1 0.9 copy.19
  137.0 3.5 %fusion.48 = (f32[3,16,64]{2,1,0:T(8,128)S(1)}, f32[3,16,64,128]{3,2,1,0:T(8,128)}) fusion(bf16[2,128,16,128]{3,1,2,0:T(8,128)(2,1)S(1)} %copy.22, bf16[1,128,16,128]{3,1,2,0:T(8,128)(2,1)} %copy.21, bf16[3,64,16,128]{3,2,1,0:T(8,128)(2,1)S(1)} %bitcast.58), kind=kOutput, calls=%fused_computation.63 | convolution fusion | flops 102629504 | bytes 3944448 | tf_op jit(solution)/shard_map/sub | solution.py:247
  140.5 2.1 %fusion.19 = bf16[3,64,16,128]{3,1,2,0:T(8,128)(2,1)S(1)} fusion(bf16[2,128,16,128]{3,1,2,0:T(8,128)(2,1)S(1)} %copy.20, bf16[1,128,16,128]{3,1,2,0:T(8,128)(2,1)} %copy.19, f32[3,16,64,128]{3,2,1,0:T(8,128)} %get-tuple-element.14, f32[3,16,64]{2,1,0:T(8,128)S(1)} %get-tuple-element.13), kind=kOutput, calls=%fused_computation.21 | convolution fusion | flops 104988672 | bytes 3944448 | tf_op jit(solution)/shard_map/ghqk,gkhd->gqhd/dot_general | solution.py:249
  142.6 0.5 copy.24
  143.1 0.2 copy.40
  143.3 0.9 slice.15
  (30 shorter events, 1.1 us)
Async XLA Ops:
  117.6 5.0 %copy-start.4 = (s32[2,16]{1,0:T(2,128)S(1)}, s32[2,16]{1,0:T(2,128)}, u32[]{:S(2)}) copy-start(s32[2,16]{1,0:T(2,128)} %param.12) | copy-start | bytes 388
  117.6 5.2 %copy-start.3 = (f32[896]{0:T(1024)S(1)}, f32[896]{0:T(1024)}, u32[]{:S(2)}) copy-start(f32[896]{0:T(1024)} %param.9) | copy-start | bytes 10756
  120.1 13.1 %collective-permute-start = (bf16[1,16,8,896]{3,2,1,0:T(8,128)(2,1)S(1)}, bf16[1,16,8,896]{3,2,1,0:T(8,128)(2,1)S(1)}, u32[]{:S(2)}, u32[]{:S(2)}) collective-permute-start(bf16[1,16,8,896]{3,2,1,0:T(8,128)(2,1)S(1)} %slice_bitcast_fusion), channel_id=1, source_target_pairs={{0,1},{1,2},{2,3},{3,4},{4,5},{5,6},{6,7},{7,8},{8,9},{9,10},{10,1... | collective-permute-start | bytes 688136 | tf_op jit(solution)/shard_map/ppermute | solution.py:24
  126.4 1.0 copy-start.2
  126.5 2.2 %copy-start = (bf16[896,2048]{1,0:T(8,128)(2,1)S(1)}, bf16[896,2048]{1,0:T(8,128)(2,1)}, u32[]{:S(2)}) copy-start(bf16[896,2048]{1,0:T(8,128)(2,1)} %get-tuple-element.9) | copy-start | bytes 11010052
  130.1 3.2 %copy-start.1 = (bf16[896,2048]{1,0:T(8,128)(2,1)S(1)}, bf16[896,2048]{1,0:T(8,128)(2,1)}, u32[]{:S(2)}) copy-start(bf16[896,2048]{1,0:T(8,128)(2,1)} %get-tuple-element.10) | copy-start | bytes 11010052

commit v15 on v14

--- a/solution.py
+++ b/solution.py
@@ -283,7 +283,9 @@
     fetched = jnp.take(arrived, shard_flat * capacity + slot_rank, axis=0).reshape(
         spans, nbr_count, length, enc_width
     )
-    prior_rows = from_behind(fetched[-1:], ("dp", "seq"), 1)
+    last_slots = (shard_flat * capacity + slot_rank)[requests - nbr_count :]
+    last_rows = jnp.take(arrived, last_slots, axis=0)[None]
+    prior_rows = from_behind(last_rows, ("dp", "seq"), 1)
     keys_own, values_own = project(fetched, enc_gain, key_weight, value_weight)
     keys_prior, values_prior = project(prior_rows, enc_gain, key_weight, value_weight)
     keys_all = jnp.concatenate([keys_prior, keys_own], axis=0)

time: 145 us -> 146 us (level)
  local copies, waits for them, and re-layouts: 10.6 us -> 14.1 us
  waiting for transfers between devices: 2.56 us -> 0.06 us
    ppermute x1, waiting for transfers between devices: 2.56 us -> 0.06 us  [from_behind(): return lax.ppermute(block, axis, route)]
    gather x0 -> x1, local copies, waits for them, and re-layouts: none -> 2.09 us  [body(): last_rows = jnp.take(arrived, last_slots, axis=0)[None]]
  transfers between devices with their start and end apart: 1 -> 1, of which waited for: 1 -> 1; matrix products, arithmetic and copies ran while one was open for 5% -> 6% of each run, Pallas kernels for 0% -> 0%
where the time goes in v15:
time: 146 us; the launch traced here: 145 us
  Pallas kernels  114 us (78%)
  local copies, waits for them, and re-layouts  14.1 us (10%)
  matrix products  11.9 us (8%)
  starting transfers between devices  2.33 us (2%)
  other arithmetic  2.08 us (1%)
    pallas_call x1, Pallas kernels, fetch(): pl.pallas_call(functools.partial(fetch_kernel, length, math.gcd(8, n)), o...  114 us
    dot_general x2, matrix products, project(): jnp.dot(flat_rows, key_weight, preferred_element_type=jnp.float32)  4.19 us
    unnamed x16, local copies, waits for them, and re-layouts  3.63 us
    sub x1, matrix products, attend(): expo = jnp.exp(scores - row_max)  3.46 us
  transfers between devices with their start and end apart: 1, of which 1 were waited for; matrix products, arithmetic and copies ran while one was open for 6% of the time, Pallas kernels for 0%

profile of v15, /device:TPU:6, one launch (start us, length us, event | category | flops | bytes accessed | tf_op | source)
XLA Modules:
  0.0 144.7 jit_solution(2344064196431899249)
XLA Ops:
  0.0 0.8 reshape.185
  0.8 0.2 convert_reduce_fusion
  1.1 0.7 broadcast_add_fusion.1
  2.2 0.1 broadcast_in_dim.69
  2.3 0.7 pad.4.wanted_ref
  3.0 113.9 %shard_map.73 = (bf16[64,16,896]{2,1,0:T(8,128)(2,1)}, bf16[896,2048]{1,0:T(8,128)(2,1)}, bf16[896,2048]{1,0:T(8,128)(2,1)}) custom-call(s32[64,8,128]{2,1,0:T(8,128)} %pad.4.wanted_ref, bf16[256,896]{1,0:T(8,128)(2,1)} %bitcast.59, bf16[896,256]{1,0:T(8,128)(2,1)} %wk_ref.1, bf16[896,256]{1,0:T(8,128)(2,1)} %wv_ref.1), custom_call_target="tpu_custom_call" | custom-call | tf_op jit(solution)/shard_map/pallas_call | solution.py:192
  117.0 2.1 %gather_fusion = bf16[16,8,896]{2,1,0:T(8,128)(2,1)S(1)} fusion(bf16[128,8,896]{2,1,0:T(8,128)(2,1)} %bitcast.60, s32[1024]{0:T(1024)S(1)} %pad_clamp_fusion.1), kind=kCustom, calls=%fused_computation | custom fusion | bytes 458816 | tf_op jit(solution)/shard_map/jit(_take)/gather | solution.py:287
  119.2 2.3 %collective-permute-start = (bf16[1,16,8,896]{3,2,1,0:T(8,128)(2,1)S(1)}, bf16[1,16,8,896]{3,2,1,0:T(8,128)(2,1)S(1)}, u32[]{:S(2)}, u32[]{:S(2)}) collective-permute-start(bf16[1,16,8,896]{3,2,1,0:T(8,128)(2,1)S(1)} %bitcast_select_fusion.1), channel_id=1, source_target_pairs={{0,1},{1,2},{2,3},{3,4},{4,5},{5,6},{6,7},{7,8},{8,9},{9,10},{10,1... | collective-permute-start | bytes 688136 | tf_op jit(solution)/shard_map/ppermute | solution.py:24
  121.7 2.1 %gather_fusion.1 = bf16[32,8,896]{2,1,0:T(8,128)(2,1)S(1)} fusion(bf16[128,8,896]{2,1,0:T(8,128)(2,1)} %bitcast.61, s32[1024]{0:T(1024)S(1)} %pad_clamp_fusion), kind=kCustom, calls=%fused_computation.1 | custom fusion | bytes 917632 | tf_op jit(solution)/shard_map/jit(_take)/gather | solution.py:283
  123.9 0.3 multiply_reduce_fusion
  124.4 3.4 %fusion.18 = bf16[32,8,16,128]{3,1,2,0:T(8,128)(2,1)S(1)} fusion(bf16[896,2048]{1,0:T(8,128)(2,1)} %get-tuple-element.10, bf16[32,8,896]{2,1,0:T(8,128)(2,1)S(1)} %gather_fusion.1, f32[896]{0:T(1024)S(1)} %copy-done.3, f32[256]{0:T(256)S(1)} %rsqrt.21, pred[256]{0:T(512)(128)(4,1)S(1)} %broadcast_in_dim.73), kind=kOutput, calls=%fused_computation.21 | convolution fusion | flops 941195264 | bytes 5182208 | tf_op jit(solution)/shard_map/dot_general | solution.py:228
  127.8 0.2 copy.27
  128.1 0.3 copy.22
  128.5 0.7 copy-done.2
  129.1 0.4 maximum_bitcast_fusion
  129.5 0.2 copy.25
  129.7 0.6 copy-done
  130.3 1.4 fusion.17
  131.7 0.2 copy.29
  131.9 0.3 copy.20
  132.3 0.1 fusion.26
  132.4 1.3 copy-done.1
  133.7 0.8 fusion.23
  134.5 0.1 copy.26
  134.7 1.0 copy.21
  135.6 0.8 fusion.22
  136.5 0.9 copy.19
  137.5 3.5 %fusion.48 = (f32[3,16,64]{2,1,0:T(8,128)S(1)}, f32[3,16,64,128]{3,2,1,0:T(8,128)}) fusion(bf16[2,128,16,128]{3,1,2,0:T(8,128)(2,1)S(1)} %copy.22, bf16[1,128,16,128]{3,1,2,0:T(8,128)(2,1)} %copy.21, bf16[3,64,16,128]{3,2,1,0:T(8,128)(2,1)S(1)} %bitcast.58), kind=kOutput, calls=%fused_computation.67 | convolution fusion | flops 102629504 | bytes 3944448 | tf_op jit(solution)/shard_map/sub | solution.py:247
  140.9 2.1 %fusion.19 = bf16[3,64,16,128]{3,1,2,0:T(8,128)(2,1)S(1)} fusion(bf16[2,128,16,128]{3,1,2,0:T(8,128)(2,1)S(1)} %copy.20, bf16[1,128,16,128]{3,1,2,0:T(8,128)(2,1)} %copy.19, f32[3,16,64,128]{3,2,1,0:T(8,128)} %get-tuple-element.16, f32[3,16,64]{2,1,0:T(8,128)S(1)} %get-tuple-element.15), kind=kOutput, calls=%fused_computation.22 | convolution fusion | flops 104988672 | bytes 3944448 | tf_op jit(solution)/shard_map/ghqk,gkhd->gqhd/dot_general | solution.py:249
  143.0 0.5 copy.24
  143.6 0.2 copy.40
  143.8 0.9 slice.12
  (33 shorter events, 1.3 us)
Async XLA Ops:
  0.0 121.5 %copy-start.4 = (s32[2,16]{1,0:T(2,128)S(1)}, s32[2,16]{1,0:T(2,128)}, u32[]{:S(2)}) copy-start(s32[2,16]{1,0:T(2,128)} %param.12) | copy-start | bytes 388
  117.0 7.5 %copy-start.3 = (f32[896]{0:T(1024)S(1)}, f32[896]{0:T(1024)}, u32[]{:S(2)}) copy-start(f32[896]{0:T(1024)} %param.9) | copy-start | bytes 10756
  119.2 13.1 %collective-permute-start = (bf16[1,16,8,896]{3,2,1,0:T(8,128)(2,1)S(1)}, bf16[1,16,8,896]{3,2,1,0:T(8,128)(2,1)S(1)}, u32[]{:S(2)}, u32[]{:S(2)}) collective-permute-start(bf16[1,16,8,896]{3,2,1,0:T(8,128)(2,1)S(1)} %bitcast_select_fusion.1), channel_id=1, source_target_pairs={{0,1},{1,2},{2,3},{3,4},{4,5},{5,6},{6,7},{7,8},{8,9},{9,10},{10,1... | collective-permute-start | bytes 688136 | tf_op jit(solution)/shard_map/ppermute | solution.py:24
  128.1 1.0 copy-start.2
  128.1 2.2 %copy-start = (bf16[896,2048]{1,0:T(8,128)(2,1)S(1)}, bf16[896,2048]{1,0:T(8,128)(2,1)}, u32[]{:S(2)}) copy-start(bf16[896,2048]{1,0:T(8,128)(2,1)} %get-tuple-element.9) | copy-start | bytes 11010052
  131.7 2.0 %copy-start.1 = (bf16[896,2048]{1,0:T(8,128)(2,1)S(1)}, bf16[896,2048]{1,0:T(8,128)(2,1)}, u32[]{:S(2)}) copy-start(bf16[896,2048]{1,0:T(8,128)(2,1)} %get-tuple-element.10) | copy-start | bytes 11010052

commit v16 on v12

--- a/solution.py
+++ b/solution.py
@@ -162,7 +162,7 @@
 
             @pl.when(k == 0)
             def _():
-                out_ref[me] = outgoing[k]
+                pltpu.make_async_copy(outgoing.at[k], out_ref.at[me], own_sem.at[2]).start()
 
             @pl.when(k > 0)
             def _():
@@ -208,6 +208,7 @@
         copy.wait_recv()
     for copy in own:
         copy.wait()
+    pltpu.make_async_copy(outgoing.at[0], out_ref.at[me], own_sem.at[2]).wait()
 
 
 def fetch(wanted, table, key_weight, value_weight, length, nd):
@@ -223,7 +224,7 @@
             jax.ShapeDtypeStruct((value_weight.shape[0], nd * value_weight.shape[1]), value_weight.dtype),
         ),
         in_specs=[vmem, vmem, anywhere, anywhere],
-        out_specs=(vmem, anywhere, anywhere),
+        out_specs=(anywhere, anywhere, anywhere),
         scratch_shapes=[
             pltpu.VMEM(wanted.shape, jnp.int32),
             pltpu.VMEM((n, 2 * length, width), table.dtype),
@@ -237,7 +238,7 @@
             pltpu.SemaphoreType.DMA((nd,)),
             pltpu.SemaphoreType.DMA((nd,)),
             pltpu.SemaphoreType.DMA((nd,)),
-            pltpu.SemaphoreType.DMA((2,)),
+            pltpu.SemaphoreType.DMA((3,)),
         ],
         compiler_params=pltpu.CompilerParams(collective_id=0, has_side_effects=True),
     )(wanted, table, key_weight, value_weight)

time: 146 us -> 145 us (level)
  no operation moved by 1% of the time
where the time goes in v16:
time: 145 us; the launch traced here: 144 us
  Pallas kernels  114 us (79%)
  matrix products  12 us (8%)
  local copies, waits for them, and re-layouts  10.6 us (7%)
  other arithmetic  2.6 us (2%)
  waiting for transfers between devices  2.53 us (2%)
  starting transfers between devices  2.37 us (2%)
    pallas_call x1, Pallas kernels, fetch(): pl.pallas_call(functools.partial(fetch_kernel, length, math.gcd(8, n)), o...  114 us
    dot_general x2, matrix products, project(): jnp.dot(flat_rows, key_weight, preferred_element_type=jnp.float32)  4.19 us
    sub x1, matrix products, attend(): expo = jnp.exp(scores - row_max)  3.46 us
  transfers between devices with their start and end apart: 1, of which 1 were waited for; matrix products, arithmetic and copies ran while one was open for 5% of the time, Pallas kernels for 0%

profile of v16, /device:TPU:6, one launch (start us, length us, event | category | flops | bytes accessed | tf_op | source)
XLA Modules:
  0.0 144.3 jit_solution(14524665738506144765)
XLA Ops:
  0.0 0.8 reshape.174
  0.8 0.2 convert_reduce_fusion
  1.0 0.7 broadcast_multiply_fusion
  1.7 0.7 broadcast_add_fusion.1
  2.8 0.1 broadcast_in_dim.56
  2.9 0.7 pad.4.wanted_ref
  3.6 113.9 %shard_map.73 = (bf16[64,16,896]{2,1,0:T(8,128)(2,1)}, bf16[896,2048]{1,0:T(8,128)(2,1)}, bf16[896,2048]{1,0:T(8,128)(2,1)}) custom-call(s32[64,8,128]{2,1,0:T(8,128)} %pad.4.wanted_ref, bf16[256,896]{1,0:T(8,128)(2,1)} %bitcast.59, bf16[896,256]{1,0:T(8,128)(2,1)} %wk_ref.1, bf16[896,256]{1,0:T(8,128)(2,1)} %wv_ref.1), custom_call_target="tpu_custom_call" | custom-call | tf_op jit(solution)/shard_map/pallas_call | solution.py:219
  117.6 2.1 %gather_fusion = bf16[32,8,896]{2,1,0:T(8,128)(2,1)S(1)} fusion(bf16[128,8,896]{2,1,0:T(8,128)(2,1)} %bitcast.60, s32[1024]{0:T(1024)S(1)} %pad_clamp_fusion), kind=kCustom, calls=%fused_computation | custom fusion | bytes 917632 | tf_op jit(solution)/shard_map/jit(_take)/gather | solution.py:312
  119.8 0.3 multiply_reduce_fusion
  120.1 2.4 %collective-permute-start = (bf16[1,16,8,896]{3,2,1,0:T(8,128)(2,1)S(1)}, bf16[1,16,8,896]{3,2,1,0:T(8,128)(2,1)S(1)}, u32[]{:S(2)}, u32[]{:S(2)}) collective-permute-start(bf16[1,16,8,896]{3,2,1,0:T(8,128)(2,1)S(1)} %slice_bitcast_fusion), channel_id=1, source_target_pairs={{0,1},{1,2},{2,3},{3,4},{4,5},{5,6},{6,7},{7,8},{8,9},{9,10},{10,1... | collective-permute-start | bytes 688136 | tf_op jit(solution)/shard_map/ppermute | solution.py:24
  122.8 3.4 %fusion.18 = bf16[32,8,16,128]{3,1,2,0:T(8,128)(2,1)S(1)} fusion(bf16[896,2048]{1,0:T(8,128)(2,1)} %get-tuple-element.10, bf16[32,8,896]{2,1,0:T(8,128)(2,1)S(1)} %gather_fusion, f32[896]{0:T(1024)S(1)} %copy-done.3, f32[256]{0:T(256)S(1)} %rsqrt.21, pred[256]{0:T(512)(128)(4,1)S(1)} %broadcast_in_dim.59), kind=kOutput, calls=%fused_computation.20 | convolution fusion | flops 941195264 | bytes 5182208 | tf_op jit(solution)/shard_map/dot_general | solution.py:257
  126.3 0.2 copy.27
  126.5 0.3 copy.22
  126.9 0.7 copy-done.2
  127.5 0.4 maximum_bitcast_fusion
  127.9 0.2 copy.25
  128.1 0.6 copy-done
  128.7 1.4 fusion.17
  130.1 0.2 copy.29
  130.3 0.3 copy.20
  130.6 2.5 %collective-permute-done = bf16[1,16,8,896]{3,2,1,0:T(8,128)(2,1)S(1)} collective-permute-done((bf16[1,16,8,896]{3,2,1,0:T(8,128)(2,1)S(1)}, bf16[1,16,8,896]{3,2,1,0:T(8,128)(2,1)S(1)}, u32[]{:S(2)}, u32[]{:S(2)}) %collective-permute-start) | collective-permute-done | bytes 229408 | tf_op jit(solution)/shard_map/ppermute | solution.py:24
  133.2 0.1 fusion.26
  133.3 0.8 fusion.23
  134.2 1.0 copy.21
  135.2 0.8 fusion.22
  136.0 0.1 copy.28
  136.1 0.9 copy.19
  137.0 3.5 %fusion.48 = (f32[3,16,64]{2,1,0:T(8,128)S(1)}, f32[3,16,64,128]{3,2,1,0:T(8,128)}) fusion(bf16[2,128,16,128]{3,1,2,0:T(8,128)(2,1)S(1)} %copy.22, bf16[1,128,16,128]{3,1,2,0:T(8,128)(2,1)} %copy.21, bf16[3,64,16,128]{3,2,1,0:T(8,128)(2,1)S(1)} %bitcast.58), kind=kOutput, calls=%fused_computation.63 | convolution fusion | flops 102629504 | bytes 3944448 | tf_op jit(solution)/shard_map/sub | solution.py:276
  140.5 2.1 %fusion.19 = bf16[3,64,16,128]{3,1,2,0:T(8,128)(2,1)S(1)} fusion(bf16[2,128,16,128]{3,1,2,0:T(8,128)(2,1)S(1)} %copy.20, bf16[1,128,16,128]{3,1,2,0:T(8,128)(2,1)} %copy.19, f32[3,16,64,128]{3,2,1,0:T(8,128)} %get-tuple-element.14, f32[3,16,64]{2,1,0:T(8,128)S(1)} %get-tuple-element.13), kind=kOutput, calls=%fused_computation.21 | convolution fusion | flops 104988672 | bytes 3944448 | tf_op jit(solution)/shard_map/ghqk,gkhd->gqhd/dot_general | solution.py:278
  142.6 0.5 copy.24
  143.1 0.2 copy.40
  143.3 0.9 slice.15
  (30 shorter events, 1.1 us)
Async XLA Ops:
  117.6 5.0 %copy-start.4 = (s32[2,16]{1,0:T(2,128)S(1)}, s32[2,16]{1,0:T(2,128)}, u32[]{:S(2)}) copy-start(s32[2,16]{1,0:T(2,128)} %param.12) | copy-start | bytes 388
  117.6 5.2 %copy-start.3 = (f32[896]{0:T(1024)S(1)}, f32[896]{0:T(1024)}, u32[]{:S(2)}) copy-start(f32[896]{0:T(1024)} %param.9) | copy-start | bytes 10756
  120.1 13.1 %collective-permute-start = (bf16[1,16,8,896]{3,2,1,0:T(8,128)(2,1)S(1)}, bf16[1,16,8,896]{3,2,1,0:T(8,128)(2,1)S(1)}, u32[]{:S(2)}, u32[]{:S(2)}) collective-permute-start(bf16[1,16,8,896]{3,2,1,0:T(8,128)(2,1)S(1)} %slice_bitcast_fusion), channel_id=1, source_target_pairs={{0,1},{1,2},{2,3},{3,4},{4,5},{5,6},{6,7},{7,8},{8,9},{9,10},{10,1... | collective-permute-start | bytes 688136 | tf_op jit(solution)/shard_map/ppermute | solution.py:24
  126.5 1.0 copy-start.2
  126.5 2.2 %copy-start = (bf16[896,2048]{1,0:T(8,128)(2,1)S(1)}, bf16[896,2048]{1,0:T(8,128)(2,1)}, u32[]{:S(2)}) copy-start(bf16[896,2048]{1,0:T(8,128)(2,1)} %get-tuple-element.9) | copy-start | bytes 11010052
  130.1 3.2 %copy-start.1 = (bf16[896,2048]{1,0:T(8,128)(2,1)S(1)}, bf16[896,2048]{1,0:T(8,128)(2,1)}, u32[]{:S(2)}) copy-start(bf16[896,2048]{1,0:T(8,128)(2,1)} %get-tuple-element.10) | copy-start | bytes 11010052
